TPU v7x, 32 devices: a whole 2x2x4 slice. The times are simulated.
32 devices in a mesh: seq: 4 (over x, core), fsdp: 8 (over z, y).
Axes of the slice: x: 2, y: 2, z: 4, core: 2. Of those that a mesh axis runs over, the one named last changes fastest.
Arguments:
- tokens: bfloat16 [8, 2560, 2048], P('fsdp', 'seq'), may hold values from -6 to 6
- cont_lengths: int32 [8, 2], P('fsdp'), may hold values from 1 to 384, as said below
- project_in: bfloat16 [2048, 6144], P('fsdp'), may hold values from -0.125 to 0.125
- project_out: bfloat16 [2048, 2048], P('fsdp'), may hold values from -1.5 to 1.5
- gate_weight: bfloat16 [2048, 5632], P('fsdp'), may hold values from -0.125 to 0.125
- up_weight: bfloat16 [2048, 5632], P('fsdp'), may hold values from -0.125 to 0.125
- down_weight: bfloat16 [5632, 2048], P('fsdp'), may hold values from -0.078125 to 0.078125
- first_gain: bfloat16 [2048], P('fsdp'), may hold values from 0.099609375 to 1.8984375
- first_bias: bfloat16 [2048], P('fsdp'), may hold values from -3 to 3
- second_gain: bfloat16 [2048], P('fsdp'), may hold values from 0.099609375 to 1.8984375
- second_bias: bfloat16 [2048], P('fsdp'), may hold values from -3 to 3
- grad_output: bfloat16 [8, 2560, 2048], P('fsdp', 'seq'), may hold values from -6 to 6
Outputs:
- layer_out: bfloat16 [8, 2560, 2048], P('fsdp', 'seq')
- input_gradient: float32 [8, 2560, 2048], P('fsdp', 'seq')
- grad_project_in: float32 [2048, 6144], P('fsdp')
- grad_project_out: float32 [2048, 2048], P('fsdp')
- grad_gate_weight: float32 [2048, 5632], P('fsdp')
- grad_up_weight: float32 [2048, 5632], P('fsdp')
- grad_down_weight: float32 [5632, 2048], P('fsdp')
- grad_first_gain: float32 [2048], P('fsdp')
- grad_first_bias: float32 [2048], P('fsdp')
- grad_second_gain: float32 [2048], P('fsdp')
- grad_second_bias: float32 [2048], P('fsdp')
Inputs may be any that keep to these rules, and one draw needn't show every extreme that they name: `cont_lengths`: each group's row sums to 512; exactly one of its entries, at a drawn place, equals 384, and every other entry is under 384.
All inputs are finite; a program needn't handle non-finite values.
Results may differ from a plain program's by a relative error of at most 0.018.
Values may be sent and summed in bfloat16 or wider, within the bound.
A program may use at most 512 MiB of HBM per device.

v0:
```python
import jax
import jax.numpy as jnp
from jax import lax
from jax.sharding import PartitionSpec as P

HEAD_DIM = 64
ROT = 16
PROMPT = 2048


epsilon = 1e-05
rope_base = 10000.0
block_limit = 512


def contract_last(left_side, right_side):
    return lax.dot_general(
        left_side, right_side, (((1,), (1,)), ((), ())), preferred_element_type=jnp.float32
    )


def contract_first(left_side, right_side):
    return lax.dot_general(
        left_side, right_side, (((0,), (0,)), ((), ())), preferred_element_type=jnp.float32
    )


def layout(lengths, total_rows):
    indices = jnp.arange(total_rows, dtype=jnp.int32)
    seg_ends = jnp.cumsum(lengths)
    starts = seg_ends - lengths
    offset = indices - PROMPT
    inside = (offset[:, None] >= starts[None, :]) & (offset[:, None] < seg_ends[None, :])
    numbers = jnp.arange(1, lengths.shape[0] + 1, dtype=jnp.int32)
    segment = jnp.sum(jnp.where(inside, numbers[None, :], 0), axis=1)
    seg_begin = jnp.sum(jnp.where(inside, starts[None, :], 0), axis=1)
    position = jnp.where(indices < PROMPT, indices, PROMPT + offset - seg_begin)
    return (segment, position)


def rotate(rows_in, position, sign):
    row_count = rows_in.shape[0]
    heads = rows_in.shape[1] // HEAD_DIM
    half = ROT // 2
    frequency = rope_base ** (-2.0 * jnp.arange(half, dtype=jnp.float32) / ROT)
    angles = position.astype(jnp.float32)[:, None] * frequency[None, :]
    cosine = jnp.cos(angles)[:, None, :]
    sine_part = sign * jnp.sin(angles)[:, None, :]
    shaped = rows_in.reshape(row_count, heads, HEAD_DIM)
    first_half = shaped[:, :, :half]
    second = shaped[:, :, half:ROT]
    turned = jnp.concatenate(
        [
            first_half * cosine - second * sine_part,
            second * cosine + first_half * sine_part,
            shaped[:, :, ROT:],
        ],
        axis=2,
    )
    return turned.reshape(row_count, heads * HEAD_DIM)


def apply_layer_norm(rows_in):
    mean_value = jnp.mean(rows_in, axis=-1, keepdims=True)
    centered = rows_in - mean_value
    inverse_deviation = lax.rsqrt(jnp.mean(centered * centered, axis=-1, keepdims=True) + epsilon)
    return (centered * inverse_deviation, inverse_deviation)


def norm_backward(normed_gradient, centered_unit, inverse_deviation, norm_gain):
    scaled_normed = normed_gradient * norm_gain.astype(jnp.float32)
    mean_value = jnp.mean(scaled_normed, axis=-1, keepdims=True)
    along_axis = jnp.mean(scaled_normed * centered_unit, axis=-1, keepdims=True)
    return inverse_deviation * (scaled_normed - mean_value - centered_unit * along_axis)


def block_scores(query_rows, key_heads, segment, block_start, block_rows):
    total_rows = segment.shape[0]
    heads = key_heads.shape[1]
    query_block = lax.dynamic_slice_in_dim(query_rows, block_start, block_rows, 0).reshape(
        block_rows, heads, HEAD_DIM
    )
    indices = jnp.arange(total_rows, dtype=jnp.int32)
    rows_here = block_start + jnp.arange(block_rows, dtype=jnp.int32)
    seg_here = lax.dynamic_slice_in_dim(segment, block_start, block_rows, 0)
    allowed = (indices[None, :] <= rows_here[:, None]) & (
        (segment[None, :] == 0) | (segment[None, :] == seg_here[:, None])
    )
    scores = jnp.einsum(
        "qhd,khd->hqk", query_block, key_heads, preferred_element_type=jnp.float32
    ) * HEAD_DIM ** (-0.5)
    return (jnp.where(allowed[None], scores, -1e30), query_block)


def attend(query_rows, key_rows, value_rows, segment):
    total_rows = query_rows.shape[0]
    heads = query_rows.shape[1] // HEAD_DIM
    block_rows = min(block_limit, total_rows)
    blocks = total_rows // block_rows
    key_heads = key_rows.reshape(total_rows, heads, HEAD_DIM)
    value_heads = value_rows.reshape(total_rows, heads, HEAD_DIM)

    def one_block(number):
        scores, unused = block_scores(
            query_rows, key_heads, segment, number * block_rows, block_rows
        )
        row_peak = jnp.max(scores, axis=2, keepdims=True)
        weights = jnp.exp(scores - row_peak)
        row_total = jnp.sum(weights, axis=2, keepdims=True)
        chances = (weights / row_total).astype(jnp.bfloat16)
        result = jnp.einsum(
            "hqk,khd->qhd", chances, value_heads, preferred_element_type=jnp.float32
        )
        return (
            result.astype(jnp.bfloat16).reshape(block_rows, heads * HEAD_DIM),
            (row_peak + jnp.log(row_total))[:, :, 0],
        )

    attended, log_norm = lax.map(one_block, jnp.arange(blocks, dtype=jnp.int32))
    return (attended.reshape(total_rows, heads * HEAD_DIM), log_norm)


def attend_back(query_rows, key_rows, value_rows, segment, log_norm, grad_attended):
    total_rows = query_rows.shape[0]
    heads = query_rows.shape[1] // HEAD_DIM
    block_rows = min(block_limit, total_rows)
    blocks = total_rows // block_rows
    key_heads = key_rows.reshape(total_rows, heads, HEAD_DIM)
    value_heads = value_rows.reshape(total_rows, heads, HEAD_DIM)
    factor = HEAD_DIM ** (-0.5)

    def one_block(carry, number):
        grad_keys, grad_values = carry
        block_start = number * block_rows
        scores, query_block = block_scores(query_rows, key_heads, segment, block_start, block_rows)
        chances = jnp.exp(scores - log_norm[number][:, :, None])
        grad_block = lax.dynamic_slice_in_dim(grad_attended, block_start, block_rows, 0).reshape(
            block_rows, heads, HEAD_DIM
        )
        grad_values = grad_values + jnp.einsum(
            "hqk,qhd->khd",
            chances.astype(jnp.bfloat16),
            grad_block,
            preferred_element_type=jnp.float32,
        )
        grad_chances = jnp.einsum(
            "qhd,khd->hqk", grad_block, value_heads, preferred_element_type=jnp.float32
        )
        grad_scores = (
            chances * (grad_chances - jnp.sum(chances * grad_chances, axis=2, keepdims=True))
        ).astype(jnp.bfloat16)
        grad_query = (
            jnp.einsum("hqk,khd->qhd", grad_scores, key_heads, preferred_element_type=jnp.float32)
            * factor
        )
        grad_keys = (
            grad_keys
            + jnp.einsum(
                "hqk,qhd->khd", grad_scores, query_block, preferred_element_type=jnp.float32
            )
            * factor
        )
        return ((grad_keys, grad_values), grad_query.reshape(block_rows, heads * HEAD_DIM))

    zero_heads = jnp.zeros((total_rows, heads, HEAD_DIM), jnp.float32)
    (grad_keys, grad_values), grad_query = lax.scan(
        one_block, (zero_heads, zero_heads), jnp.arange(blocks, dtype=jnp.int32)
    )
    width = heads * HEAD_DIM
    return (
        grad_query.reshape(total_rows, width),
        grad_keys.reshape(total_rows, width),
        grad_values.reshape(total_rows, width),
    )


def local(
    tokens,
    cont_lengths,
    project_in,
    project_out,
    gate_weight,
    up_weight,
    down_weight,
    first_gain,
    first_bias,
    second_gain,
    second_bias,
    grad_output,
):
    rows_dev = tokens.shape[1]
    width = tokens.shape[2]
    seq_size = lax.axis_size("seq")
    total_rows = rows_dev * seq_size
    segment, position = layout(cont_lengths[0], total_rows)
    own_position = lax.dynamic_slice_in_dim(position, lax.axis_index("seq") * rows_dev, rows_dev, 0)
    residual_stream = tokens[0].astype(jnp.float32)

    def fetch_attention():
        return (
            lax.all_gather(project_in, "fsdp", axis=0, tiled=True),
            lax.all_gather(project_out, "fsdp", axis=0, tiled=True),
            lax.all_gather(first_gain, "fsdp", axis=0, tiled=True),
            lax.all_gather(first_bias, "fsdp", axis=0, tiled=True),
        )

    def fetch_feed():
        return (
            lax.all_gather(gate_weight, "fsdp", axis=0, tiled=True),
            lax.all_gather(up_weight, "fsdp", axis=0, tiled=True),
            lax.all_gather(down_weight, "fsdp", axis=0, tiled=True),
            lax.all_gather(second_gain, "fsdp", axis=0, tiled=True),
            lax.all_gather(second_bias, "fsdp", axis=0, tiled=True),
        )

    in_full, out_full, first_norm_gain, first_norm_bias = fetch_attention()
    first_centered_unit, first_inverse_deviation = apply_layer_norm(residual_stream)
    normed_first = (
        first_centered_unit * first_norm_gain.astype(jnp.float32)
        + first_norm_bias.astype(jnp.float32)
    ).astype(jnp.bfloat16)
    mixed = jnp.dot(normed_first, in_full, preferred_element_type=jnp.float32)
    query = rotate(mixed[:, :width], own_position, 1.0).astype(jnp.bfloat16)
    key_tok = rotate(mixed[:, width : 2 * width], own_position, 1.0).astype(jnp.bfloat16)
    value_tok = mixed[:, 2 * width :].astype(jnp.bfloat16)
    query_heads, key_heads, value_heads = (
        lax.all_to_all(query, "seq", split_axis=1, concat_axis=0, tiled=True),
        lax.all_to_all(key_tok, "seq", split_axis=1, concat_axis=0, tiled=True),
        lax.all_to_all(value_tok, "seq", split_axis=1, concat_axis=0, tiled=True),
    )
    attended_heads, log_norm = attend(query_heads, key_heads, value_heads, segment)
    attended = lax.all_to_all(attended_heads, "seq", split_axis=0, concat_axis=1, tiled=True)
    hidden_state = residual_stream + jnp.dot(attended, out_full, preferred_element_type=jnp.float32)
    gate_full, up_full, down_full, second_norm_gain, second_norm_bias = fetch_feed()
    second_centered_unit, second_inverse_deviation = apply_layer_norm(hidden_state)
    normed_second = (
        second_centered_unit * second_norm_gain.astype(jnp.float32)
        + second_norm_bias.astype(jnp.float32)
    ).astype(jnp.bfloat16)
    gate_pre = jnp.dot(normed_second, gate_full, preferred_element_type=jnp.float32)
    up_pre = jnp.dot(normed_second, up_full, preferred_element_type=jnp.float32)
    sigmoid_gate = jax.nn.sigmoid(gate_pre)
    silu_gate = gate_pre * sigmoid_gate
    product = (silu_gate * up_pre).astype(jnp.bfloat16)
    layer_rows = hidden_state + jnp.dot(product, down_full, preferred_element_type=jnp.float32)
    layer_out = layer_rows.astype(jnp.bfloat16)[None]
    upstream = grad_output[0]
    gate_full, up_full, down_full, second_norm_gain, second_norm_bias = fetch_feed()
    grad_mid = contract_last(upstream, down_full)
    grad_gate = (grad_mid * up_pre * sigmoid_gate * (1.0 + gate_pre * (1.0 - sigmoid_gate))).astype(
        jnp.bfloat16
    )
    grad_up = (grad_mid * silu_gate).astype(jnp.bfloat16)
    second_normed_gradient = contract_last(grad_gate, gate_full) + contract_last(grad_up, up_full)
    hidden_gradient = upstream.astype(jnp.float32) + norm_backward(
        second_normed_gradient, second_centered_unit, second_inverse_deviation, second_norm_gain
    )
    low_hidden = hidden_gradient.astype(jnp.bfloat16)
    second_gain_total = jnp.sum(second_normed_gradient * second_centered_unit, axis=0)
    bias_sum_two = jnp.sum(second_normed_gradient, axis=0)
    feed_parts = (
        lax.psum_scatter(
            contract_first(normed_second, grad_gate).astype(jnp.bfloat16),
            "fsdp",
            scatter_dimension=0,
            tiled=True,
        ).astype(jnp.float32),
        lax.psum_scatter(
            contract_first(normed_second, grad_up).astype(jnp.bfloat16),
            "fsdp",
            scatter_dimension=0,
            tiled=True,
        ).astype(jnp.float32),
        lax.psum_scatter(
            contract_first(product, upstream).astype(jnp.bfloat16),
            "fsdp",
            scatter_dimension=0,
            tiled=True,
        ).astype(jnp.float32),
        lax.psum_scatter(
            second_gain_total.astype(jnp.bfloat16), "fsdp", scatter_dimension=0, tiled=True
        ).astype(jnp.float32),
        lax.psum_scatter(
            bias_sum_two.astype(jnp.bfloat16), "fsdp", scatter_dimension=0, tiled=True
        ).astype(jnp.float32),
    )
    in_full, out_full, first_norm_gain, first_norm_bias = fetch_attention()
    grad_attended = contract_last(low_hidden, out_full).astype(jnp.bfloat16)
    grad_attended_heads = lax.all_to_all(
        grad_attended, "seq", split_axis=1, concat_axis=0, tiled=True
    )
    grad_query, grad_key, grad_value = attend_back(
        query_heads, key_heads, value_heads, segment, log_norm, grad_attended_heads
    )
    back_query = rotate(grad_query, position, -1.0).astype(jnp.bfloat16)
    back_key = rotate(grad_key, position, -1.0).astype(jnp.bfloat16)
    back_value = grad_value.astype(jnp.bfloat16)
    tok_query, tok_key, tok_value = (
        lax.all_to_all(back_query, "seq", split_axis=0, concat_axis=1, tiled=True),
        lax.all_to_all(back_key, "seq", split_axis=0, concat_axis=1, tiled=True),
        lax.all_to_all(back_value, "seq", split_axis=0, concat_axis=1, tiled=True),
    )
    grad_mixed = jnp.concatenate([tok_query, tok_key, tok_value], axis=1)
    first_normed_gradient = contract_last(grad_mixed, in_full)
    input_gradient = hidden_gradient + norm_backward(
        first_normed_gradient, first_centered_unit, first_inverse_deviation, first_norm_gain
    )
    first_gain_total = jnp.sum(first_normed_gradient * first_centered_unit, axis=0)
    bias_sum_one = jnp.sum(first_normed_gradient, axis=0)
    attn_parts = (
        lax.psum_scatter(
            contract_first(normed_first, grad_mixed).astype(jnp.bfloat16),
            "fsdp",
            scatter_dimension=0,
            tiled=True,
        ).astype(jnp.float32),
        lax.psum_scatter(
            contract_first(attended, low_hidden).astype(jnp.bfloat16),
            "fsdp",
            scatter_dimension=0,
            tiled=True,
        ).astype(jnp.float32),
        lax.psum_scatter(
            first_gain_total.astype(jnp.bfloat16), "fsdp", scatter_dimension=0, tiled=True
        ).astype(jnp.float32),
        lax.psum_scatter(
            bias_sum_one.astype(jnp.bfloat16), "fsdp", scatter_dimension=0, tiled=True
        ).astype(jnp.float32),
    )
    summed = (
        lax.psum(attn_parts[0].astype(jnp.bfloat16), "seq").astype(jnp.float32),
        lax.psum(attn_parts[1].astype(jnp.bfloat16), "seq").astype(jnp.float32),
        lax.psum(feed_parts[0].astype(jnp.bfloat16), "seq").astype(jnp.float32),
        lax.psum(feed_parts[1].astype(jnp.bfloat16), "seq").astype(jnp.float32),
        lax.psum(feed_parts[2].astype(jnp.bfloat16), "seq").astype(jnp.float32),
        lax.psum(attn_parts[2].astype(jnp.bfloat16), "seq").astype(jnp.float32),
        lax.psum(attn_parts[3].astype(jnp.bfloat16), "seq").astype(jnp.float32),
        lax.psum(feed_parts[3].astype(jnp.bfloat16), "seq").astype(jnp.float32),
        lax.psum(feed_parts[4].astype(jnp.bfloat16), "seq").astype(jnp.float32),
    )
    return (
        layer_out,
        input_gradient[None],
        summed[0],
        summed[1],
        summed[2],
        summed[3],
        summed[4],
        summed[5],
        summed[6],
        summed[7],
        summed[8],
    )


def solution(mesh):
    return jax.shard_map(
        local,
        mesh=mesh,
        in_specs=(
            P("fsdp", "seq", None),
            P("fsdp", None),
            P("fsdp", None),
            P("fsdp", None),
            P("fsdp", None),
            P("fsdp", None),
            P("fsdp", None),
            P("fsdp"),
            P("fsdp"),
            P("fsdp"),
            P("fsdp"),
            P("fsdp", "seq", None),
        ),
        out_specs=(
            P("fsdp", "seq", None),
            P("fsdp", "seq", None),
            P("fsdp", None),
            P("fsdp", None),
            P("fsdp", None),
            P("fsdp", None),
            P("fsdp", None),
            P("fsdp"),
            P("fsdp"),
            P("fsdp"),
            P("fsdp"),
        ),
        check_vma=False,
    )
```

profile of v0, /device:TPU:9, one launch (start us, length us, event | category | flops | bytes accessed | tf_op | source)
XLA Modules:
  0.0 3974.6 jit_solution(10900901142298167609)
XLA Ops:
  10.0 45.1 %all-gather.1 = bf16[8,1,256]{2,1,0:T(2,128)(2,1)S(1)} all-gather(bf16[1,1,256]{2,1,0:T(2,128)(2,1)S(1)} %reshape.442), channel_id=1, replica_groups=mesh['seq'=4,'fsdp'=8] {'fsdp'}, dimensions={0}, use_global_device_ids=true | all-gather | bytes 4608 | tf_op jit(solution)/shard_map/all_gather | solution.py:204
  55.1 19.7 all-gather
  77.3 414.3 %all-gather.10.cloned.1.call-done = bf16[2048,6144]{1,0:T(8,128)(2,1)} async-done(((bf16[256,6144]{1,0:T(8,128)(2,1)}), bf16[2048,6144]{1,0:T(8,128)(2,1)}) %all-gather.10.cloned.1.call-update) | async-done | bytes 25165840 | tf_op jit(solution)/shard_map/all_gather | solution.py:201
  491.6 22.8 fusion.43
  544.5 34.2 all_to_all.131
  587.7 26.0 all-to-all-done.1
  656.5 308.9 %while.27 = (s32[]{:T(128)}, bf16[5,512,512]{2,1,0:T(8,128)(2,1)}, f32[5,8,512]{2,1,0:T(8,128)}, s32[5]{0:T(128)S(1)}, s32[2560]{0:T(1024)S(1)}, /*index=5*/bf16...) while((s32[]{:T(128)}, bf16[5,512,512]{2,1,0:T(8,128)(2,1)}, ...), condition=%wide.region_8.9_spmd, body=%wide.region_5.8_spmd.sunk | while | flops 2815687680 | bytes 151162096 | solution.py:119
  660.9 18.8 fusion.108
  679.7 18.9 fusion.109
  722.6 18.8 fusion.108
  741.4 18.9 fusion.109
  784.4 18.8 fusion.108
  803.2 18.9 fusion.109
  846.2 18.8 fusion.108
  865.0 18.9 fusion.109
  908.0 18.8 fusion.108
  926.8 18.9 fusion.109
  971.1 19.1 all-gather.3
  990.2 18.1 all-gather.2
  1025.6 34.2 all-gather.14.cloned.1.call-done
  1059.9 22.4 fusion.48
  1082.3 420.1 %all-gather.16.cloned.1.call-done = bf16[2048,5632]{1,0:T(8,128)(2,1)} async-done(((bf16[256,5632]{1,0:T(8,128)(2,1)}), bf16[2048,5632]{1,0:T(8,128)(2,1)}) %all-gather.16.cloned.1.call-update) | async-done | bytes 23068688 | tf_op jit(solution)/shard_map/all_gather | solution.py:210
  1502.4 23.3 fusion.49
  1525.7 419.2 %all-gather.18.cloned.1.call-done = bf16[5632,2048]{1,0:T(8,128)(2,1)} async-done(((bf16[704,2048]{1,0:T(8,128)(2,1)}), bf16[5632,2048]{1,0:T(8,128)(2,1)}) %all-gather.18.cloned.1.call-update) | async-done | bytes 23068688 | tf_op jit(solution)/shard_map/all_gather | solution.py:211
  1944.9 30.8 multiply_convert_fusion.1
  1975.7 21.8 fusion.50
  1997.5 23.7 multiply_reduce_fusion.1
  2034.9 26.0 convolution_convert_fusion.3
  2061.0 25.8 convolution_convert_fusion.2
  2103.3 24.5 convolution_convert_fusion.1
  2133.9 814.9 %while.28 = (s32[]{:T(128)}, f32[2560,8,64]{0,2,1:T(8,128)}, f32[2560,8,64]{0,2,1:T(8,128)}, f32[5,512,512]{1,0,2:T(8,128)}, s32[5]{0:T(128)S(1)}, /*index=5*/bf...) while((s32[]{:T(128)}, f32[2560,8,64]{0,2,1:T(8,128)}, ...), condition=%wide.region_15.16_spmd.clone, body=%wide.region_13.15_spmd.clone.sunk | while | flops 6817315840 | bytes 356633856 | solution.py:166
  2140.5 18.8 fusion.121
  2164.1 30.2 multiply_reduce_fusion.7
  2194.2 35.5 multiply_convert_fusion.5
  2273.6 21.9 dynamic_update_slice.20
  2301.8 18.4 fusion.121
  2324.9 30.5 multiply_reduce_fusion.7
  2355.5 35.1 multiply_convert_fusion.5
  2406.0 19.1 bitcast_add_fusion.5
  2437.7 21.7 dynamic_update_slice.20
  2465.8 18.2 fusion.121
  2488.8 30.3 multiply_reduce_fusion.7
  2519.1 34.7 multiply_convert_fusion.5
  2568.6 19.5 bitcast_add_fusion.5
  2600.7 21.9 dynamic_update_slice.20
  2628.9 18.4 fusion.121
  2652.0 30.3 multiply_reduce_fusion.7
  2682.3 35.1 multiply_convert_fusion.5
  2732.2 18.9 bitcast_add_fusion.5
  2763.9 21.8 dynamic_update_slice.20
  2792.0 18.5 fusion.121
  2815.2 30.1 multiply_reduce_fusion.7
  2845.3 34.9 multiply_convert_fusion.5
  2895.5 18.7 bitcast_add_fusion.5
  2926.9 21.7 dynamic_update_slice.20
  3009.6 22.0 all-to-all-done.6
  3031.6 35.9 all_to_all.132
  3067.5 27.9 convolution_convert_fusion
  3097.3 216.1 %reduce-scatter.14.cloned.1.call-done = bf16[704,2048]{1,0:T(8,128)(2,1)} async-done(((bf16[5632,2048]{1,0:T(8,128)(2,1)}), bf16[704,2048]{1,0:T(8,128)(2,1)}) %reduce-scatter.14.cloned.1.call-update) | async-done | bytes 2883600 | tf_op jit(solution)/shard_map/reduce_scatter | solution.py:274
  3313.4 406.9 %reduce-scatter.6.cloned.1.call-done = bf16[256,6144]{1,0:T(8,128)(2,1)} async-done(((bf16[2048,6144]{1,0:T(8,128)(2,1)}), bf16[256,6144]{1,0:T(8,128)(2,1)}) %reduce-scatter.6.cloned.1.call-update) | async-done | bytes 3145744 | tf_op jit(solution)/shard_map/reduce_scatter | solution.py:311
  3720.3 23.6 fusion.31
  3743.9 29.3 fusion.28
  3773.2 27.8 all-reduce.4
  3822.9 127.9 %all-reduce.9.cloned.1.call-done = (bf16[256,6144]{1,0:T(8,128)(2,1)}, bf16[256,2048]{1,0:T(8,128)(2,1)}, bf16[256,5632]{1,0:T(8,128)(2,1)}, bf16[256,5632]{1,0:T(8,128)(2,1)}, bf16[704,2048]{1,0:T(8,128)(2,1)}) async-done(((bf16[256,6144]{1,0:T(8,128)(2,1)}, bf16[256,2048]{1,0:T(8,128)(2,1)}, bf16[256,5632]{1,0:T(8,128)(2,1)}, bf16[256,5632]{1,0:T(8,128)(2,1)}, bf16[704,2048]{1,0:T(8,128)(2,1)}), ...) | async-done | bytes 12845072 | tf_op jit(solution)/shard_map/psum | solution.py:331
  (319 shorter events, 560.6 us)
Async XLA Ops:
  7.2 2.8 copy-start.30
  7.2 47.9 %copy-start.31 = (bf16[256]{0:T(256)(128)(2,1)S(1)}, bf16[256]{0:T(256)(128)(2,1)}, u32[]{:S(2)}) copy-start(bf16[256]{0:T(256)(128)(2,1)} %param.23) | copy-start | bytes 1540
  7.2 67.7 %copy-start.32 = (s32[1,2]{1,0:T(1,128)S(1)}, s32[1,2]{1,0:T(1,128)}, u32[]{:S(2)}) copy-start(s32[1,2]{1,0:T(1,128)} %param.17) | copy-start | bytes 28
  7.2 68.7 %copy-start.3 = (bf16[1,640,2048]{2,1,0:T(8,128)(2,1)S(1)}, bf16[1,640,2048]{2,1,0:T(8,128)(2,1)}, u32[]{:S(2)}) copy-start(bf16[1,640,2048]{2,1,0:T(8,128)(2,1)} %param.16) | copy-start | bytes 7864324
  7.2 484.4 %all-gather.10.cloned.1.call-start = ((), (), s32[]{:S(2)}) async-start(), calls=%async_computation.13 | async-start | bytes 28311552 | tf_op jit(solution)/shard_map/all_gather | solution.py:201
  8.0 1005.2 %all-gather.12.cloned.1.call-start = ((), (), s32[]{:S(2)}) async-start(), calls=%async_computation.14 | async-start | bytes 9437184 | tf_op jit(solution)/shard_map/all_gather | solution.py:202
  8.7 1051.2 %all-gather.14.cloned.1.call-start = ((), (), s32[]{:S(2)}) async-start(), calls=%async_computation.15 | async-start | bytes 25952256 | tf_op jit(solution)/shard_map/all_gather | solution.py:209
  9.4 1492.9 %all-gather.16.cloned.1.call-start = ((), (), s32[]{:S(2)}) async-start(), calls=%async_computation.16 | async-start | bytes 25952256 | tf_op jit(solution)/shard_map/all_gather | solution.py:210
  55.1 459.3 %copy-start.24 = (f32[8,1,256]{2,1,0:T(1,128)}, f32[8,1,256]{2,1,0:T(1,128)S(1)}, u32[]{:S(2)}) copy-start(f32[8,1,256]{2,1,0:T(1,128)S(1)} %convert_element_type.216) | copy-start | bytes 24580
  74.8 439.6 %copy-start.20 = (f32[8,1,256]{2,1,0:T(1,128)}, f32[8,1,256]{2,1,0:T(1,128)S(1)}, u32[]{:S(2)}) copy-start(f32[8,1,256]{2,1,0:T(1,128)S(1)} %convert_element_type.215) | copy-start | bytes 24580
  75.1 2.1 copy-start.28
  76.3 438.1 %copy-start.18 = (f32[640]{0:T(1024)}, f32[640]{0:T(1024)S(1)}, u32[]{:S(2)}) copy-start(f32[640]{0:T(1024)S(1)} %broadcast_multiply_fusion.5) | copy-start | bytes 7684
  77.2 437.3 %copy-start.22 = (f32[640]{0:T(1024)}, f32[640]{0:T(1024)S(1)}, u32[]{:S(2)}) copy-start(f32[640]{0:T(1024)S(1)} %add_rsqrt_fusion.1) | copy-start | bytes 7684
  578.7 34.9 all-to-all-start.1
  613.7 35.9 all-to-all-start.2
  619.0 1325.9 %all-gather.18.cloned.1.call-start = ((), (), s32[]{:S(2)}) async-start(), calls=%async_computation.17 | async-start | bytes 25952256 | tf_op jit(solution)/shard_map/all_gather | solution.py:211
  679.7 18.9 copy-start.1
  741.4 18.9 copy-start.1
  803.2 18.9 copy-start.1
  865.0 18.9 copy-start.1
  926.8 18.9 copy-start.1
  965.3 47.8 %copy-start.8 = (s32[2560]{0:T(1024)}, s32[2560]{0:T(1024)S(1)}, u32[]{:S(2)}) copy-start(s32[2560]{0:T(1024)S(1)} %get-tuple-element.568) | copy-start | bytes 30724
  965.3 5.7 copy-start.33
  965.3 24.9 copy-start.34
  965.3 47.8 %copy-start.4 = (bf16[1,640,2048]{2,1,0:T(8,128)(2,1)S(1)}, bf16[1,640,2048]{2,1,0:T(8,128)(2,1)}, u32[]{:S(2)}) copy-start(bf16[1,640,2048]{2,1,0:T(8,128)(2,1)} %param.16) | copy-start | bytes 7864324
  965.3 43.0 %all-to-all-start.3 = ((bf16[4,640,512]{2,1,0:T(8,128)(2,1)}), bf16[4,640,512]{2,1,0:T(8,128)(2,1)}, u32[]{:S(2)}, u32[]{:S(2)}) async-start(bf16[4,640,512]{2,1,0:T(8,128)(2,1)} %bitcast.228), calls=%async_computation.3 | async-start | bytes 5242880 | tf_op jit(solution)/shard_map/all_to_all | solution.py:232
  971.1 2126.2 %reduce-scatter.8.cloned.1.call-start = ((), (), s32[]{:S(2)}) async-start(), calls=%async_computation.19 | async-start | bytes 9437184 | tf_op jit(solution)/shard_map/reduce_scatter | solution.py:317
  1022.3 2.4 copy-start.2
  1025.6 34.2 copy-start.14
  1082.3 862.6 %copy-start.13 = (bf16[1,640,2048]{2,1,0:T(8,128)(2,1)S(1)}, bf16[1,640,2048]{2,1,0:T(8,128)(2,1)}, u32[]{:S(2)}) copy-start(bf16[1,640,2048]{2,1,0:T(8,128)(2,1)} %param.27) | copy-start | bytes 7864324
  1975.7 45.6 %slice-start = ((s8[5242880]{0:T(1024)(128)(4,1)}), s8[4194304]{0:T(1024)(128)(4,1)S(1)}, s32[]{:S(2)}) async-start(s8[5242880]{0:T(1024)(128)(4,1)} %bitcast.210), calls=%async_computation.24 | async-start | bytes 8388608
  1997.5 23.8 slice-start.1
  2021.3 4.5 copy-start.15
  2023.5 2.4 copy-start.6
  2034.9 1062.4 %reduce-scatter.10.cloned.1.call-start = ((), (), s32[]{:S(2)}) async-start(), calls=%async_computation.20 | async-start | bytes 25952256 | tf_op jit(solution)/shard_map/reduce_scatter | solution.py:262
  2061.0 1036.3 %reduce-scatter.12.cloned.1.call-start = ((), (), s32[]{:S(2)}) async-start(), calls=%async_computation.21 | async-start | bytes 25952256 | tf_op jit(solution)/shard_map/reduce_scatter | solution.py:268
  2098.3 35.6 all-to-all-start.4
  2103.3 1210.1 %reduce-scatter.14.cloned.1.call-start = ((), (), s32[]{:S(2)}) async-start(), calls=%async_computation.22 | async-start | bytes 25952256 | tf_op jit(solution)/shard_map/reduce_scatter | solution.py:274
  2127.8 6.0 copy-start
  2127.8 6.0 copy-start.9
  2958.3 6.6 copy-start.17
  2958.4 6.6 copy-start.29
  2960.2 35.4 all-to-all-start.7
  2977.7 2.4 copy-start.7
  2995.5 36.0 all-to-all-start.6
  3001.0 719.3 %reduce-scatter.6.cloned.1.call-start = ((), (), s32[]{:S(2)}) async-start(), calls=%async_computation.18 | async-start | bytes 28311552 | tf_op jit(solution)/shard_map/reduce_scatter | solution.py:311
  3005.9 61.6 %copy-start.5 = (bf16[1,640,2048]{2,1,0:T(8,128)(2,1)S(1)}, bf16[1,640,2048]{2,1,0:T(8,128)(2,1)}, u32[]{:S(2)}) copy-start(bf16[1,640,2048]{2,1,0:T(8,128)(2,1)} %param.16) | copy-start | bytes 7864324
  3005.9 61.6 %copy-start.19 = (f32[640]{0:T(1024)S(1)}, f32[640]{0:T(1024)}, u32[]{:S(2)}) copy-start(f32[640]{0:T(1024)} %copy-done.18) | copy-start | bytes 7684
  3005.9 61.6 %copy-start.21 = (f32[8,1,256]{2,1,0:T(1,128)S(1)}, f32[8,1,256]{2,1,0:T(1,128)}, u32[]{:S(2)}) copy-start(f32[8,1,256]{2,1,0:T(1,128)} %copy-done.20) | copy-start | bytes 24580
  3005.9 61.6 %copy-start.23 = (f32[640]{0:T(1024)S(1)}, f32[640]{0:T(1024)}, u32[]{:S(2)}) copy-start(f32[640]{0:T(1024)} %copy-done.22) | copy-start | bytes 7684
  3005.9 61.6 %copy-start.25 = (f32[8,1,256]{2,1,0:T(1,128)S(1)}, f32[8,1,256]{2,1,0:T(1,128)}, u32[]{:S(2)}) copy-start(f32[8,1,256]{2,1,0:T(1,128)} %copy-done.24) | copy-start | bytes 24580
  3095.3 0.7 copy-start.35
  3095.4 855.5 %all-reduce.9.cloned.1.call-start = ((), (), s32[]{:S(2)}) async-start(), calls=%async_computation.23 | async-start | bytes 25690112 | tf_op jit(solution)/shard_map/psum | solution.py:331
  3743.9 29.3 copy-start.26
  3743.9 29.3 copy-start.27
  3950.9 5.5 copy-start.16
  3950.9 7.1 copy-start.12
  3956.4 4.8 copy-start.11
  3961.1 3.2 copy-start.10
Sparse Core Ops, SparseCore 0:
  9.6 481.9 all-gather.9
  493.7 122.4 all-gather.11
  617.8 442.0 all-gather.13
  1061.2 441.0 all-gather.15
  1503.7 441.0 all-gather.17
  2035.0 147.8 reduce-scatter.7
  2187.2 371.8 reduce-scatter.9
  2563.5 372.7 reduce-scatter.11
  2940.6 372.7 reduce-scatter.13
  3317.6 402.6 reduce-scatter.5
  3723.6 227.2 all-reduce.8
where the time goes:
time: 3990 us; the launch traced here: 3970 us
  waiting for transfers between devices  2120 us (53%)
  matrix products  978 us (25%)
  other arithmetic  336 us (8%)
  local copies, waits for them, and re-layouts  266 us (7%)
  blocking collectives  213 us (5%)
    all_gather x1, waiting for transfers between devices, fetch_feed(): lax.all_gather(up_weight, 'fsdp', axis=0, tiled=True)  420 us
    all_gather x1, waiting for transfers between devices, fetch_feed(): lax.all_gather(down_weight, 'fsdp', axis=0, tiled=True)  419 us
    all_gather x1, waiting for transfers between devices, fetch_attention(): lax.all_gather(project_in, 'fsdp', axis=0, tiled=True)  414 us
    reduce_scatter x1, waiting for transfers between devices, local(): lax.psum_scatter(contract_first(normed_first, grad_mixed).astype(jnp.bflo...  407 us
    dot_general x10, matrix products, block_scores(): jnp.einsum('qhd,khd->hqk', query_block, key_heads, preferred_element_type...  245 us
    reduce_scatter x1, waiting for transfers between devices, local(): lax.psum_scatter(contract_first(product, upstream).astype(jnp.bfloat16),...  216 us
    convert_element_type x5, other arithmetic, one_block(): grad_scores = (chances * (grad_chances - jnp.sum(chances * grad_chances,...  175 us
    psum x1, waiting for transfers between devices, local(): lax.psum(attn_parts[0].astype(jnp.bfloat16), 'seq').astype(jnp.float32)  128 us
  transfers between devices with their start and end apart: 17, of which 12 were waited for; matrix products, arithmetic and copies ran while one was open for 37% of the time, Pallas kernels for 0%

commit v1 on v0

v1 whole, which is shorter than its diff:
```python
import functools

import jax
import jax.numpy as jnp
from jax import lax
from jax.experimental import pallas as pl
from jax.experimental.pallas import tpu as pltpu
from jax.sharding import PartitionSpec as P

HEAD_DIM = 64
ROT = 16
PROMPT = 2048
LANES = 128

epsilon = 1e-05
rope_base = 10000.0

BF16 = jnp.bfloat16
F32 = jnp.float32
CORES = 2
VMEM_LIMIT = 56 * 1024 * 1024


def dot_last(left_side, right_side):
    return lax.dot_general(
        left_side, right_side, (((1,), (1,)), ((), ())), preferred_element_type=F32
    )


def dot_first(left_side, right_side):
    return lax.dot_general(
        left_side, right_side, (((0,), (0,)), ((), ())), preferred_element_type=F32
    )


def dot(left_side, right_side):
    return jnp.dot(left_side, right_side, preferred_element_type=F32)


def cont_ends(lengths):
    count = lengths.shape[0]
    before = jnp.arange(count)[None, :] <= jnp.arange(count)[:, None]
    return jnp.sum(jnp.where(before, lengths[None, :], 0), axis=1)


def rope_tables(lengths, total_rows):
    ends = cont_ends(lengths)
    starts = ends - lengths
    indices = jnp.arange(total_rows, dtype=jnp.int32)
    offset = indices - PROMPT
    inside = (offset[:, None] >= starts[None, :]) & (offset[:, None] < ends[None, :])
    seg_begin = jnp.sum(jnp.where(inside, starts[None, :], 0), axis=1)
    position = jnp.where(indices < PROMPT, indices, PROMPT + offset - seg_begin)
    half = ROT // 2
    within = jnp.arange(LANES, dtype=jnp.int32) % HEAD_DIM
    frequency = rope_base ** (-2.0 * (within % half).astype(F32) / ROT)
    angles = position.astype(F32)[:, None] * frequency[None, :]
    turning = (within < ROT)[None, :]
    sign = jnp.where(within < half, -1.0, 1.0)[None, :]
    cosine = jnp.where(turning, jnp.cos(angles), 1.0)
    sine = jnp.where(turning, sign * jnp.sin(angles), 0.0)
    return cosine, sine, ends


def turn(rows_in, cosine, sine):
    half = ROT // 2
    lane = lax.broadcasted_iota(jnp.int32, rows_in.shape, 1) % HEAD_DIM
    partner = jnp.where(
        lane < half,
        pltpu.roll(rows_in, LANES - half, 1),
        pltpu.roll(rows_in, half, 1),
    )
    return rows_in * cosine + partner * sine


def project_kernel(x_ref, w_ref, cos_ref, sin_ref, out_ref):
    cosine = cos_ref[...]
    sine = sin_ref[...]
    pairs = out_ref.shape[1] // (3 * LANES)
    x = x_ref[...]
    for pair in range(pairs):
        base = 3 * LANES * pair
        mixed = dot(x, w_ref[:, base : base + 3 * LANES])
        query = turn(mixed[:, :LANES], cosine, sine) * HEAD_DIM ** (-0.5)
        key = turn(mixed[:, LANES : 2 * LANES], cosine, sine)
        out_ref[:, base : base + LANES] = query.astype(BF16)
        out_ref[:, base + LANES : base + 2 * LANES] = key.astype(BF16)
        out_ref[:, base + 2 * LANES : base + 3 * LANES] = mixed[:, 2 * LANES :].astype(BF16)


def project(x, weight, cosine, sine):
    rows, depth = x.shape
    columns = weight.shape[1]
    block = 512
    return pl.pallas_call(
        project_kernel,
        grid=(rows // block,),
        in_specs=[
            pl.BlockSpec((block, depth), lambda i: (i, 0)),
            pl.BlockSpec((depth, columns), lambda i: (0, 0), pipeline_mode=pl.Buffered(1)),
            pl.BlockSpec((block, LANES), lambda i: (i, 0)),
            pl.BlockSpec((block, LANES), lambda i: (i, 0)),
        ],
        out_specs=pl.BlockSpec((block, columns), lambda i: (i, 0)),
        out_shape=jax.ShapeDtypeStruct((rows, columns), BF16),
        compiler_params=pltpu.CompilerParams(vmem_limit_bytes=VMEM_LIMIT),
        cost_estimate=pl.CostEstimate(
            flops=2 * rows * depth * columns,
            bytes_accessed=2 * (rows * depth + depth * columns + rows * columns),
            transcendentals=0,
        ),
        name="project_in_rope",
    )(x, weight, cosine, sine)


BLOCK = 512
NEG = -1e30


def segment_of(index, ends_ref):
    count = jnp.zeros_like(index)
    for c in range(ends_ref.shape[0] - 1):
        count = count + (index >= PROMPT + ends_ref[c]).astype(jnp.int32)
    return count


def attend_kernel(ends_ref, q_ref, k_ref, v_ref, o_ref, qx_ref):
    number = pl.program_id(1)
    lane = lax.broadcasted_iota(jnp.int32, (BLOCK, LANES), 1)
    q = q_ref[...]
    inside = [lane < HEAD_DIM, lane >= HEAD_DIM]
    q_head = [jnp.where(inside[h], q, jnp.zeros_like(q)) for h in range(2)]

    def step(start, carry, masked):
        k = k_ref[pl.ds(start, BLOCK), :]
        v = v_ref[pl.ds(start, BLOCK), :]
        if masked:
            row = lax.broadcasted_iota(jnp.int32, (BLOCK, 1), 0) + start
            col = lax.broadcasted_iota(jnp.int32, (1, BLOCK), 1) + start
            visible = (col <= row) & (segment_of(row, ends_ref) == segment_of(col, ends_ref))
        new = []
        for h in range(2):
            peak, acc = carry[h]
            scores = dot_last(q_head[h], k)
            if masked:
                scores = jnp.where(visible, scores, NEG)
            higher = jnp.maximum(peak, jnp.max(scores, axis=1, keepdims=True))
            weights = jnp.exp(scores - higher)
            shrink = jnp.exp(peak - higher)
            v_one = jnp.where(inside[h], v, jnp.ones_like(v))
            acc = acc * shrink + dot(weights.astype(BF16), v_one)
            new.append((higher, acc))
        return tuple(new)

    init = tuple(
        (jnp.full((BLOCK, 1), NEG, F32), jnp.zeros((BLOCK, LANES), F32)) for _ in range(2)
    )
    carry = lax.fori_loop(
        0, number, lambda j, c: step(pl.multiple_of(j * BLOCK, BLOCK), c, False), init
    )
    carry = step(pl.multiple_of(number * BLOCK, BLOCK), carry, True)
    outs = []
    for h in range(2):
        peak, acc = carry[h]
        outs.append(acc / pltpu.roll(acc, HEAD_DIM, 1))
        total = jnp.where(inside[h], 1.0, acc)
        minus = -(peak + jnp.log(total))
        high = minus.astype(BF16)
        rest = minus - high.astype(F32)
        mid = rest.astype(BF16)
        low = (rest - mid.astype(F32)).astype(BF16)
        base = HEAD_DIM * (1 - h)
        zero = jnp.zeros_like(high)
        spare = jnp.where(lane == base, high, jnp.where(lane == base + 1, mid, zero))
        spare = jnp.where(lane == base + 2, low, spare)
        qx_ref[h] = jnp.where(inside[h], q, spare)
    o_ref[...] = jnp.where(inside[0], outs[0], outs[1]).astype(BF16)


def attend(ends, qkv):
    rows, columns = qkv.shape
    pairs = columns // (3 * LANES)
    blocks = rows // BLOCK
    work = rows * rows // 2 * pairs * 2
    return pl.pallas_call(
        attend_kernel,
        grid_spec=pltpu.PrefetchScalarGridSpec(
            num_scalar_prefetch=1,
            grid=(pairs, blocks),
            in_specs=[
                pl.BlockSpec((BLOCK, LANES), lambda p, i, e: (i, 3 * p)),
                pl.BlockSpec((rows, LANES), lambda p, i, e: (0, 3 * p + 1)),
                pl.BlockSpec((rows, LANES), lambda p, i, e: (0, 3 * p + 2)),
            ],
            out_specs=[
                pl.BlockSpec((BLOCK, LANES), lambda p, i, e: (i, p)),
                pl.BlockSpec((2, BLOCK, LANES), lambda p, i, e: (p, i, 0)),
            ],
        ),
        out_shape=[
            jax.ShapeDtypeStruct((rows, pairs * LANES), BF16),
            jax.ShapeDtypeStruct((2 * pairs, rows, LANES), BF16),
        ],
        compiler_params=pltpu.CompilerParams(vmem_limit_bytes=VMEM_LIMIT),
        cost_estimate=pl.CostEstimate(
            flops=work * 1024, bytes_accessed=2 * rows * columns * 3, transcendentals=work
        ),
        name="attend",
    )(ends, qkv, qkv, qkv)


def attend_back_kernel(
    ends_ref, qx_ref, k_ref, v_ref, g_ref, o_ref, cos_ref, sin_ref, out_ref,
    gx_ref, dq_ref, dk_ref, dv_ref,
):
    number = pl.program_id(1)
    blocks = pl.num_programs(1)
    rows = qx_ref.shape[1]
    lane = lax.broadcasted_iota(jnp.int32, (BLOCK, LANES), 1)
    inside = [lane < HEAD_DIM, lane >= HEAD_DIM]

    @pl.when(number == 0)
    def _():
        dq_ref[...] = jnp.zeros_like(dq_ref)

        @pl.loop(0, rows // BLOCK)
        def _(j):
            here = pl.ds(pl.multiple_of(j * BLOCK, BLOCK), BLOCK)
            g = g_ref[here, :]
            both = g.astype(F32) * o_ref[here, :].astype(F32)
            for h in range(2):
                minus = -jnp.sum(jnp.where(inside[h], both, 0.0), axis=1, keepdims=True)
                high = minus.astype(BF16)
                rest = minus - high.astype(F32)
                mid = rest.astype(BF16)
                low = (rest - mid.astype(F32)).astype(BF16)
                base = HEAD_DIM * (1 - h)
                spare = jnp.where(
                    lane == base, high, jnp.where(lane == base + 1, mid, jnp.zeros_like(g))
                )
                spare = jnp.where(lane == base + 2, low, spare)
                gx_ref[h, here, :] = jnp.where(inside[h], g, spare)

    k = k_ref[...]
    v = v_ref[...]
    k_one = [jnp.where(inside[h], k, jnp.ones_like(k)) for h in range(2)]
    v_one = [jnp.where(inside[h], v, jnp.ones_like(v)) for h in range(2)]
    k_turned = [jnp.where(inside[h], k, jnp.zeros_like(k)).T for h in range(2)]
    dk_ref[...] = jnp.zeros_like(dk_ref)
    dv_ref[...] = jnp.zeros_like(dv_ref)

    def step(start, masked):
        here = pl.ds(start, BLOCK)
        if masked:
            row = lax.broadcasted_iota(jnp.int32, (1, BLOCK), 1) + start
            col = lax.broadcasted_iota(jnp.int32, (BLOCK, 1), 0) + start
            visible = (col <= row) & (segment_of(row, ends_ref) == segment_of(col, ends_ref))
        total = None
        for h in range(2):
            qx = qx_ref[h, here, :]
            gx = gx_ref[h, here, :]
            chances = jnp.exp(dot_last(k_one[h], qx))
            if masked:
                chances = jnp.where(visible, chances, 0.0)
            dv_ref[h] += dot(chances.astype(BF16), gx)
            grad_scores = (chances * dot_last(v_one[h], gx)).astype(BF16)
            dk_ref[h] += dot(grad_scores, qx)
            part = dot(k_turned[h], grad_scores)
            total = part if total is None else total + part
        dq_ref[:, here] += total

    step(pl.multiple_of(number * BLOCK, BLOCK), True)

    @pl.loop(number + 1, blocks)
    def _(j):
        step(pl.multiple_of(j * BLOCK, BLOCK), False)

    here = pl.ds(pl.multiple_of(number * BLOCK, BLOCK), BLOCK)
    dk = jnp.where(inside[0], dk_ref[0], dk_ref[1])
    dk = turn(dk, cos_ref[here, :], -sin_ref[here, :])
    out_ref[here, LANES : 2 * LANES] = dk.astype(BF16)
    out_ref[here, 2 * LANES :] = jnp.where(inside[0], dv_ref[0], dv_ref[1]).astype(BF16)

    @pl.when(number == blocks - 1)
    def _():
        for j in range(rows // BLOCK):
            here = slice(j * BLOCK, (j + 1) * BLOCK)
            dq = dq_ref[:, here].T * HEAD_DIM ** (-0.5)
            dq = turn(dq, cos_ref[here, :], -sin_ref[here, :])
            out_ref[here, :LANES] = dq.astype(BF16)


def attend_back(ends, qkv, qx, grad, attended, cosine, sine):
    rows, columns = qkv.shape
    pairs = columns // (3 * LANES)
    blocks = rows // BLOCK
    work = rows * rows // 2 * pairs * 2
    return pl.pallas_call(
        attend_back_kernel,
        grid_spec=pltpu.PrefetchScalarGridSpec(
            num_scalar_prefetch=1,
            grid=(pairs, blocks),
            in_specs=[
                pl.BlockSpec((2, rows, LANES), lambda p, i, e: (p, 0, 0)),
                pl.BlockSpec((BLOCK, LANES), lambda p, i, e: (i, 3 * p + 1)),
                pl.BlockSpec((BLOCK, LANES), lambda p, i, e: (i, 3 * p + 2)),
                pl.BlockSpec((rows, LANES), lambda p, i, e: (0, p)),
                pl.BlockSpec((rows, LANES), lambda p, i, e: (0, p)),
                pl.BlockSpec((rows, LANES), lambda p, i, e: (0, 0)),
                pl.BlockSpec((rows, LANES), lambda p, i, e: (0, 0)),
            ],
            out_specs=pl.BlockSpec((rows, 3 * LANES), lambda p, i, e: (0, p)),
            scratch_shapes=[
                pltpu.VMEM((2, rows, LANES), BF16),
                pltpu.VMEM((LANES, rows), F32),
                pltpu.VMEM((2, BLOCK, LANES), F32),
                pltpu.VMEM((2, BLOCK, LANES), F32),
            ],
        ),
        out_shape=jax.ShapeDtypeStruct((rows, columns), BF16),
        compiler_params=pltpu.CompilerParams(vmem_limit_bytes=VMEM_LIMIT),
        cost_estimate=pl.CostEstimate(
            flops=work * 2560, bytes_accessed=2 * rows * columns * 4, transcendentals=work
        ),
        name="attend_back",
    )(ends, qx, qkv, qkv, grad, attended, cosine, sine)


def seq_shift(value, chips, shift):
    size = chips * CORES
    return lax.ppermute(
        value, "seq", [(i, (i + shift * CORES) % size) for i in range(size)]
    )


def core_swap(value, chips):
    return lax.ppermute(value, "seq", [(i, i ^ 1) for i in range(chips * CORES)])


def gather_rows(block, chips):
    rows = block.shape[0]
    me = lax.axis_index("seq")
    core = me % CORES
    chip = me // CORES
    whole = jnp.zeros((rows * chips * CORES,) + block.shape[1:], block.dtype)
    for shift in range(chips):
        mine = block if shift == 0 else seq_shift(block, chips, shift)
        other = core_swap(mine, chips)
        source = (chip + chips - shift) % chips
        for held, which in ((mine, core), (other, 1 - core)):
            start = (source * CORES + which) * rows
            whole = lax.dynamic_update_slice_in_dim(whole, held, start, 0)
    return whole


def scatter_rows(partial, chips):
    rows = partial.shape[0] // (chips * CORES)
    me = lax.axis_index("seq")
    core = me % CORES
    chip = me // CORES

    def block_of(which_chip, which_core):
        start = (which_chip * CORES + which_core) * rows
        return lax.dynamic_slice_in_dim(partial, start, rows, 0)

    summed = []
    for shift in range(chips):
        target = (chip + shift) % chips
        theirs = core_swap(block_of(target, 1 - core), chips)
        summed.append(block_of(target, core).astype(F32) + theirs.astype(F32))
    total = summed[0]
    for shift in range(1, chips):
        total = total + seq_shift(summed[shift].astype(BF16), chips, shift).astype(F32)
    return total


def exchange_shards(value, seq_size, fsdp_size, back):
    ratio = fsdp_size // seq_size
    pairs = []
    for shard in range(fsdp_size):
        for copy in range(seq_size):
            source = copy * fsdp_size + shard
            target = (shard // ratio) * fsdp_size + (shard % ratio) * seq_size + copy
            pairs.append((target, source) if back else (source, target))
    return lax.ppermute(value, ("seq", "fsdp"), pairs)


def unit_rows(rows_in):
    mean_value = jnp.mean(rows_in, axis=-1, keepdims=True)
    centered = rows_in - mean_value
    inverse = lax.rsqrt(jnp.mean(centered * centered, axis=-1, keepdims=True) + epsilon)
    return centered * inverse, inverse


def norm_backward(gradient, unit, inverse, gain):
    scaled = gradient * gain
    mean_value = jnp.mean(scaled, axis=-1, keepdims=True)
    along = jnp.mean(scaled * unit, axis=-1, keepdims=True)
    return inverse * (scaled - mean_value - unit * along)


def gather_fsdp(value):
    return lax.all_gather(value, "fsdp", axis=0, tiled=True)


def scatter_fsdp(value):
    return lax.psum_scatter(value, "fsdp", scatter_dimension=0, tiled=True)


def local(
    tokens,
    cont_lengths,
    project_in,
    project_out,
    gate_weight,
    up_weight,
    down_weight,
    first_gain,
    first_bias,
    second_gain,
    second_bias,
    grad_output,
):
    rows_dev, width = tokens.shape[1:]
    seq_size = lax.axis_size("seq")
    fsdp_size = lax.axis_size("fsdp")
    chips = seq_size // CORES
    total_rows = rows_dev * seq_size
    me = lax.axis_index("seq")
    shard_rows = project_in.shape[0]
    hidden_units = gate_weight.shape[1]
    own_units = hidden_units // seq_size
    own_pairs = width // LANES // seq_size
    pieces_out = project_out.shape[0] // seq_size
    pieces_down = down_weight.shape[0] // seq_size

    in_cols = lax.dynamic_slice_in_dim(
        project_in.reshape(shard_rows, 3, width), me * own_pairs * LANES, own_pairs * LANES, 2
    )
    in_part = jnp.concatenate(
        [
            in_cols[:, part, pair * LANES : (pair + 1) * LANES]
            for pair in range(own_pairs)
            for part in range(3)
        ],
        axis=1,
    )
    gate_part = lax.dynamic_slice_in_dim(gate_weight, me * own_units, own_units, 1)
    up_part = lax.dynamic_slice_in_dim(up_weight, me * own_units, own_units, 1)
    out_piece = exchange_shards(
        lax.dynamic_slice_in_dim(project_out, me * pieces_out, pieces_out, 0),
        seq_size, fsdp_size, False,
    )
    down_piece = exchange_shards(
        lax.dynamic_slice_in_dim(down_weight, me * pieces_down, pieces_down, 0),
        seq_size, fsdp_size, False,
    )
    vectors = gather_fsdp(
        jnp.stack([first_gain, first_bias, second_gain, second_bias], axis=1)
    ).astype(F32)
    gain_one, bias_one, gain_two, bias_two = [vectors[:, i] for i in range(4)]
    w_in = gather_fsdp(in_part)
    w_out = gather_fsdp(out_piece)
    w_gate = gather_fsdp(gate_part)
    w_up = gather_fsdp(up_part)
    w_down = gather_fsdp(down_piece)

    cosine, sine, ends = rope_tables(cont_lengths[0], total_rows)

    residual = tokens[0].astype(F32)
    all_tokens = gather_rows(tokens[0], chips)
    all_unit, _ = unit_rows(all_tokens.astype(F32))
    normed_first = (all_unit * gain_one + bias_one).astype(BF16)
    qkv = project(normed_first, w_in, cosine, sine)
    attended, qx = attend(ends, qkv)
    hidden = residual + scatter_rows(dot(attended, w_out).astype(BF16), chips)
    unit_two, inverse_two = unit_rows(hidden)
    normed_second = gather_rows((unit_two * gain_two + bias_two).astype(BF16), chips)
    all_upstream = gather_rows(grad_output[0], chips)

    gate_pre = dot(normed_second, w_gate)
    up_pre = dot(normed_second, w_up)
    sigmoid = jax.nn.sigmoid(gate_pre)
    silu = gate_pre * sigmoid
    product = (silu * up_pre).astype(BF16)
    grad_mid = dot_last(all_upstream, w_down)
    grad_gate = (grad_mid * up_pre * sigmoid * (1.0 + gate_pre * (1.0 - sigmoid))).astype(BF16)
    grad_up = (grad_mid * silu).astype(BF16)

    second_gradient = scatter_rows(
        (dot_last(grad_gate, w_gate) + dot_last(grad_up, w_up)).astype(BF16), chips
    )
    upstream = grad_output[0].astype(F32)
    grad_hidden = upstream + norm_backward(second_gradient, unit_two, inverse_two, gain_two)
    low_hidden = gather_rows(grad_hidden.astype(BF16), chips)

    layer_rows = hidden + scatter_rows(dot(product, w_down).astype(BF16), chips)

    grad_gate_piece = scatter_fsdp(dot_first(normed_second, grad_gate).astype(BF16))
    grad_up_piece = scatter_fsdp(dot_first(normed_second, grad_up).astype(BF16))
    grad_down_piece = scatter_fsdp(dot_first(product, all_upstream).astype(BF16))

    grad_attended = dot_last(low_hidden, w_out).astype(BF16)
    grad_out_piece = scatter_fsdp(dot_first(attended, low_hidden).astype(BF16))
    grad_qkv = attend_back(ends, qkv, qx, grad_attended, attended, cosine, sine)
    grad_in_piece = scatter_fsdp(dot_first(normed_first, grad_qkv).astype(BF16))
    first_gradient = scatter_rows(dot_last(grad_qkv, w_in).astype(BF16), chips)
    unit_one, inverse_one = unit_rows(residual)
    input_gradient = grad_hidden + norm_backward(first_gradient, unit_one, inverse_one, gain_one)

    sums = jnp.stack(
        [
            jnp.sum(first_gradient * unit_one, axis=0),
            jnp.sum(first_gradient, axis=0),
            jnp.sum(second_gradient * unit_two, axis=0),
            jnp.sum(second_gradient, axis=0),
        ],
        axis=1,
    )
    sums = lax.psum(scatter_fsdp(sums), "seq")

    def gathered(piece):
        return gather_rows(piece, chips).reshape((seq_size,) + piece.shape)

    grad_in = gathered(grad_in_piece).reshape(seq_size, shard_rows, own_pairs, 3, LANES)
    grad_in = jnp.transpose(grad_in, (1, 3, 0, 2, 4)).reshape(shard_rows, 3 * width).astype(F32)
    grad_gate_w = jnp.transpose(gathered(grad_gate_piece), (1, 0, 2)).reshape(gate_weight.shape)
    grad_up_w = jnp.transpose(gathered(grad_up_piece), (1, 0, 2)).reshape(up_weight.shape)
    grad_out = gather_rows(exchange_shards(grad_out_piece, seq_size, fsdp_size, True), chips)
    grad_down = gather_rows(exchange_shards(grad_down_piece, seq_size, fsdp_size, True), chips)

    return (
        layer_rows.astype(BF16)[None],
        input_gradient[None],
        grad_in,
        grad_out.astype(F32),
        grad_gate_w.astype(F32),
        grad_up_w.astype(F32),
        grad_down.astype(F32),
        sums[:, 0],
        sums[:, 1],
        sums[:, 2],
        sums[:, 3],
    )


def solution(mesh):
    return jax.shard_map(
        local,
        mesh=mesh,
        in_specs=(
            P("fsdp", "seq", None),
            P("fsdp", None),
            P("fsdp", None),
            P("fsdp", None),
            P("fsdp", None),
            P("fsdp", None),
            P("fsdp", None),
            P("fsdp"),
            P("fsdp"),
            P("fsdp"),
            P("fsdp"),
            P("fsdp", "seq", None),
        ),
        out_specs=(
            P("fsdp", "seq", None),
            P("fsdp", "seq", None),
            P("fsdp", None),
            P("fsdp", None),
            P("fsdp", None),
            P("fsdp", None),
            P("fsdp", None),
            P("fsdp"),
            P("fsdp"),
            P("fsdp"),
            P("fsdp"),
        ),
        check_vma=False,
    )
```

time: 3990 us -> 1420 us (0.36)
  waiting for transfers between devices: 2120 us -> 549 us
  matrix products: 978 us -> 282 us
  other arithmetic: 336 us -> 88.3 us
  Pallas kernels: 0 us -> 214 us
  blocking collectives: 213 us -> 38.2 us
  local copies, waits for them, and re-layouts: 266 us -> 158 us
  starting transfers between devices: 31.2 us -> 72.4 us
    all_gather x5, waiting for transfers between devices: 1290 us -> 19.4 us  [gather_fsdp(): return lax.all_gather(value, 'fsdp', axis=0, tiled=True)]
    dot_general x50 -> x14, matrix products: 978 us -> 282 us  [the longest x5 112 us: dot_last(): lax.dot_general(left_side, right_side, (((1,), (1,)), ((), ())), preferre...]
    reduce_scatter x5, waiting for transfers between devices: 623 us -> 0.03 us  [scatter_fsdp(): return lax.psum_scatter(value, 'fsdp', scatter_dimension=0, tiled=True)]
    ppermute x0 -> x43, waiting for transfers between devices: none -> 477 us  [the longest x13 275 us: seq_shift(): lax.ppermute(value, 'seq', [(i, (i + shift * CORES) % size) for i in rang...]
    pallas_call x0 -> x3, Pallas kernels: none -> 214 us  [the longest x1 108 us: attend_back(): pl.pallas_call(attend_back_kernel, grid_spec=pltpu.PrefetchScalarGridSpec...]
    convert_element_type x22 -> x10, other arithmetic: 201 us -> 34.1 us  [the longest x4 16.8 us: scatter_rows(): summed[shift].astype(BF16)]
    psum x1 -> x0, waiting for transfers between devices: 128 us -> none  [local(): lax.psum(attn_parts[0].astype(jnp.bfloat16), 'seq').astype(jnp.float32)]
    dynamic_update_slice x20 -> x34, local copies, waits for them, and re-layouts: 125 us -> 45.1 us  [gather_rows(): whole = lax.dynamic_update_slice_in_dim(whole, held, start, 0)]
  transfers between devices with their start and end apart: 17 -> 54, of which waited for: 12 -> 20; matrix products, arithmetic and copies ran while one was open for 37% -> 30% of each run, Pallas kernels for 0% -> 15%
where the time goes in v1:
time: 1420 us
  waiting for transfers between devices  549 us (39%)
  matrix products  282 us (20%)
  Pallas kernels  214 us (15%)
  local copies, waits for them, and re-layouts  158 us (11%)
  other arithmetic  88.3 us (6%)
  starting transfers between devices  72.4 us (5%)
  blocking collectives  38.2 us (3%)
  between operations  15.3 us (1%)
    ppermute x13, waiting for transfers between devices, seq_shift(): lax.ppermute(value, 'seq', [(i, (i + shift * CORES) % size) for i in rang...  275 us
    ppermute x4, waiting for transfers between devices, exchange_shards(): return lax.ppermute(value, ('seq', 'fsdp'), pairs)  190 us
    dot_general x5, matrix products, dot_last(): lax.dot_general(left_side, right_side, (((1,), (1,)), ((), ())), preferre...  112 us
    pallas_call x1, Pallas kernels, attend_back(): pl.pallas_call(attend_back_kernel, grid_spec=pltpu.PrefetchScalarGridSpec...  108 us
    dot_general x5, matrix products, dot_first(): lax.dot_general(left_side, right_side, (((0,), (0,)), ((), ())), preferre...  98 us
    pallas_call x1, Pallas kernels, attend(): pl.pallas_call(attend_kernel, grid_spec=pltpu.PrefetchScalarGridSpec(num_...  77.5 us
    dot_general x4, matrix products, dot(): return jnp.dot(left_side, right_side, preferred_element_type=F32)  71.7 us
    unnamed x12, waiting for transfers between devices  52.6 us
  transfers between devices with their start and end apart: 54, of which 20 were waited for; matrix products, arithmetic and copies ran while one was open for 30% of the time, Pallas kernels for 15%

profile of v1, /device:TPU:9, one launch (start us, length us, event | category | flops | bytes accessed | tf_op | source)
XLA Modules:
  0.0 1416.9 jit_solution(8602900035546155794)
XLA Ops:
  7.2 4.8 copy.57
  31.1 20.5 %collective-permute-done.3 = bf16[64,2048]{1,0:T(8,128)(2,1)S(1)} collective-permute-done((bf16[64,2048]{1,0:T(8,128)(2,1)S(1)}, bf16[64,2048]{1,0:T(8,128)(2,1)S(1)}, u32[]{:S(2)}, u32[]{:S(2)}) %collective-permute-start.3) | collective-permute-done | bytes 262176 | tf_op jit(solution)/shard_map/ppermute | solution.py:385
  53.5 8.2 collective-permute-start
  65.5 40.4 %collective-permute-done.1 = bf16[640,2048]{1,0:T(8,128)(2,1)} collective-permute-done((bf16[640,2048]{1,0:T(8,128)(2,1)}, bf16[640,2048]{1,0:T(8,128)(2,1)}, u32[]{:S(2)}, u32[]{:S(2)}) %collective-permute-start.1) | collective-permute-done | bytes 2621472 | tf_op jit(solution)/shard_map/ppermute | solution.py:331
  105.9 7.1 collective-permute-start.2
  113.1 30.6 %all_gather.18 = bf16[2048,4]{0,1:T(4,128)(2,1)S(1)} all-gather(bf16[256,4]{0,1:T(4,128)(2,1)S(1)} %pad_maximum_fusion.1), channel_id=1, replica_groups=mesh['seq'=4,'fsdp'=8] {'fsdp'}, dimensions={0}, use_global_device_ids=true | all-gather | bytes 18432 | tf_op jit(solution)/shard_map/all_gather | solution.py:403
  145.8 6.3 fusion.22
  162.8 6.6 fusion.5.x_ref
  169.4 28.5 %project_in_rope.1.q_ref.k_ref.v_ref = bf16[2560,1536]{1,0:T(8,128)(2,1)} custom-call(bf16[2560,2048]{1,0:T(8,128)(2,1)} %fusion.5.x_ref, bf16[2048,1536]{1,0:T(8,128)(2,1)} %all-gather.6.cloned.1.call-done.w_ref, f32[2560,128]{1,0:T(8,128)} %get-tuple-element.95.cos_ref, f32[2560,128]{1,0:T(8,128)} %get-tuple-element.94.sin_ref), custom_call_target="tpu_custom_call" | custom-call | flops 16106127360 | bytes 24641536 | tf_op jit(solution)/shard_map/project_in_rope/pallas_call | solution.py:95
  197.9 77.5 %attend.1 = (bf16[2560,512]{1,0:T(8,128)(2,1)}, bf16[8,2560,128]{2,1,0:T(8,128)(2,1)}) custom-call(s32[2]{0:T(128)} %copy-done.26, bf16[2560,1536]{1,0:T(8,128)(2,1)} %project_in_rope.1.q_ref.k_ref.v_ref, bf16[2560,1536]{1,0:T(8,128)(2,1)} %project_in_rope.1.q_ref.k_ref.v_ref, bf16[2560,1536]{1,0:T(8,128)(2,1)} %project_in_rope.1.q_ref.k_ref.v_ref), custom_call_target="tpu_custom_call" | custom-call | flops 26843545600 | bytes 23592960 | tf_op jit(solution)/shard_map/attend/pallas_call | solution.py:185
  275.4 7.8 convolution_convert_fusion.2
  285.9 4.1 collective-permute-start.5
  290.0 8.2 collective-permute-done.5
  302.7 56.5 %collective-permute-done.6 = bf16[640,2048]{1,0:T(8,128)(2,1)} collective-permute-done((bf16[640,2048]{1,0:T(8,128)(2,1)}, bf16[640,2048]{1,0:T(8,128)(2,1)}, u32[]{:S(2)}, u32[]{:S(2)}) %collective-permute-start.6) | collective-permute-done | bytes 2621472 | tf_op jit(solution)/shard_map/ppermute | solution.py:331
  359.2 6.4 fusion.30
  366.3 5.3 broadcast.214.clone.1
  371.6 3.3 constant_dynamic-update-slice_fusion.31
  380.2 122.6 %collective-permute-done.10 = bf16[176,2048]{1,0:T(8,128)(2,1)S(1)} collective-permute-done((bf16[176,2048]{1,0:T(8,128)(2,1)S(1)}, bf16[176,2048]{1,0:T(8,128)(2,1)S(1)}, u32[]{:S(2)}, u32[]{:S(2)}) %collective-permute-start.10) | collective-permute-done | bytes 720928 | tf_op jit(solution)/shard_map/ppermute | solution.py:385
  516.6 5.2 constant_dynamic-update-slice_fusion.30
  523.5 3.6 constant_dynamic-update-slice_fusion.28
  527.1 22.4 %fusion.33 = f32[2560,1408]{1,0:T(8,128)} fusion(bf16[2560,2048]{1,0:T(8,128)(2,1)} %constant_dynamic-update-slice_fusion.28, bf16[2048,1408]{1,0:T(8,128)(2,1)} %all-gather.10.cloned.1.call-done), kind=kOutput, calls=%fused_computation.167 | convolution fusion | flops 14763950080 | bytes 30670848 | tf_op jit(solution)/shard_map/dot_general | solution.py:37
  549.5 22.2 %fusion.34 = f32[2560,1408]{1,0:T(8,128)} fusion(bf16[2560,2048]{1,0:T(8,128)(2,1)} %constant_dynamic-update-slice_fusion.28, bf16[2048,1408]{1,0:T(8,128)(2,1)} %all-gather.12.cloned.1.call-done), kind=kOutput, calls=%fused_computation.168 | convolution fusion | flops 14763950080 | bytes 30670848 | tf_op jit(solution)/shard_map/dot_general | solution.py:37
  571.7 19.4 %all-gather.14.cloned.1.call-done = bf16[1408,2048]{1,0:T(8,128)(2,1)} async-done(((bf16[176,2048]{1,0:T(8,128)(2,1)}), bf16[1408,2048]{1,0:T(8,128)(2,1)}) %all-gather.14.cloned.1.call-update) | async-done | bytes 5767184 | tf_op jit(solution)/shard_map/all_gather | solution.py:403
  591.1 31.1 %multiply_convert_fusion = (bf16[2560,1408]{1,0:T(8,128)(2,1)}, bf16[2560,1408]{1,0:T(8,128)(2,1)}, bf16[2560,1408]{1,0:T(8,128)(2,1)}) fusion(f32[2560,1408]{1,0:T(8,128)} %fusion.33, f32[2560,1408]{1,0:T(8,128)} %fusion.34, bf16[2560,2048]{1,0:T(8,128)(2,1)} %copy-done.7, bf16[1408,2048]{1,0:T(8,128)(2,1)} %all-gather.14.cloned.1.call-done), kind=kOutput, calls=%fused_computation.9 | convolution fusion | flops 14818017280 | bytes 66715648 | tf_op jit(solution)/shard_map/dot_general | solution.py:25
  622.1 22.3 %convolution_convert_fusion.6 = bf16[2048,1408]{1,0:T(8,128)(2,1)} fusion(bf16[2560,2048]{1,0:T(8,128)(2,1)} %constant_dynamic-update-slice_fusion.28, bf16[2560,1408]{1,0:T(8,128)(2,1)} %get-tuple-element.66), kind=kOutput, calls=%fused_computation.23 | convolution fusion | flops 14766833664 | bytes 23461888 | tf_op jit(solution)/shard_map/dot_general | solution.py:31
  644.5 22.1 %convolution_convert_fusion.5 = bf16[2048,1408]{1,0:T(8,128)(2,1)} fusion(bf16[2560,2048]{1,0:T(8,128)(2,1)} %constant_dynamic-update-slice_fusion.28, bf16[2560,1408]{1,0:T(8,128)(2,1)} %get-tuple-element.65), kind=kOutput, calls=%fused_computation.22 | convolution fusion | flops 14766833664 | bytes 23461888 | tf_op jit(solution)/shard_map/dot_general | solution.py:31
  666.7 23.0 %fusion.35 = f32[2560,2048]{1,0:T(8,128)} fusion(bf16[2560,1408]{1,0:T(8,128)(2,1)} %get-tuple-element.66, bf16[2048,1408]{1,0:T(8,128)(2,1)} %all-gather.10.cloned.1.call-done), kind=kOutput, calls=%fused_computation.169 | convolution fusion | flops 14763950080 | bytes 33947648 | tf_op jit(solution)/shard_map/dot_general | solution.py:25
  689.8 24.3 %add_convert_fusion = bf16[2560,2048]{1,0:T(8,128)(2,1)} fusion(f32[2560,2048]{1,0:T(8,128)} %fusion.35, bf16[2560,1408]{1,0:T(8,128)(2,1)} %get-tuple-element.65, bf16[2048,1408]{1,0:T(8,128)(2,1)} %all-gather.12.cloned.1.call-done), kind=kOutput, calls=%fused_computation.8 | convolution fusion | flops 14774435840 | bytes 44433408 | tf_op jit(solution)/shard_map/dot_general | solution.py:25
  714.1 4.8 constant_dynamic-slice_fusion.14
  720.5 19.3 %convolution_convert_fusion.1 = bf16[2560,2048]{1,0:T(8,128)(2,1)S(1)} fusion(bf16[2560,1408]{1,0:T(8,128)(2,1)} %get-tuple-element.67, bf16[1408,2048]{1,0:T(8,128)(2,1)S(1)} %bitcast.132), kind=kOutput, calls=%fused_computation.15 | convolution fusion | flops 14769192960 | bytes 23461888 | tf_op jit(solution)/shard_map/dot_general | solution.py:37
  743.6 6.5 add_convert_fusion.2
  755.3 20.1 %convolution_convert_fusion.3 = bf16[1408,2048]{1,0:T(8,128)(2,1)} fusion(bf16[2560,1408]{1,0:T(8,128)(2,1)} %get-tuple-element.67, bf16[2560,2048]{1,0:T(8,128)(2,1)S(1)} %bitcast.113), kind=kOutput, calls=%fused_computation.20 | convolution fusion | flops 14766833664 | bytes 23461888 | tf_op jit(solution)/shard_map/dot_general | solution.py:31
  775.5 33.0 %collective-permute-done.19 = bf16[640,2048]{1,0:T(8,128)(2,1)} collective-permute-done((bf16[640,2048]{1,0:T(8,128)(2,1)S(1)}, bf16[640,2048]{1,0:T(8,128)(2,1)}, u32[]{:S(2)}, u32[]{:S(2)}) %collective-permute-start.19) | collective-permute-done | bytes 2621472 | tf_op jit(solution)/shard_map/ppermute | solution.py:331
  808.5 56.2 %collective-permute-done.13 = bf16[640,2048]{1,0:T(8,128)(2,1)} collective-permute-done((bf16[640,2048]{1,0:T(8,128)(2,1)}, bf16[640,2048]{1,0:T(8,128)(2,1)}, u32[]{:S(2)}, u32[]{:S(2)}) %collective-permute-start.13) | collective-permute-done | bytes 2621472 | tf_op jit(solution)/shard_map/ppermute | solution.py:331
  864.7 11.3 multiply_reduce_fusion
  876.0 5.4 broadcast.214
  881.4 6.5 constant_dynamic-update-slice_fusion.23
  890.1 55.6 %collective-permute-done.21 = bf16[640,2048]{1,0:T(8,128)(2,1)S(1)} collective-permute-done((bf16[640,2048]{1,0:T(8,128)(2,1)S(1)}, bf16[640,2048]{1,0:T(8,128)(2,1)S(1)}, u32[]{:S(2)}, u32[]{:S(2)}) %collective-permute-start.21) | collective-permute-done | bytes 2621472 | tf_op jit(solution)/shard_map/ppermute | solution.py:331
  953.6 11.1 convolution_convert_fusion.8
  964.8 11.2 convolution_convert_fusion.7.g_ref
  976.0 107.5 %attend_back.1 = bf16[2560,1536]{1,0:T(8,128)(2,1)} custom-call(s32[2]{0:T(128)} %copy-done.26, bf16[8,2560,128]{2,1,0:T(8,128)(2,1)} %get-tuple-element.14.qx_ref, bf16[2560,1536]{1,0:T(8,128)(2,1)} %project_in_rope.1.q_ref.k_ref.v_ref, bf16[2560,1536]{1,0:T(8,128)(2,1)} %project_in_rope.1.q_ref.k_ref.v_ref, ...), custom_call_target="tpu_custom_call" | custom-call | flops 67108864000 | bytes 31457280 | tf_op jit(solution)/shard_map/attend_back/pallas_call | solution.py:298
  1083.5 22.3 %convolution_convert_fusion.4 = bf16[2048,1536]{1,0:T(8,128)(2,1)} fusion(bf16[2560,2048]{1,0:T(8,128)(2,1)} %fusion.5.x_ref, bf16[2560,1536]{1,0:T(8,128)(2,1)} %attend_back.1), kind=kOutput, calls=%fused_computation.21 | convolution fusion | flops 16109273088 | bytes 24641536 | tf_op jit(solution)/shard_map/dot_general | solution.py:31
  1106.6 22.6 %convolution_convert_fusion = bf16[2560,2048]{1,0:T(8,128)(2,1)} fusion(bf16[2560,1536]{1,0:T(8,128)(2,1)} %attend_back.1, bf16[2048,1536]{1,0:T(8,128)(2,1)} %all-gather.6.cloned.1.call-done.w_ref), kind=kOutput, calls=%fused_computation.14 | convolution fusion | flops 16111370240 | bytes 24641536 | tf_op jit(solution)/shard_map/dot_general | solution.py:25
  1129.6 5.8 constant_dynamic-slice_fusion.12
  1142.8 11.9 collective-permute-done.34
  1158.4 16.4 %collective-permute-done.39 = bf16[176,2048]{1,0:T(8,128)(2,1)} collective-permute-done((bf16[176,2048]{1,0:T(8,128)(2,1)}, bf16[176,2048]{1,0:T(8,128)(2,1)}, u32[]{:S(2)}, u32[]{:S(2)}) %collective-permute-start.39) | collective-permute-done | bytes 720928 | tf_op jit(solution)/shard_map/ppermute | solution.py:385
  1176.9 6.4 collective-permute-done.37
  1184.6 14.7 %collective-permute-start.41 = (bf16[176,2048]{1,0:T(8,128)(2,1)}, bf16[176,2048]{1,0:T(8,128)(2,1)}, u32[]{:S(2)}, u32[]{:S(2)}) collective-permute-start(bf16[176,2048]{1,0:T(8,128)(2,1)} %collective-permute-done.39), channel_id=1, source_target_pairs={{0,16},{8,24},{16,0},{24,8},{1,17},{9,25},{17,1},{25,9},{2,18},{10... | collective-permute-start | bytes 2162696 | tf_op jit(solution)/shard_map/ppermute | solution.py:331
  1202.4 13.7 collective-permute-done.41
  1216.8 5.2 add_convert_fusion.1
  1229.7 6.5 copy.65
  1236.2 6.2 copy.68
  1242.4 6.2 copy.66
  1248.7 6.2 copy.69
  1256.1 30.0 %collective-permute-done.29 = bf16[64,2048]{1,0:T(8,128)(2,1)S(1)} collective-permute-done((bf16[64,2048]{1,0:T(8,128)(2,1)}, bf16[64,2048]{1,0:T(8,128)(2,1)S(1)}, u32[]{:S(2)}, u32[]{:S(2)}) %collective-permute-start.29) | collective-permute-done | bytes 262176 | tf_op jit(solution)/shard_map/ppermute | solution.py:385
  1286.1 3.2 collective-permute-start.31
  1290.5 3.3 convert_element_type.251
  1299.4 6.8 fusion.17
  1309.5 6.5 fusion.16
  1316.1 52.4 %reduce-scatter.19.cloned.1.call-done = f32[256,4]{1,0:T(8,128)} async-done(((f32[2048,4]{1,0:T(8,128)}), f32[256,4]{1,0:T(8,128)}) %reduce-scatter.19.cloned.1.call-update) | async-done | bytes 4112
  1369.5 7.6 psum.7
  1391.8 4.8 reshape.150
  1396.6 6.5 copy.64
  1403.1 6.7 copy.67
  (287 shorter events, 140.3 us)
Async XLA Ops:
  7.2 162.2 %all-gather.6.cloned.1.call-start = ((), (), s32[]{:S(2)}) async-start(), calls=%async_computation.6 | async-start | bytes 7077888 | tf_op jit(solution)/shard_map/all_gather | solution.py:403
  12.0 51.8 %copy-start.30 = (bf16[256]{0:T(256)(128)(2,1)S(1)}, bf16[256]{0:T(256)(128)(2,1)}, u32[]{:S(2)}) copy-start(bf16[256]{0:T(256)(128)(2,1)} %param.20) | copy-start | bytes 1540
  12.0 51.8 %copy-start.31 = (bf16[256]{0:T(256)(128)(2,1)S(1)}, bf16[256]{0:T(256)(128)(2,1)}, u32[]{:S(2)}) copy-start(bf16[256]{0:T(256)(128)(2,1)} %param.19) | copy-start | bytes 1540
  27.0 248.4 %all-gather.8.cloned.1.call-start = ((), (), s32[]{:S(2)}) async-start(), calls=%async_computation.7 | async-start | bytes 2359296 | tf_op jit(solution)/shard_map/all_gather | solution.py:403
  28.0 23.6 %collective-permute-start.3 = (bf16[64,2048]{1,0:T(8,128)(2,1)S(1)}, bf16[64,2048]{1,0:T(8,128)(2,1)S(1)}, u32[]{:S(2)}, u32[]{:S(2)}) collective-permute-start(bf16[64,2048]{1,0:T(8,128)(2,1)S(1)} %constant_dynamic-slice_fusion.22), channel_id=1, source_target_pairs={{0,0},{8,1},{16,2},{24,3},{1,4},{9,5},{17,6},{25,7},{2,8},{10,9},{... | collective-permute-start | bytes 786440 | tf_op jit(solution)/shard_map/ppermute | solution.py:385
  52.3 474.7 %all-gather.10.cloned.1.call-start = ((), (), s32[]{:S(2)}) async-start(), calls=%async_computation.8 | async-start | bytes 6488064 | tf_op jit(solution)/shard_map/all_gather | solution.py:403
  53.3 496.1 %all-gather.12.cloned.1.call-start = ((), (), s32[]{:S(2)}) async-start(), calls=%async_computation.9 | async-start | bytes 6488064 | tf_op jit(solution)/shard_map/all_gather | solution.py:403
  53.4 52.5 %collective-permute-start.1 = (bf16[640,2048]{1,0:T(8,128)(2,1)}, bf16[640,2048]{1,0:T(8,128)(2,1)}, u32[]{:S(2)}, u32[]{:S(2)}) collective-permute-start(bf16[640,2048]{1,0:T(8,128)(2,1)} %bitcast.104), channel_id=1, source_target_pairs={{0,16},{8,24},{16,0},{24,8},{1,17},{9,25},{17,1},{25,9},{2,18},{10... | collective-permute-start | bytes 7864328 | tf_op jit(solution)/shard_map/ppermute | solution.py:331
  53.5 98.6 %collective-permute-start = (bf16[640,2048]{1,0:T(8,128)(2,1)}, bf16[640,2048]{1,0:T(8,128)(2,1)}, u32[]{:S(2)}, u32[]{:S(2)}) collective-permute-start(bf16[640,2048]{1,0:T(8,128)(2,1)} %bitcast.105), channel_id=1, source_target_pairs={{0,8},{8,0},{16,24},{24,16},{1,9},{9,1},{17,25},{25,17},{2,10},{10... | collective-permute-start | bytes 7864328 | tf_op jit(solution)/shard_map/ppermute | solution.py:337
  63.7 527.3 %all-gather.14.cloned.1.call-start = ((), (), s32[]{:S(2)}) async-start(), calls=%async_computation.10 | async-start | bytes 6488064 | tf_op jit(solution)/shard_map/all_gather | solution.py:403
  64.7 80.3 %copy-start.26 = (s32[2]{0:T(128)}, s32[2]{0:T(128)S(1)}, u32[]{:S(2)}) copy-start(s32[2]{0:T(128)S(1)} %fusion.24.ends_ref) | copy-start | bytes 28
  105.9 50.4 %collective-permute-start.2 = (bf16[640,2048]{1,0:T(8,128)(2,1)}, bf16[640,2048]{1,0:T(8,128)(2,1)}, u32[]{:S(2)}, u32[]{:S(2)}) collective-permute-start(bf16[640,2048]{1,0:T(8,128)(2,1)} %collective-permute-done.1), channel_id=1, source_target_pairs={{0,8},{8,0},{16,24},{24,16},{1,9},{9,1},{17,25},{25,17},{2,10},{10... | collective-permute-start | bytes 7864328 | tf_op jit(solution)/shard_map/ppermute | solution.py:337
  143.7 227.9 %copy-start.15 = (f32[2048,1]{0,1:T(1,128)}, f32[2048,1]{0,1:T(1,128)S(1)}, u32[]{:S(2)}) copy-start(f32[2048,1]{0,1:T(1,128)S(1)} %get-tuple-element.90) | copy-start | bytes 24580
  285.9 12.4 collective-permute-start.5
  290.0 12.7 collective-permute-start.4
  300.8 58.4 %collective-permute-start.6 = (bf16[640,2048]{1,0:T(8,128)(2,1)}, bf16[640,2048]{1,0:T(8,128)(2,1)}, u32[]{:S(2)}, u32[]{:S(2)}) collective-permute-start(bf16[640,2048]{1,0:T(8,128)(2,1)} %add_convert_fusion.6), channel_id=1, source_target_pairs={{0,16},{8,24},{16,0},{24,8},{1,17},{9,25},{17,1},{25,9},{2,18},{10... | collective-permute-start | bytes 7864328 | tf_op jit(solution)/shard_map/ppermute | solution.py:331
  300.8 203.0 %collective-permute-start.15 = (bf16[640,2048]{1,0:T(8,128)(2,1)}, bf16[640,2048]{1,0:T(8,128)(2,1)}, u32[]{:S(2)}, u32[]{:S(2)}) collective-permute-start(bf16[640,2048]{1,0:T(8,128)(2,1)} %bitcast.22), channel_id=1, source_target_pairs={{0,16},{8,24},{16,0},{24,8},{1,17},{9,25},{17,1},{25,9},{2,18},{10... | collective-permute-start | bytes 7864328 | tf_op jit(solution)/shard_map/ppermute | solution.py:331
  302.7 62.9 %copy-start.19 = (f32[640]{0:T(1024)}, f32[640]{0:T(1024)S(1)}, u32[]{:S(2)}) copy-start(f32[640]{0:T(1024)S(1)} %broadcast_multiply_fusion.3) | copy-start | bytes 7684
  374.9 129.5 %collective-permute-start.8 = (bf16[640,2048]{1,0:T(8,128)(2,1)}, bf16[640,2048]{1,0:T(8,128)(2,1)S(1)}, u32[]{:S(2)}, u32[]{:S(2)}) collective-permute-start(bf16[640,2048]{1,0:T(8,128)(2,1)} %get-tuple-element.62), channel_id=1, source_target_pairs={{0,16},{8,24},{16,0},{24,8},{1,17},{9,25},{17,1},{25,9},{2,18},{10... | collective-permute-start | bytes 7864328 | tf_op jit(solution)/shard_map/ppermute | solution.py:331
  376.3 126.5 %collective-permute-start.10 = (bf16[176,2048]{1,0:T(8,128)(2,1)S(1)}, bf16[176,2048]{1,0:T(8,128)(2,1)S(1)}, u32[]{:S(2)}, u32[]{:S(2)}) collective-permute-start(bf16[176,2048]{1,0:T(8,128)(2,1)S(1)} %constant_dynamic-slice_fusion.17), channel_id=1, source_target_pairs={{0,0},{8,1},{16,2},{24,3},{1,4},{9,5},{17,6},{25,7},{2,8},{10,9},{... | collective-permute-start | bytes 2162696 | tf_op jit(solution)/shard_map/ppermute | solution.py:385
  378.3 129.6 %collective-permute-start.14 = (bf16[640,2048]{1,0:T(8,128)(2,1)}, bf16[640,2048]{1,0:T(8,128)(2,1)}, u32[]{:S(2)}, u32[]{:S(2)}) collective-permute-start(bf16[640,2048]{1,0:T(8,128)(2,1)} %bitcast.22), channel_id=1, source_target_pairs={{0,8},{8,0},{16,24},{24,16},{1,9},{9,1},{17,25},{25,17},{2,10},{10... | collective-permute-start | bytes 7864328 | tf_op jit(solution)/shard_map/ppermute | solution.py:337
  503.7 625.5 %reduce-scatter.13.cloned.1.call-start = ((), (), s32[]{:S(2)}) async-start(), calls=%async_computation.13 | async-start | bytes 6488064 | tf_op jit(solution)/shard_map/reduce_scatter | solution.py:407
  503.8 8.7 collective-permute-start.16
  503.9 12.7 collective-permute-start.7
  504.4 19.1 %collective-permute-start.9 = (bf16[640,2048]{1,0:T(8,128)(2,1)S(1)}, bf16[640,2048]{1,0:T(8,128)(2,1)}, u32[]{:S(2)}, u32[]{:S(2)}) collective-permute-start(bf16[640,2048]{1,0:T(8,128)(2,1)S(1)} %collective-permute-done.8), channel_id=1, source_target_pairs={{0,8},{8,0},{16,24},{24,16},{1,9},{9,1},{17,25},{25,17},{2,10},{10... | collective-permute-start | bytes 7864328 | tf_op jit(solution)/shard_map/ppermute | solution.py:337
  644.5 491.9 %reduce-scatter.15.cloned.1.call-start = ((), (), s32[]{:S(2)}) async-start(), calls=%async_computation.14 | async-start | bytes 6488064 | tf_op jit(solution)/shard_map/reduce_scatter | solution.py:407
  666.7 470.3 %reduce-scatter.17.cloned.1.call-start = ((), (), s32[]{:S(2)}) async-start(), calls=%async_computation.15 | async-start | bytes 6488064 | tf_op jit(solution)/shard_map/reduce_scatter | solution.py:407
  666.7 53.8 %slice-start.3 = ((s8[5767168]{0:T(1024)(128)(4,1)}), s8[4194304]{0:T(1024)(128)(4,1)S(1)}, s32[]{:S(2)}) async-start(s8[5767168]{0:T(1024)(128)(4,1)} %bitcast.131), calls=%async_computation.20 | async-start | bytes 8388608
  718.8 24.7 %collective-permute-start.18 = (bf16[640,2048]{1,0:T(8,128)(2,1)S(1)}, bf16[640,2048]{1,0:T(8,128)(2,1)S(1)}, u32[]{:S(2)}, u32[]{:S(2)}) collective-permute-start(bf16[640,2048]{1,0:T(8,128)(2,1)S(1)} %get-tuple-element.71), channel_id=1, source_target_pairs={{0,8},{8,0},{16,24},{24,16},{1,9},{9,1},{17,25},{25,17},{2,10},{10... | collective-permute-start | bytes 7864328 | tf_op jit(solution)/shard_map/ppermute | solution.py:337
  743.1 8.5 collective-permute-start.12
  743.1 32.4 %collective-permute-start.17 = (bf16[640,2048]{1,0:T(8,128)(2,1)}, bf16[640,2048]{1,0:T(8,128)(2,1)}, u32[]{:S(2)}, u32[]{:S(2)}) collective-permute-start(bf16[640,2048]{1,0:T(8,128)(2,1)} %get-tuple-element.70), channel_id=1, source_target_pairs={{0,8},{8,0},{16,24},{24,16},{1,9},{9,1},{17,25},{25,17},{2,10},{10... | collective-permute-start | bytes 7864328 | tf_op jit(solution)/shard_map/ppermute | solution.py:337
  743.6 31.9 %collective-permute-start.11 = (bf16[640,2048]{1,0:T(8,128)(2,1)}, bf16[640,2048]{1,0:T(8,128)(2,1)}, u32[]{:S(2)}, u32[]{:S(2)}) collective-permute-start(bf16[640,2048]{1,0:T(8,128)(2,1)} %get-tuple-element.72), channel_id=1, source_target_pairs={{0,8},{8,0},{16,24},{24,16},{1,9},{9,1},{17,25},{25,17},{2,10},{10... | collective-permute-start | bytes 7864328 | tf_op jit(solution)/shard_map/ppermute | solution.py:337
  750.1 58.5 %collective-permute-start.19 = (bf16[640,2048]{1,0:T(8,128)(2,1)S(1)}, bf16[640,2048]{1,0:T(8,128)(2,1)}, u32[]{:S(2)}, u32[]{:S(2)}) collective-permute-start(bf16[640,2048]{1,0:T(8,128)(2,1)S(1)} %add_convert_fusion.2), channel_id=1, source_target_pairs={{0,16},{8,24},{16,0},{24,8},{1,17},{9,25},{17,1},{25,9},{2,18},{10... | collective-permute-start | bytes 7864328 | tf_op jit(solution)/shard_map/ppermute | solution.py:331
  754.1 110.6 %collective-permute-start.13 = (bf16[640,2048]{1,0:T(8,128)(2,1)}, bf16[640,2048]{1,0:T(8,128)(2,1)}, u32[]{:S(2)}, u32[]{:S(2)}) collective-permute-start(bf16[640,2048]{1,0:T(8,128)(2,1)} %add_convert_fusion.4), channel_id=1, source_target_pairs={{0,16},{8,24},{16,0},{24,8},{1,17},{9,25},{17,1},{25,9},{2,18},{10... | collective-permute-start | bytes 7864328 | tf_op jit(solution)/shard_map/ppermute | solution.py:331
  775.4 89.3 %copy-start.16 = (f32[2048,1]{0,1:T(1,128)S(1)}, f32[2048,1]{0,1:T(1,128)}, u32[]{:S(2)}) copy-start(f32[2048,1]{0,1:T(1,128)} %copy-done.15) | copy-start | bytes 24580
  775.4 89.3 %copy-start.18 = (f32[640]{0:T(1024)S(1)}, f32[640]{0:T(1024)}, u32[]{:S(2)}) copy-start(f32[640]{0:T(1024)} %copy-done.17) | copy-start | bytes 7684
  775.4 89.3 %copy-start.22 = (f32[640]{0:T(1024)S(1)}, f32[640]{0:T(1024)}, u32[]{:S(2)}) copy-start(f32[640]{0:T(1024)} %copy-done.21) | copy-start | bytes 7684
  775.5 450.9 %reduce-scatter.11.cloned.1.call-start = ((), (), s32[]{:S(2)}) async-start(), calls=%async_computation.12 | async-start | bytes 2359296 | tf_op jit(solution)/shard_map/reduce_scatter | solution.py:407
  887.9 57.8 %collective-permute-start.21 = (bf16[640,2048]{1,0:T(8,128)(2,1)S(1)}, bf16[640,2048]{1,0:T(8,128)(2,1)S(1)}, u32[]{:S(2)}, u32[]{:S(2)}) collective-permute-start(bf16[640,2048]{1,0:T(8,128)(2,1)S(1)} %get-tuple-element.58), channel_id=1, source_target_pairs={{0,16},{8,24},{16,0},{24,8},{1,17},{9,25},{17,1},{25,9},{2,18},{10... | collective-permute-start | bytes 7864328 | tf_op jit(solution)/shard_map/ppermute | solution.py:331
  888.9 58.2 %collective-permute-start.20 = (bf16[640,2048]{1,0:T(8,128)(2,1)S(1)}, bf16[640,2048]{1,0:T(8,128)(2,1)S(1)}, u32[]{:S(2)}, u32[]{:S(2)}) collective-permute-start(bf16[640,2048]{1,0:T(8,128)(2,1)S(1)} %get-tuple-element.58), channel_id=1, source_target_pairs={{0,8},{8,0},{16,24},{24,16},{1,9},{9,1},{17,25},{25,17},{2,10},{10... | collective-permute-start | bytes 7864328 | tf_op jit(solution)/shard_map/ppermute | solution.py:337
  945.7 6.0 collective-permute-start.22
  964.7 342.9 %reduce-scatter.9.cloned.1.call-start = ((), (), s32[]{:S(2)}) async-start(), calls=%async_computation.11 | async-start | bytes 7077888 | tf_op jit(solution)/shard_map/reduce_scatter | solution.py:407
  1105.9 262.6 %reduce-scatter.19.cloned.1.call-start = ((), (), s32[]{:S(2)}) async-start(), calls=%async_computation.16 | async-start | bytes 1179648
  1129.2 12.0 collective-permute-start.33
  1135.4 81.4 %collective-permute-start.24 = (bf16[640,2048]{1,0:T(8,128)(2,1)}, bf16[640,2048]{1,0:T(8,128)(2,1)}, u32[]{:S(2)}, u32[]{:S(2)}) collective-permute-start(bf16[640,2048]{1,0:T(8,128)(2,1)} %get-tuple-element.69), channel_id=1, source_target_pairs={{0,8},{8,0},{16,24},{24,16},{1,9},{9,1},{17,25},{25,17},{2,10},{10... | collective-permute-start | bytes 7864328 | tf_op jit(solution)/shard_map/ppermute | solution.py:337
  1135.6 19.1 %collective-permute-start.34 = (bf16[256,1408]{1,0:T(8,128)(2,1)S(1)}, bf16[256,1408]{1,0:T(8,128)(2,1)}, u32[]{:S(2)}, u32[]{:S(2)}) collective-permute-start(bf16[256,1408]{1,0:T(8,128)(2,1)S(1)} %copy-done.11), channel_id=1, source_target_pairs={{0,16},{8,24},{16,0},{24,8},{1,17},{9,25},{17,1},{25,9},{2,18},{10... | collective-permute-start | bytes 2162696 | tf_op jit(solution)/shard_map/ppermute | solution.py:331
  1136.4 40.0 %collective-permute-start.36 = (bf16[256,1408]{1,0:T(8,128)(2,1)}, bf16[256,1408]{1,0:T(8,128)(2,1)}, u32[]{:S(2)}, u32[]{:S(2)}) collective-permute-start(bf16[256,1408]{1,0:T(8,128)(2,1)} %reduce-scatter.15.cloned.1.call-done), channel_id=1, source_target_pairs={{0,8},{8,0},{16,24},{24,16},{1,9},{9,1},{17,25},{25,17},{2,10},{10... | collective-permute-start | bytes 2162696 | tf_op jit(solution)/shard_map/ppermute | solution.py:337
  1137.0 37.8 %collective-permute-start.39 = (bf16[176,2048]{1,0:T(8,128)(2,1)}, bf16[176,2048]{1,0:T(8,128)(2,1)}, u32[]{:S(2)}, u32[]{:S(2)}) collective-permute-start(bf16[176,2048]{1,0:T(8,128)(2,1)} %reduce-scatter.17.cloned.1.call-done), channel_id=1, source_target_pairs={{0,0},{1,8},{2,16},{3,24},{4,1},{5,9},{6,17},{7,25},{8,2},{9,10},{... | collective-permute-start | bytes 2162696 | tf_op jit(solution)/shard_map/ppermute | solution.py:385
  1141.2 42.1 %collective-permute-start.37 = (bf16[256,1408]{1,0:T(8,128)(2,1)}, bf16[256,1408]{1,0:T(8,128)(2,1)S(1)}, u32[]{:S(2)}, u32[]{:S(2)}) collective-permute-start(bf16[256,1408]{1,0:T(8,128)(2,1)} %reduce-scatter.15.cloned.1.call-done), channel_id=1, source_target_pairs={{0,16},{8,24},{16,0},{24,8},{1,17},{9,25},{17,1},{25,9},{2,18},{10... | collective-permute-start | bytes 2162696 | tf_op jit(solution)/shard_map/ppermute | solution.py:331
  1154.6 144.7 %collective-permute-start.23 = (bf16[640,2048]{1,0:T(8,128)(2,1)}, bf16[640,2048]{1,0:T(8,128)(2,1)}, u32[]{:S(2)}, u32[]{:S(2)}) collective-permute-start(bf16[640,2048]{1,0:T(8,128)(2,1)} %get-tuple-element.68), channel_id=1, source_target_pairs={{0,8},{8,0},{16,24},{24,16},{1,9},{9,1},{17,25},{25,17},{2,10},{10... | collective-permute-start | bytes 7864328 | tf_op jit(solution)/shard_map/ppermute | solution.py:337
  1174.8 9.8 collective-permute-start.35
  1176.4 52.1 %collective-permute-start.40 = (bf16[176,2048]{1,0:T(8,128)(2,1)}, bf16[176,2048]{1,0:T(8,128)(2,1)}, u32[]{:S(2)}, u32[]{:S(2)}) collective-permute-start(bf16[176,2048]{1,0:T(8,128)(2,1)} %collective-permute-done.39), channel_id=1, source_target_pairs={{0,8},{8,0},{16,24},{24,16},{1,9},{9,1},{17,25},{25,17},{2,10},{10... | collective-permute-start | bytes 2162696 | tf_op jit(solution)/shard_map/ppermute | solution.py:337
  1183.3 40.2 %collective-permute-start.38 = (bf16[256,1408]{1,0:T(8,128)(2,1)S(1)}, bf16[256,1408]{1,0:T(8,128)(2,1)S(1)}, u32[]{:S(2)}, u32[]{:S(2)}) collective-permute-start(bf16[256,1408]{1,0:T(8,128)(2,1)S(1)} %collective-permute-done.37), channel_id=1, source_target_pairs={{0,8},{8,0},{16,24},{24,16},{1,9},{9,1},{17,25},{25,17},{2,10},{10... | collective-permute-start | bytes 2162696 | tf_op jit(solution)/shard_map/ppermute | solution.py:337
  1184.6 31.5 %collective-permute-start.41 = (bf16[176,2048]{1,0:T(8,128)(2,1)}, bf16[176,2048]{1,0:T(8,128)(2,1)}, u32[]{:S(2)}, u32[]{:S(2)}) collective-permute-start(bf16[176,2048]{1,0:T(8,128)(2,1)} %collective-permute-done.39), channel_id=1, source_target_pairs={{0,16},{8,24},{16,0},{24,8},{1,17},{9,25},{17,1},{25,9},{2,18},{10... | collective-permute-start | bytes 2162696 | tf_op jit(solution)/shard_map/ppermute | solution.py:331
  1216.1 73.2 %collective-permute-start.42 = (bf16[176,2048]{1,0:T(8,128)(2,1)}, bf16[176,2048]{1,0:T(8,128)(2,1)}, u32[]{:S(2)}, u32[]{:S(2)}) collective-permute-start(bf16[176,2048]{1,0:T(8,128)(2,1)} %collective-permute-done.41), channel_id=1, source_target_pairs={{0,8},{8,0},{16,24},{24,16},{1,9},{9,1},{17,25},{25,17},{2,10},{10... | collective-permute-start | bytes 2162696 | tf_op jit(solution)/shard_map/ppermute | solution.py:337
  1222.0 77.3 %collective-permute-start.25 = (bf16[640,2048]{1,0:T(8,128)(2,1)}, bf16[640,2048]{1,0:T(8,128)(2,1)}, u32[]{:S(2)}, u32[]{:S(2)}) collective-permute-start(bf16[640,2048]{1,0:T(8,128)(2,1)} %add_convert_fusion.1), channel_id=1, source_target_pairs={{0,16},{8,24},{16,0},{24,8},{1,17},{9,25},{17,1},{25,9},{2,18},{10... | collective-permute-start | bytes 7864328 | tf_op jit(solution)/shard_map/ppermute | solution.py:331
  1226.4 59.7 %collective-permute-start.29 = (bf16[64,2048]{1,0:T(8,128)(2,1)}, bf16[64,2048]{1,0:T(8,128)(2,1)S(1)}, u32[]{:S(2)}, u32[]{:S(2)}) collective-permute-start(bf16[64,2048]{1,0:T(8,128)(2,1)} %reduce-scatter.11.cloned.1.call-done), channel_id=1, source_target_pairs={{0,0},{1,8},{2,16},{3,24},{4,1},{5,9},{6,17},{7,25},{8,2},{9,10},{... | collective-permute-start | bytes 786440 | tf_op jit(solution)/shard_map/ppermute | solution.py:385
  1286.1 10.5 collective-permute-start.30
  1286.1 9.4 collective-permute-start.31
  1295.5 2.2 collective-permute-start.32
  1307.6 75.9 %collective-permute-start.26 = (bf16[256,1536]{1,0:T(8,128)(2,1)}, bf16[256,1536]{1,0:T(8,128)(2,1)}, u32[]{:S(2)}, u32[]{:S(2)}) collective-permute-start(bf16[256,1536]{1,0:T(8,128)(2,1)} %reduce-scatter.9.cloned.1.call-done), channel_id=1, source_target_pairs={{0,8},{8,0},{16,24},{24,16},{1,9},{9,1},{17,25},{25,17},{2,10},{10... | collective-permute-start | bytes 2359304 | tf_op jit(solution)/shard_map/ppermute | solution.py:337
  1308.1 69.0 %collective-permute-start.27 = (bf16[256,1536]{1,0:T(8,128)(2,1)}, bf16[256,1536]{1,0:T(8,128)(2,1)}, u32[]{:S(2)}, u32[]{:S(2)}) collective-permute-start(bf16[256,1536]{1,0:T(8,128)(2,1)} %reduce-scatter.9.cloned.1.call-done), channel_id=1, source_target_pairs={{0,16},{8,24},{16,0},{24,8},{1,17},{9,25},{17,1},{25,9},{2,18},{10... | collective-permute-start | bytes 2359304 | tf_op jit(solution)/shard_map/ppermute | solution.py:331
  1309.5 68.9 %copy-start.9 = (bf16[256,1536]{1,0:T(8,128)(2,1)S(1)}, bf16[256,1536]{1,0:T(8,128)(2,1)}, u32[]{:S(2)}) copy-start(bf16[256,1536]{1,0:T(8,128)(2,1)} %reduce-scatter.9.cloned.1.call-done) | copy-start | bytes 2359300
  1377.1 11.2 collective-permute-start.28
  (28 other events, 373.9 us)
Sparse Core Ops, SparseCore 0:
  27.1 109.2 all-gather.5
  139.1 49.0 all-gather.7
  191.0 89.6 all-gather.9
  283.3 90.8 all-gather.11
  503.9 87.1 all-gather.13
  644.6 110.2 reduce-scatter.12
  759.1 109.7 reduce-scatter.14
  873.2 109.7 reduce-scatter.16
  987.1 66.1 reduce-scatter.10
  1106.0 154.1 reduce-scatter.8
  1307.7 60.7 reduce-scatter.18

commit v2 on v1

v2 whole, which is shorter than its diff:
```python
import functools

import jax
import jax.numpy as jnp
from jax import lax
from jax.experimental import pallas as pl
from jax.experimental.pallas import tpu as pltpu
from jax.sharding import PartitionSpec as P

HEAD_DIM = 64
ROT = 16
PROMPT = 2048
LANES = 128

epsilon = 1e-05
rope_base = 10000.0

BF16 = jnp.bfloat16
F32 = jnp.float32
CORES = 2
VMEM_LIMIT = 56 * 1024 * 1024


def dot_last(left_side, right_side):
    return lax.dot_general(
        left_side, right_side, (((1,), (1,)), ((), ())), preferred_element_type=F32
    )


def dot_first(left_side, right_side):
    return lax.dot_general(
        left_side, right_side, (((0,), (0,)), ((), ())), preferred_element_type=F32
    )


def dot(left_side, right_side):
    return jnp.dot(left_side, right_side, preferred_element_type=F32)


def cont_ends(lengths):
    count = lengths.shape[0]
    before = jnp.arange(count)[None, :] <= jnp.arange(count)[:, None]
    return jnp.sum(jnp.where(before, lengths[None, :], 0), axis=1)


def rope_tables(lengths, total_rows):
    ends = cont_ends(lengths)
    starts = ends - lengths
    indices = jnp.arange(total_rows, dtype=jnp.int32)
    offset = indices - PROMPT
    inside = (offset[:, None] >= starts[None, :]) & (offset[:, None] < ends[None, :])
    seg_begin = jnp.sum(jnp.where(inside, starts[None, :], 0), axis=1)
    position = jnp.where(indices < PROMPT, indices, PROMPT + offset - seg_begin)
    half = ROT // 2
    within = jnp.arange(LANES, dtype=jnp.int32) % HEAD_DIM
    frequency = rope_base ** (-2.0 * (within % half).astype(F32) / ROT)
    angles = position.astype(F32)[:, None] * frequency[None, :]
    turning = (within < ROT)[None, :]
    sign = jnp.where(within < half, -1.0, 1.0)[None, :]
    cosine = jnp.where(turning, jnp.cos(angles), 1.0)
    sine = jnp.where(turning, sign * jnp.sin(angles), 0.0)
    return cosine, sine, ends


def turn(rows_in, cosine, sine):
    half = ROT // 2
    lane = lax.broadcasted_iota(jnp.int32, rows_in.shape, 1) % HEAD_DIM
    partner = jnp.where(
        lane < half,
        pltpu.roll(rows_in, LANES - half, 1),
        pltpu.roll(rows_in, half, 1),
    )
    return rows_in * cosine + partner * sine


def project_kernel(x_ref, w_ref, gain_ref, bias_ref, cos_ref, sin_ref, out_ref, normed_ref):
    cosine = cos_ref[...]
    sine = sin_ref[...]
    pairs = out_ref.shape[1] // (3 * LANES)
    x = x_ref[...].astype(F32)
    x = x - jnp.mean(x, axis=1, keepdims=True)
    x = x * lax.rsqrt(jnp.mean(x * x, axis=1, keepdims=True) + epsilon)
    x = (x * gain_ref[0:1, :] + bias_ref[0:1, :]).astype(BF16)
    normed_ref[...] = x
    for first in range(0, pairs, 2):
        begin = 3 * LANES * first
        mixed = dot(x, w_ref[:, begin : begin + 6 * LANES])
        for pair in range(2):
            base = 3 * LANES * pair
            query = turn(mixed[:, base : base + LANES], cosine, sine) * HEAD_DIM ** (-0.5)
            key = turn(mixed[:, base + LANES : base + 2 * LANES], cosine, sine)
            value = mixed[:, base + 2 * LANES : base + 3 * LANES]
            base = base + begin
            out_ref[:, base : base + LANES] = query.astype(BF16)
            out_ref[:, base + LANES : base + 2 * LANES] = key.astype(BF16)
            out_ref[:, base + 2 * LANES : base + 3 * LANES] = value.astype(BF16)


def project(x, weight, gain, bias, cosine, sine):
    rows, depth = x.shape
    columns = weight.shape[1]
    block = 512
    vector = pl.BlockSpec((8, depth), lambda i: (0, 0))
    return pl.pallas_call(
        project_kernel,
        grid=(rows // block,),
        in_specs=[
            pl.BlockSpec((block, depth), lambda i: (i, 0)),
            pl.BlockSpec((depth, columns), lambda i: (0, 0), pipeline_mode=pl.Buffered(1)),
            vector,
            vector,
            pl.BlockSpec((block, LANES), lambda i: (i, 0)),
            pl.BlockSpec((block, LANES), lambda i: (i, 0)),
        ],
        out_specs=[
            pl.BlockSpec((block, columns), lambda i: (i, 0)),
            pl.BlockSpec((block, depth), lambda i: (i, 0)),
        ],
        out_shape=[
            jax.ShapeDtypeStruct((rows, columns), BF16),
            jax.ShapeDtypeStruct((rows, depth), BF16),
        ],
        compiler_params=pltpu.CompilerParams(vmem_limit_bytes=VMEM_LIMIT),
        cost_estimate=pl.CostEstimate(
            flops=2 * rows * depth * columns,
            bytes_accessed=2 * (rows * depth + depth * columns + rows * columns),
            transcendentals=0,
        ),
        name="project_in_rope",
    )(
        x,
        weight,
        jnp.broadcast_to(gain[None], (8, depth)),
        jnp.broadcast_to(bias[None], (8, depth)),
        cosine,
        sine,
    )


BLOCK = 512
NEG = -1e30


def segment_of(index, ends_ref):
    count = jnp.zeros_like(index)
    for c in range(ends_ref.shape[0] - 1):
        count = count + (index >= PROMPT + ends_ref[c]).astype(jnp.int32)
    return count


def attend_kernel(ends_ref, *refs):
    held = len(refs) // 3
    q_refs, k_refs, v_refs = refs[:held], refs[held : 2 * held], refs[2 * held : 3 * held]
    o_ref, qx_ref = refs[3 * held :]
    rows = k_refs[0].shape[0]
    lane = lax.broadcasted_iota(jnp.int32, (BLOCK, LANES), 1)
    inside = [lane < HEAD_DIM, lane >= HEAD_DIM]

    def one_block(number):
        start = number * BLOCK
        end = start + BLOCK
        full = min(start, PROMPT)
        row = lax.broadcasted_iota(jnp.int32, (BLOCK, 1), 0) + start
        col = lax.broadcasted_iota(jnp.int32, (1, end - full), 1) + full
        visible = col <= row
        if end > PROMPT:
            visible = visible & (segment_of(row, ends_ref) == segment_of(col, ends_ref))
        for pair in range(held):
            q = q_refs[pair][...]
            outs = []
            for h in range(2):
                q_head = jnp.where(inside[h], q, jnp.zeros_like(q))
                v = v_refs[pair][:end, :]
                lane_v = lax.broadcasted_iota(jnp.int32, v.shape, 1)
                own_v = (lane_v < HEAD_DIM) if h == 0 else (lane_v >= HEAD_DIM)
                v_one = jnp.where(own_v, v, jnp.ones_like(v))
                near = dot_last(q_head, k_refs[pair][full:end, :])
                near = jnp.where(visible, near, NEG)
                peak = jnp.max(near, axis=1, keepdims=True)
                if full:
                    early = dot_last(q_head, k_refs[pair][:full, :])
                    peak = jnp.maximum(peak, jnp.max(early, axis=1, keepdims=True))
                acc = dot(jnp.exp(near - peak).astype(BF16), v_one[full:])
                if full:
                    acc = acc + dot(jnp.exp(early - peak).astype(BF16), v_one[:full])
                outs.append(acc / pltpu.roll(acc, HEAD_DIM, 1))
                minus = -(peak + jnp.log(jnp.where(inside[h], 1.0, acc)))
                high = minus.astype(BF16)
                rest = minus - high.astype(F32)
                mid = rest.astype(BF16)
                low = (rest - mid.astype(F32)).astype(BF16)
                base = HEAD_DIM * (1 - h)
                spare = jnp.where(
                    lane == base, high, jnp.where(lane == base + 1, mid, jnp.zeros_like(high))
                )
                spare = jnp.where(lane == base + 2, low, spare)
                qx_ref[2 * pair + h] = jnp.where(inside[h], q, spare)
            o_ref[:, pair * LANES : (pair + 1) * LANES] = jnp.where(
                inside[0], outs[0], outs[1]
            ).astype(BF16)

    for number in range(rows // BLOCK):
        pl.when(pl.program_id(1) == number)(functools.partial(one_block, number))


def attend(ends, qkv):
    rows, columns = qkv.shape
    pairs = columns // (3 * LANES)
    held = 2
    work = rows * rows // 2 * pairs * 2

    def part(which, height, pair):
        return pl.BlockSpec(
            (height, LANES),
            lambda p, i, e: (i if height == BLOCK else 0, 3 * (p * held + pair) + which),
        )

    return pl.pallas_call(
        attend_kernel,
        grid_spec=pltpu.PrefetchScalarGridSpec(
            num_scalar_prefetch=1,
            grid=(pairs // held, rows // BLOCK),
            in_specs=[
                part(which, BLOCK if which == 0 else rows, pair)
                for which in range(3)
                for pair in range(held)
            ],
            out_specs=[
                pl.BlockSpec((BLOCK, held * LANES), lambda p, i, e: (i, p)),
                pl.BlockSpec((2 * held, BLOCK, LANES), lambda p, i, e: (p, i, 0)),
            ],
        ),
        out_shape=[
            jax.ShapeDtypeStruct((rows, pairs * LANES), BF16),
            jax.ShapeDtypeStruct((2 * pairs, rows, LANES), BF16),
        ],
        compiler_params=pltpu.CompilerParams(vmem_limit_bytes=VMEM_LIMIT),
        cost_estimate=pl.CostEstimate(
            flops=work * 1024, bytes_accessed=2 * rows * columns, transcendentals=0
        ),
        name="attend",
    )(ends, *([qkv] * (3 * held)))


def attend_back_kernel(
    ends_ref, qx_ref, k_ref, v_ref, g_ref, o_ref, cos_ref, sin_ref, out_ref,
    gx_ref, dq_ref, dk_ref, dv_ref,
):
    number = pl.program_id(1)
    blocks = pl.num_programs(1)
    rows = qx_ref.shape[1]
    lane = lax.broadcasted_iota(jnp.int32, (BLOCK, LANES), 1)
    inside = [lane < HEAD_DIM, lane >= HEAD_DIM]

    @pl.when(number == 0)
    def _():
        dq_ref[...] = jnp.zeros_like(dq_ref)

        @pl.loop(0, rows // BLOCK)
        def _(j):
            here = pl.ds(pl.multiple_of(j * BLOCK, BLOCK), BLOCK)
            g = g_ref[here, :]
            both = g.astype(F32) * o_ref[here, :].astype(F32)
            for h in range(2):
                minus = -jnp.sum(jnp.where(inside[h], both, 0.0), axis=1, keepdims=True)
                high = minus.astype(BF16)
                rest = minus - high.astype(F32)
                mid = rest.astype(BF16)
                low = (rest - mid.astype(F32)).astype(BF16)
                base = HEAD_DIM * (1 - h)
                spare = jnp.where(
                    lane == base, high, jnp.where(lane == base + 1, mid, jnp.zeros_like(g))
                )
                spare = jnp.where(lane == base + 2, low, spare)
                gx_ref[h, here, :] = jnp.where(inside[h], g, spare)

    k = k_ref[...]
    v = v_ref[...]
    k_one = [jnp.where(inside[h], k, jnp.ones_like(k)) for h in range(2)]
    v_one = [jnp.where(inside[h], v, jnp.ones_like(v)) for h in range(2)]
    k_turned = [jnp.where(inside[h], k, jnp.zeros_like(k)).T for h in range(2)]
    dk_ref[...] = jnp.zeros_like(dk_ref)
    dv_ref[...] = jnp.zeros_like(dv_ref)

    def step(start, masked):
        here = pl.ds(start, BLOCK)
        if masked:
            row = lax.broadcasted_iota(jnp.int32, (1, BLOCK), 1) + start
            col = lax.broadcasted_iota(jnp.int32, (BLOCK, 1), 0) + start
            visible = (col <= row) & (segment_of(row, ends_ref) == segment_of(col, ends_ref))
        total = None
        for h in range(2):
            qx = qx_ref[h, here, :]
            gx = gx_ref[h, here, :]
            chances = jnp.exp(dot_last(k_one[h], qx))
            if masked:
                chances = jnp.where(visible, chances, 0.0)
            dv_ref[h] += dot(chances.astype(BF16), gx)
            grad_scores = (chances * dot_last(v_one[h], gx)).astype(BF16)
            dk_ref[h] += dot(grad_scores, qx)
            part = dot(k_turned[h], grad_scores)
            total = part if total is None else total + part
        dq_ref[:, here] += total

    step(pl.multiple_of(number * BLOCK, BLOCK), True)

    @pl.loop(number + 1, blocks)
    def _(j):
        step(pl.multiple_of(j * BLOCK, BLOCK), False)

    here = pl.ds(pl.multiple_of(number * BLOCK, BLOCK), BLOCK)
    dk = jnp.where(inside[0], dk_ref[0], dk_ref[1])
    dk = turn(dk, cos_ref[here, :], -sin_ref[here, :])
    out_ref[here, LANES : 2 * LANES] = dk.astype(BF16)
    out_ref[here, 2 * LANES :] = jnp.where(inside[0], dv_ref[0], dv_ref[1]).astype(BF16)

    @pl.when(number == blocks - 1)
    def _():
        for j in range(rows // BLOCK):
            here = slice(j * BLOCK, (j + 1) * BLOCK)
            dq = dq_ref[:, here].T * HEAD_DIM ** (-0.5)
            dq = turn(dq, cos_ref[here, :], -sin_ref[here, :])
            out_ref[here, :LANES] = dq.astype(BF16)


def attend_back(ends, qkv, qx, grad, attended, cosine, sine):
    rows, columns = qkv.shape
    pairs = columns // (3 * LANES)
    blocks = rows // BLOCK
    work = rows * rows // 2 * pairs * 2
    return pl.pallas_call(
        attend_back_kernel,
        grid_spec=pltpu.PrefetchScalarGridSpec(
            num_scalar_prefetch=1,
            grid=(pairs, blocks),
            in_specs=[
                pl.BlockSpec((2, rows, LANES), lambda p, i, e: (p, 0, 0)),
                pl.BlockSpec((BLOCK, LANES), lambda p, i, e: (i, 3 * p + 1)),
                pl.BlockSpec((BLOCK, LANES), lambda p, i, e: (i, 3 * p + 2)),
                pl.BlockSpec((rows, LANES), lambda p, i, e: (0, p)),
                pl.BlockSpec((rows, LANES), lambda p, i, e: (0, p)),
                pl.BlockSpec((rows, LANES), lambda p, i, e: (0, 0)),
                pl.BlockSpec((rows, LANES), lambda p, i, e: (0, 0)),
            ],
            out_specs=pl.BlockSpec((rows, 3 * LANES), lambda p, i, e: (0, p)),
            scratch_shapes=[
                pltpu.VMEM((2, rows, LANES), BF16),
                pltpu.VMEM((LANES, rows), F32),
                pltpu.VMEM((2, BLOCK, LANES), F32),
                pltpu.VMEM((2, BLOCK, LANES), F32),
            ],
        ),
        out_shape=jax.ShapeDtypeStruct((rows, columns), BF16),
        compiler_params=pltpu.CompilerParams(vmem_limit_bytes=VMEM_LIMIT),
        cost_estimate=pl.CostEstimate(
            flops=work * 2560, bytes_accessed=2 * rows * columns, transcendentals=0
        ),
        name="attend_back",
    )(ends, qx, qkv, qkv, grad, attended, cosine, sine)


def params():
    return pltpu.CompilerParams(vmem_limit_bytes=VMEM_LIMIT)


def cost(rows, depth, columns):
    return pl.CostEstimate(
        flops=2 * rows * depth * columns,
        bytes_accessed=2 * (rows * depth + depth * columns + rows * columns),
        transcendentals=0,
    )


def chip_matmul(x, weight, order, rows, turned, name):
    depth = x.shape[1]
    columns = weight.shape[0] if turned else weight.shape[1]
    half = rows // 2
    count = order.shape[0]

    def kernel(order_ref, x_ref, w_ref, *outs):
        multiply = dot_last if turned else dot
        made = multiply(x_ref[...], w_ref[...]).astype(BF16)
        for b in range(count):

            @pl.when(pl.program_id(0) // 2 == b)
            def _(b=b):
                outs[b][...] = made

    made = pl.pallas_call(
        kernel,
        grid_spec=pltpu.PrefetchScalarGridSpec(
            num_scalar_prefetch=1,
            grid=(2 * count,),
            in_specs=[
                pl.BlockSpec((half, depth), lambda i, o: (o[i // 2] * 2 + i % 2, 0)),
                pl.BlockSpec(weight.shape, lambda i, o: (0, 0), pipeline_mode=pl.Buffered(1)),
            ],
            out_specs=[
                pl.BlockSpec((half, columns), lambda i, o, b=b: (jnp.clip(i - 2 * b, 0, 1), 0))
                for b in range(count)
            ],
        ),
        out_shape=[jax.ShapeDtypeStruct((rows, columns), BF16)] * count,
        compiler_params=params(),
        cost_estimate=cost(count * rows, depth, columns),
        name=name,
    )(order, x, weight)
    return [(made[2 * i], made[2 * i + 1]) for i in range(count // 2)]


def buffers(steps):
    return pl.Buffered(1 if steps == 1 else 2)


def weight_grad(x, g, name):
    rows, columns = g.shape
    height = x.shape[1]
    tile = 256 if height % 256 == 0 else height
    part = columns if height % 256 == 0 else 512

    def kernel(x_ref, g_ref, out_ref):
        out_ref[...] = dot_first(x_ref[...], g_ref[...]).astype(BF16)

    return pl.pallas_call(
        kernel,
        grid=(height // tile, columns // part),
        in_specs=[
            pl.BlockSpec((rows, tile), lambda i, j: (0, i), pipeline_mode=buffers(height // tile)),
            pl.BlockSpec((rows, part), lambda i, j: (0, j), pipeline_mode=buffers(columns // part)),
        ],
        out_specs=pl.BlockSpec((tile, part), lambda i, j: (i, j)),
        out_shape=jax.ShapeDtypeStruct((height, columns), BF16),
        compiler_params=params(),
        cost_estimate=cost(height, rows, columns),
        name=name,
    )(x, g)


def own_heads(project_in, me, pairs):
    rows, columns = project_in.shape
    every = columns // 3 // LANES

    def kernel(first_ref, in_ref, out_ref):
        out_ref[...] = in_ref[...]

    return pl.pallas_call(
        kernel,
        grid_spec=pltpu.PrefetchScalarGridSpec(
            num_scalar_prefetch=1,
            grid=(3, pairs),
            in_specs=[
                pl.BlockSpec((rows, LANES), lambda part, p, f: (0, part * every + f[0] + p))
            ],
            out_specs=pl.BlockSpec((rows, LANES), lambda part, p, f: (0, 3 * p + part)),
        ),
        out_shape=jax.ShapeDtypeStruct((rows, 3 * pairs * LANES), BF16),
        compiler_params=params(),
        name="own_heads",
    )(jnp.full((1,), me * pairs, jnp.int32), project_in)


def feed(normed, upstream, w_gate_up, w_down):
    count, rows, width = normed.shape
    units = w_down.shape[0]
    half = rows // 2
    total = rows * count

    def kernel(x_ref, *refs):
        ups, refs = refs[:count], refs[count:]
        wgu_ref, wd_ref, product_ref, grads_ref, normed_ref, upstream_ref = refs
        for b in range(count):

            @pl.when(pl.program_id(0) // 2 == b)
            def _(b=b):
                upstream_ref[...] = ups[b][...]

        x = x_ref[0]
        normed_ref[...] = x
        both = dot(x, wgu_ref[...])
        mid = dot_last(upstream_ref[...], wd_ref[...])
        gate = both[:, :units]
        up = both[:, units:]
        sigmoid = 1.0 / (1.0 + jnp.exp(-gate))
        silu = gate * sigmoid
        product_ref[...] = (silu * up).astype(BF16)
        slope = sigmoid * (1.0 + gate * (1.0 - sigmoid))
        grads_ref[:, :units] = (mid * up * slope).astype(BF16)
        grads_ref[:, units:] = (mid * silu).astype(BF16)

    def here(i):
        return (i, 0)

    def block_spec(b):
        return pl.BlockSpec((half, width), lambda i: (jnp.clip(i - 2 * b, 0, 1), 0))

    return pl.pallas_call(
        kernel,
        grid=(2 * count,),
        in_specs=[pl.BlockSpec((1, half, width), lambda i: (i // 2, i % 2, 0))]
        + [block_spec(b) for b in range(count)]
        + [
            pl.BlockSpec(w_gate_up.shape, lambda i: (0, 0), pipeline_mode=pl.Buffered(1)),
            pl.BlockSpec(w_down.shape, lambda i: (0, 0), pipeline_mode=pl.Buffered(1)),
        ],
        out_specs=[
            pl.BlockSpec((half, units), here),
            pl.BlockSpec((half, 2 * units), here),
            pl.BlockSpec((half, width), here),
            pl.BlockSpec((half, width), here),
        ],
        out_shape=[
            jax.ShapeDtypeStruct((total, units), BF16),
            jax.ShapeDtypeStruct((total, 2 * units), BF16),
            jax.ShapeDtypeStruct((total, width), BF16),
            jax.ShapeDtypeStruct((total, width), BF16),
        ],
        compiler_params=params(),
        cost_estimate=cost(total, 3 * width, units),
        name="feed",
    )(normed, *upstream, w_gate_up, w_down)


def near_and_down(grads, w_gate_up, product, upstream, rows):
    columns = grads.shape[1]
    total, units = product.shape
    width = upstream.shape[1]
    half = rows // 2
    tile = 512

    def kernel(g_ref, w_ref, p_ref, up_ref, own_ref, other_ref, out_ref):
        step = pl.program_id(0)

        @pl.when(step < 4)
        def _():
            made = dot_last(g_ref[...], w_ref[...]).astype(BF16)

            @pl.when(step < 2)
            def _():
                own_ref[...] = made

            @pl.when(step >= 2)
            def _():
                other_ref[...] = made

        @pl.when(step >= 4)
        def _():
            out_ref[...] = dot_first(p_ref[...], up_ref[...]).astype(BF16)

    def late(i):
        return jnp.maximum(i - 4, 0)

    return pl.pallas_call(
        kernel,
        grid=(4 + width // tile,),
        in_specs=[
            pl.BlockSpec((half, columns), lambda i: (jnp.minimum(i, 3), 0)),
            pl.BlockSpec(w_gate_up.shape, lambda i: (0, 0), pipeline_mode=pl.Buffered(1)),
            pl.BlockSpec(product.shape, lambda i: (0, 0), pipeline_mode=pl.Buffered(1)),
            pl.BlockSpec((total, tile), lambda i: (0, late(i))),
        ],
        out_specs=[
            pl.BlockSpec((half, width), lambda i: (jnp.minimum(i, 1), 0)),
            pl.BlockSpec((half, width), lambda i: (jnp.clip(i - 2, 0, 1), 0)),
            pl.BlockSpec((units, tile), lambda i: (0, late(i))),
        ],
        out_shape=[
            jax.ShapeDtypeStruct((rows, width), BF16),
            jax.ShapeDtypeStruct((rows, width), BF16),
            jax.ShapeDtypeStruct((units, width), BF16),
        ],
        compiler_params=params(),
        cost_estimate=cost(total + rows, width, columns),
        name="near_and_down",
    )(grads, w_gate_up, product, upstream)


def blocks_matmul(blocks, weight, order):
    rows, depth = blocks[0].shape
    columns = weight.shape[0]
    half = rows // 2
    count = len(blocks)

    def kernel(order_ref, *refs):
        ins, (w_ref, out_ref, copy_ref) = refs[:count], refs[count:]
        for b in range(count):

            @pl.when(pl.program_id(0) // 2 == b)
            def _(b=b):
                copy_ref[...] = ins[b][...]

        out_ref[...] = dot_last(copy_ref[...], w_ref[...]).astype(BF16)

    def block_spec(b):
        return pl.BlockSpec((half, depth), lambda i, o: (jnp.clip(i - 2 * b, 0, 1), 0))

    return pl.pallas_call(
        kernel,
        grid_spec=pltpu.PrefetchScalarGridSpec(
            num_scalar_prefetch=1,
            grid=(2 * count,),
            in_specs=[block_spec(b) for b in range(count)]
            + [pl.BlockSpec(weight.shape, lambda i, o: (0, 0), pipeline_mode=pl.Buffered(1))],
            out_specs=[
                pl.BlockSpec((half, columns), lambda i, o: (o[i // 2] * 2 + i % 2, 0)),
                pl.BlockSpec((half, depth), lambda i, o: (o[i // 2] * 2 + i % 2, 0)),
            ],
        ),
        out_shape=[
            jax.ShapeDtypeStruct((rows * count, columns), BF16),
            jax.ShapeDtypeStruct((rows * count, depth), BF16),
        ],
        compiler_params=params(),
        cost_estimate=cost(rows * count, depth, columns),
        name="grad_attended",
    )(order, *blocks, weight)


def tie(value, *others):
    return lax.optimization_barrier((value, others))[0]


def from_chip(value, chips, ahead):
    size = chips * CORES
    return lax.ppermute(value, "seq", [(i, (i - ahead * CORES) % size) for i in range(size)])


def to_chip(value, chips, ahead):
    return from_chip(value, chips, chips - ahead)


def core_swap(value, chips):
    return lax.ppermute(value, "seq", [(i, i ^ 1) for i in range(chips * CORES)])


def seq_order(chips):
    me = lax.axis_index("seq")
    core, chip = me % CORES, me // CORES
    found = []
    for ahead in range(chips):
        base = (chip + ahead) % chips * CORES
        found += [base + core, base + 1 - core]
    return jnp.stack(found).astype(jnp.int32)


def planes(size):
    return 4 if size % 4 == 0 else 1


def remote(src, dst, send, recv, **where):
    return pltpu.make_async_remote_copy(
        src_ref=src, dst_ref=dst, send_sem=send, recv_sem=recv, device_id=where,
        device_id_type=pl.DeviceIdType.MESH,
    )


def rows_at(ref, index, rows):
    return ref.at[pl.ds(pl.multiple_of(index * rows, rows), rows)]


class Place:
    def __init__(self, seq_size, fsdp_size):
        self.chips = seq_size // CORES
        self.seq_size, self.fsdp_size = seq_size, fsdp_size
        self.deep = planes(fsdp_size)
        self.across = fsdp_size // self.deep
        self.seq = lax.axis_index("seq")
        self.fsdp = lax.axis_index("fsdp")
        self.core, self.chip = self.seq % CORES, self.seq // CORES
        self.z, self.y = self.fsdp // self.across, self.fsdp % self.across

    def along_x(self, k):
        return (self.chip + k) % self.chips * CORES + self.core

    def other(self):
        return self.chip * CORES + 1 - self.core

    def along_z(self, k):
        return (self.z + k) % self.deep * self.across + self.y

    def along_y(self, k):
        return self.z * self.across + (self.y + k) % self.across

    def shard(self, kz, ky):
        return (self.z + kz) % self.deep * self.across + (self.y + ky) % self.across


def greet_device(**where):
    pl.semaphore_signal(
        pltpu.get_barrier_semaphore(),
        inc=1,
        device_id=where,
        device_id_type=pl.DeviceIdType.MESH,
    )


def greet(place, over_fsdp):
    count = place.chips
    for k in range(1, place.chips):
        greet_device(seq=place.along_x(k))
    greet_device(seq=place.other())
    if over_fsdp:
        count += place.fsdp_size - 1
        for k in range(1, place.fsdp_size):
            greet_device(fsdp=(place.fsdp + k) % place.fsdp_size)
    pl.semaphore_wait(pltpu.get_barrier_semaphore(), count)


def greet_all(place):
    for k in range(1, place.seq_size):
        greet_device(seq=(place.seq + k) % place.seq_size)
    for k in range(1, place.fsdp_size):
        greet_device(fsdp=(place.fsdp + k) % place.fsdp_size)
    count = place.seq_size + place.fsdp_size - 2
    pl.semaphore_wait(pltpu.get_barrier_semaphore(), count)


class FsdpGather:
    def __init__(self, place, own, whole, sems):
        self.place, self.own, self.whole = place, own, whole
        self.rows = own.shape[0]
        self.send_z, self.recv_z, self.send_y, self.recv_y = sems

    def slot(self, index):
        return rows_at(self.whole, index, self.rows)

    def z(self, up, d):
        p = self.place
        sign = 1 if up else -1
        slot = self.slot(p.shard(sign * (1 - d), 0))
        index = (0 if up else p.deep) + d
        return remote(
            self.own if d == 1 else slot, slot,
            self.send_z.at[index], self.recv_z.at[index], fsdp=p.along_z(sign),
        )

    def sends(self, up, d):
        z, deep = self.place.z, self.place.deep
        return (z >= d - 1) & (z + 1 < deep) if up else (z + d - 1 < deep) & (z >= 1)

    def gets(self, up, d):
        z, deep = self.place.z, self.place.deep
        return z >= d if up else z + d < deep

    def y(self, kz, ky):
        p = self.place
        slot = self.slot(p.shard(-kz, 0))
        return remote(
            self.own if kz == 0 else slot, slot,
            self.send_y.at[kz, ky], self.recv_y.at[kz, ky], fsdp=p.along_y(ky),
        )

    def start(self):
        for up in (True, False):
            pl.when(self.sends(up, 1))(lambda up=up: self.z(up, 1).start())
        for ky in range(1, self.place.across):
            self.y(0, ky).start()

    def pass_on(self, d):
        deep = self.place.deep
        for up in (True, False):

            @pl.when(self.gets(up, d))
            def _(up=up):
                self.z(up, d).wait_recv()
                for ky in range(1, self.place.across):
                    self.y(d if up else deep - d, ky).start()

            if d + 1 < deep:
                pl.when(self.sends(up, d + 1))(lambda up=up: self.z(up, d + 1).start())

    def finish(self):
        deep, across = self.place.deep, self.place.across
        for kz in range(deep):
            for ky in range(1, across):
                self.y(kz, ky).wait()
        for d in range(1, deep):
            for up in (True, False):
                pl.when(self.sends(up, d))(lambda up=up, d=d: self.z(up, d).wait_send())


def fsdp_sems(place_deep, place_across):
    return [pltpu.SemaphoreType.DMA((2 * place_deep,))] * 2 + [
        pltpu.SemaphoreType.DMA((place_deep, place_across))
    ] * 2


def opening(tokens, in_part, out_slice, vectors, seq_size, fsdp_size):
    rows, width = tokens.shape
    chips = seq_size // CORES
    deep = planes(fsdp_size)
    across = fsdp_size // deep
    dma = pltpu.SemaphoreType.DMA

    def kernel(
        tok_ref, in_ref, out_ref, vec_ref, tok_all, w_in, w_out, vec_all,
        here, x_send, x_recv, c_send, c_recv, v_send, v_recv, *sems,
    ):
        p = Place(seq_size, fsdp_size)
        greet(p, True)

        def tok_slot(index):
            return rows_at(tok_all, index, rows)

        def tok_x(k):
            return remote(
                tok_ref, tok_slot(p.seq), x_send.at[k], x_recv.at[k], seq=p.along_x(k)
            )

        def tok_core(k):
            slot = tok_slot(p.along_x(-k))
            return remote(
                tok_ref if k == 0 else slot, slot, c_send.at[k], c_recv.at[k], seq=p.other()
            )

        def vec(k):
            return remote(
                vec_ref, vec_all.at[p.fsdp], v_send.at[k], v_recv.at[k],
                fsdp=(p.fsdp + k) % fsdp_size,
            )

        into = FsdpGather(p, in_ref, w_in, sems[:4])
        outof = FsdpGather(p, out_ref, w_out, sems[4:])
        own = [
            pltpu.make_async_copy(tok_ref, tok_slot(p.seq), here.at[0]),
            pltpu.make_async_copy(in_ref, into.slot(p.fsdp), here.at[1]),
            pltpu.make_async_copy(vec_ref, vec_all.at[p.fsdp], here.at[2]),
            pltpu.make_async_copy(out_ref, outof.slot(p.fsdp), here.at[3]),
        ]
        for k in range(1, fsdp_size):
            vec(k).start()
        for k in range(1, chips):
            tok_x(k).start()
        into.start()
        tok_core(0).start()
        for copy in own:
            copy.start()
        into.pass_on(1)
        outof.start()
        for d in range(2, deep):
            into.pass_on(d)
            outof.pass_on(d - 1)
        for d in range(max(deep - 1, 1), deep):
            outof.pass_on(d)
        for k in range(1, chips):
            tok_x(k).wait_recv()
            tok_core(k).start()
        into.finish()
        outof.finish()
        for k in range(chips):
            tok_core(k).wait()
        for k in range(1, chips):
            tok_x(k).wait_send()
        for k in range(1, fsdp_size):
            vec(k).wait()
        for copy in own:
            copy.wait()

    any_space = pl.BlockSpec(memory_space=pl.ANY)
    return pl.pallas_call(
        kernel,
        in_specs=[pl.BlockSpec(memory_space=pltpu.VMEM)] * 4,
        out_specs=[any_space] * 4,
        out_shape=[
            jax.ShapeDtypeStruct((rows * seq_size, width), BF16),
            jax.ShapeDtypeStruct((in_part.shape[0] * fsdp_size, in_part.shape[1]), BF16),
            jax.ShapeDtypeStruct((out_slice.shape[0] * fsdp_size, width), BF16),
            jax.ShapeDtypeStruct((fsdp_size,) + vectors.shape, F32),
        ],
        scratch_shapes=[
            dma((4,)), dma((chips,)), dma((chips,)), dma((chips,)), dma((chips,)),
            dma((fsdp_size,)), dma((fsdp_size,)),
        ]
        + fsdp_sems(deep, across) * 2,
        compiler_params=talking(1),
        name="opening",
    )(tokens, in_part, out_slice, vectors)


def talking(collective_id):
    return pltpu.CompilerParams(
        collective_id=collective_id, has_side_effects=True, vmem_limit_bytes=VMEM_LIMIT
    )


CHUNKS = 4


def hidden_rows(parts, residual, gain, bias, seq_size, fsdp_size):
    rows, width = residual.shape
    chips = seq_size // CORES
    part = rows // CHUNKS
    dma = pltpu.SemaphoreType.DMA

    def kernel(*refs):
        own = refs[0 : 2 * chips : 2]
        other = refs[1 : 2 * chips : 2]
        res_ref, gain_ref, bias_ref, hidden_ref, normed_ref = refs[2 * chips : 2 * chips + 5]
        (
            from_core, total, from_x, mine,
            c_send, c_recv, x_send, x_recv, g_send, g_recv, f_send, f_recv, here,
        ) = refs[2 * chips + 5 :]
        p = Place(seq_size, fsdp_size)
        greet(p, False)

        def span(c):
            return pl.ds(c * part, part)

        def to_core(k, c):
            return remote(
                other[k].at[span(c)], from_core.at[k, span(c)],
                c_send.at[k, c], c_recv.at[k, c], seq=p.other(),
            )

        def along(k, c):
            return remote(
                total.at[k - 1, span(c)], from_x.at[k - 1, span(c)],
                x_send.at[k, c], x_recv.at[k, c], seq=p.along_x(k),
            )

        def share(k, c):
            return remote(
                mine.at[span(c)], normed_ref.at[2 * k, span(c)],
                g_send.at[k, c], g_recv.at[k, c], seq=p.along_x(-k),
            )

        def pass_on(k, c):
            return remote(
                mine.at[span(c)] if k == 0 else normed_ref.at[2 * k, span(c)],
                normed_ref.at[2 * k + 1, span(c)],
                f_send.at[k, c], f_recv.at[k, c], seq=p.other(),
            )

        far = range(1, chips)
        for k in [*far, 0]:
            for c in range(CHUNKS):
                to_core(k, c).start()
        for c in range(CHUNKS):
            for k in far:
                to_core(k, c).wait_recv()
                both = own[k][span(c)].astype(F32) + from_core[k, span(c)].astype(F32)
                total[k - 1, span(c)] = both.astype(BF16)
                along(k, c).start()
        for c in range(CHUNKS):
            to_core(0, c).wait_recv()
            rows_here = own[0][span(c)].astype(F32) + from_core[0, span(c)].astype(F32)
            for k in far:
                along(k, c).wait_recv()
                rows_here = rows_here + from_x[k - 1, span(c)].astype(F32)
            rows_here = rows_here + res_ref[span(c)].astype(F32)
            hidden_ref[span(c)] = rows_here
            unit = rows_here - jnp.mean(rows_here, axis=1, keepdims=True)
            unit = unit * lax.rsqrt(jnp.mean(unit * unit, axis=1, keepdims=True) + epsilon)
            mine[span(c)] = (unit * gain_ref[0:1, :] + bias_ref[0:1, :]).astype(BF16)
            for k in far:
                share(k, c).start()
            pass_on(0, c).start()
        keep = pltpu.make_async_copy(mine, normed_ref.at[0], here)
        keep.start()
        for c in range(CHUNKS):
            for k in far:
                share(k, c).wait_recv()
                pass_on(k, c).start()
        for c in range(CHUNKS):
            for k in range(chips):
                to_core(k, c).wait_send()
                pass_on(k, c).wait()
            for k in far:
                along(k, c).wait_send()
                share(k, c).wait_send()
        keep.wait()

    vmem = pl.BlockSpec(memory_space=pltpu.VMEM)
    block = (rows, width)
    several = (max(chips - 1, 1),) + block
    return pl.pallas_call(
        kernel,
        in_specs=[vmem] * (2 * chips + 3),
        out_specs=[vmem, pl.BlockSpec(memory_space=pl.ANY)],
        out_shape=[
            jax.ShapeDtypeStruct(block, F32),
            jax.ShapeDtypeStruct((2 * chips,) + block, BF16),
        ],
        scratch_shapes=[
            pltpu.VMEM((chips,) + block, BF16),
            pltpu.VMEM(several, BF16),
            pltpu.VMEM(several, BF16),
            pltpu.VMEM(block, BF16),
        ]
        + [dma((chips, CHUNKS))] * 8
        + [dma],
        compiler_params=talking(2),
        name="hidden_rows",
    )(
        *[value for pair in parts for value in pair],
        residual,
        jnp.broadcast_to(gain[None], (8, width)),
        jnp.broadcast_to(bias[None], (8, width)),
    )


def closing_rows(parts, arriving, base, prior, gain, seq_size, fsdp_size, low, collective_id):
    rows, width = base.shape
    chips = seq_size // CORES
    held = len(parts)
    part = rows // CHUNKS
    dma = pltpu.SemaphoreType.DMA
    far = range(1, held)

    def kernel(*refs):
        own, other = refs[0 : 2 * held : 2], refs[1 : 2 * held : 2]
        refs = refs[2 * held :]
        came, refs = refs[: len(arriving)], refs[len(arriving) :]
        base_ref, prior_ref, gain_ref, grad_ref = refs[:4]
        refs = refs[4:]
        if low:
            low_ref, refs = refs[0], refs[1:]
        sums_ref, from_core, total, from_x, c_send, c_recv, x_send, x_recv = refs
        p = Place(seq_size, fsdp_size)
        greet(p, False)

        def span(c):
            return pl.ds(c * part, part)

        def to_core(k, c):
            return remote(
                other[k].at[span(c)], from_core.at[k, span(c)],
                c_send.at[k, c], c_recv.at[k, c], seq=p.other(),
            )

        def along(k, c):
            return remote(
                total.at[k - 1, span(c)], from_x.at[k - 1, span(c)],
                x_send.at[k, c], x_recv.at[k, c], seq=p.along_x(k),
            )

        for k in [*far, 0]:
            for c in range(CHUNKS):
                to_core(k, c).start()
        for c in range(CHUNKS):
            for k in far:
                to_core(k, c).wait_recv()
                both = own[k][span(c)].astype(F32) + from_core[k, span(c)].astype(F32)
                total[k - 1, span(c)] = both.astype(BF16)
                along(k, c).start()
        gained = jnp.zeros((1, width), F32)
        biased = jnp.zeros((1, width), F32)
        for c in range(CHUNKS):
            to_core(0, c).wait_recv()
            gradient = own[0][span(c)].astype(F32) + from_core[0, span(c)].astype(F32)
            for k in far:
                along(k, c).wait_recv()
                gradient = gradient + from_x[k - 1, span(c)].astype(F32)
            for ref in came:
                gradient = gradient + ref[span(c)].astype(F32)
            unit = base_ref[span(c)].astype(F32)
            unit = unit - jnp.mean(unit, axis=1, keepdims=True)
            inverse = lax.rsqrt(jnp.mean(unit * unit, axis=1, keepdims=True) + epsilon)
            unit = unit * inverse
            gained = gained + jnp.sum(gradient * unit, axis=0, keepdims=True)
            biased = biased + jnp.sum(gradient, axis=0, keepdims=True)
            scaled = gradient * gain_ref[0:1, :]
            middle = jnp.mean(scaled, axis=1, keepdims=True)
            tilt = jnp.mean(scaled * unit, axis=1, keepdims=True)
            result = prior_ref[span(c)].astype(F32) + inverse * (scaled - middle - unit * tilt)
            grad_ref[span(c)] = result
            if low:
                low_ref[span(c)] = result.astype(BF16)
        which = lax.broadcasted_iota(jnp.int32, (8, width), 0)
        sums_ref[...] = jnp.where(which == 0, gained, jnp.where(which == 1, biased, 0.0))
        for c in range(CHUNKS):
            for k in range(held):
                to_core(k, c).wait_send()
            for k in far:
                along(k, c).wait_send()

    vmem = pl.BlockSpec(memory_space=pltpu.VMEM)
    block = (rows, width)
    several = (max(held - 1, 1),) + (block if held > 1 else (8, LANES))
    kinds = [(block, F32)] + ([(block, BF16)] if low else []) + [((8, width), F32)]
    operands = [value for pair in parts for value in pair] + list(arriving)
    operands += [base, prior, jnp.broadcast_to(gain[None], (8, width))]
    return pl.pallas_call(
        kernel,
        in_specs=[vmem] * len(operands),
        out_specs=[vmem] * len(kinds),
        out_shape=[jax.ShapeDtypeStruct(*kind) for kind in kinds],
        scratch_shapes=[
            pltpu.VMEM((held,) + block, BF16),
            pltpu.VMEM(several, BF16),
            pltpu.VMEM(several, BF16),
        ]
        + [dma((held, CHUNKS))] * 4,
        compiler_params=talking(collective_id),
        name="closing_rows",
    )(*operands)


class SeqShare:
    def __init__(self, place, piece, whole, sems, number):
        self.place, self.piece, self.whole = place, piece, whole
        self.x_send, self.x_recv, self.c_send, self.c_recv, self.here = (
            [sem.at[number] for sem in sems]
        )

    def x(self, k):
        p = self.place
        return remote(
            self.piece, self.whole.at[p.seq], self.x_send.at[k], self.x_recv.at[k],
            seq=p.along_x(k),
        )

    def core(self, k):
        p = self.place
        slot = self.whole.at[p.along_x(-k)]
        return remote(
            self.piece if k == 0 else slot, slot, self.c_send.at[k], self.c_recv.at[k],
            seq=p.other(),
        )

    def keep(self):
        return pltpu.make_async_copy(self.piece, self.whole.at[self.place.seq], self.here)

    def start(self):
        for k in range(1, self.place.chips):
            self.x(k).start()
        self.core(0).start()
        self.keep().start()

    def finish(self):
        for k in range(1, self.place.chips):
            self.x(k).wait_recv()
            self.core(k).start()
        for k in range(self.place.chips):
            self.core(k).wait()
        for k in range(1, self.place.chips):
            self.x(k).wait_send()
        self.keep().wait()


def share_sems(chips, count):
    dma = pltpu.SemaphoreType.DMA
    return [dma((count, chips))] * 4 + [dma((count,))]


def share_pieces(pieces, seq_size, fsdp_size, collective_id):
    chips = seq_size // CORES
    count = len(pieces)

    def kernel(*refs):
        ins, outs, sems = refs[:count], refs[count : 2 * count], refs[2 * count :]
        p = Place(seq_size, fsdp_size)
        greet(p, False)
        shares = [SeqShare(p, ins[i], outs[i], sems, i) for i in range(count)]
        for share in shares:
            share.start()
        for share in shares:
            share.finish()

    return pl.pallas_call(
        kernel,
        in_specs=[pl.BlockSpec(memory_space=pltpu.VMEM)] * count,
        out_specs=[pl.BlockSpec(memory_space=pl.ANY)] * count,
        out_shape=[jax.ShapeDtypeStruct((seq_size,) + v.shape, v.dtype) for v in pieces],
        scratch_shapes=share_sems(chips, count),
        compiler_params=talking(collective_id),
        name="share_pieces",
    )(*pieces)


def sum_and_share(partial, vectors, pieces, seq_size, fsdp_size, collective_id):
    chips = seq_size // CORES
    deep = planes(fsdp_size)
    across = fsdp_size // deep
    rows, width = partial.shape[0] // fsdp_size, partial.shape[1]
    lanes = vectors.shape[1] // fsdp_size
    count = len(pieces) + 1
    dma = pltpu.SemaphoreType.DMA

    def kernel(part_ref, vec_ref, *refs):
        ins, refs = refs[: count - 1], refs[count - 1 :]
        outs, refs = refs[:count], refs[count:]
        (
            vec_out, from_y, over_y, from_z, piece, vec_cut, vec_f, vec_s, vec_sum,
            y_send, y_recv, z_send, z_recv, f_send, f_recv, s_send, s_recv,
        ) = refs[:17]
        sems = refs[17:]
        p = Place(seq_size, fsdp_size)
        greet_all(p)

        def block(z, y):
            return pl.ds(pl.multiple_of((z * across + y) * rows, rows), rows)

        def to_y(z, k):
            return remote(
                part_ref.at[block(z, (p.y + k) % across)], from_y.at[k, z],
                y_send.at[k, z], y_recv.at[k, z], fsdp=p.along_y(k),
            )

        def to_z(k):
            return remote(
                over_y.at[(p.z + k) % deep], from_z.at[k],
                z_send.at[k], z_recv.at[k], fsdp=p.along_z(k),
            )

        def vec_to(k):
            return remote(
                vec_cut.at[(p.fsdp + k) % fsdp_size], vec_f.at[k],
                f_send.at[k], f_recv.at[k], fsdp=(p.fsdp + k) % fsdp_size,
            )

        def vec_over(k):
            return remote(
                vec_sum, vec_s.at[k], s_send.at[k], s_recv.at[k], seq=(p.seq + k) % seq_size
            )

        for f in range(fsdp_size):
            vec_cut[f] = vec_ref[:, f * lanes : (f + 1) * lanes]
        for k in range(1, fsdp_size):
            vec_to(k).start()
        for z in range(deep):
            for k in range(1, across):
                to_y(z, k).start()
        shares = [SeqShare(p, ins[i], outs[i], sems, i) for i in range(count - 1)]
        for share in shares:
            share.start()
        for z in range(deep):
            total = part_ref[block(z, p.y)].astype(F32)
            for k in range(1, across):
                to_y(z, k).wait_recv()
                total = total + from_y[k, z].astype(F32)
            over_y[z] = total.astype(BF16)
        for k in range(1, deep):
            to_z(k).start()
        vec_total = vec_cut[p.fsdp]
        for k in range(1, fsdp_size):
            vec_to(k).wait_recv()
            vec_total = vec_total + vec_f[k]
        vec_sum[...] = vec_total
        for k in range(1, seq_size):
            vec_over(k).start()
        total = over_y[p.z].astype(F32)
        for k in range(1, deep):
            to_z(k).wait_recv()
            total = total + from_z[k].astype(F32)
        piece[...] = total.astype(BF16)
        shares.append(SeqShare(p, piece, outs[-1], sems, count - 1))
        shares[-1].start()
        for k in range(1, seq_size):
            vec_over(k).wait_recv()
            vec_total = vec_total + vec_s[k]
        vec_out[...] = vec_total
        for share in shares:
            share.finish()
        for z in range(deep):
            for k in range(1, across):
                to_y(z, k).wait_send()
        for k in range(1, deep):
            to_z(k).wait_send()
        for k in range(1, fsdp_size):
            vec_to(k).wait_send()
        for k in range(1, seq_size):
            vec_over(k).wait_send()

    vmem = pl.BlockSpec(memory_space=pltpu.VMEM)
    shapes = [v.shape for v in pieces] + [(rows, width)]
    cut = (8, lanes)
    return pl.pallas_call(
        kernel,
        in_specs=[vmem] * (count + 1),
        out_specs=[pl.BlockSpec(memory_space=pl.ANY)] * count + [vmem],
        out_shape=[jax.ShapeDtypeStruct((seq_size,) + shape, BF16) for shape in shapes]
        + [jax.ShapeDtypeStruct(cut, F32)],
        scratch_shapes=[
            pltpu.VMEM((across, deep, rows, width), BF16),
            pltpu.VMEM((deep, rows, width), BF16),
            pltpu.VMEM((deep, rows, width), BF16),
            pltpu.VMEM((rows, width), BF16),
            pltpu.VMEM((fsdp_size,) + cut, F32),
            pltpu.VMEM((fsdp_size,) + cut, F32),
            pltpu.VMEM((seq_size,) + cut, F32),
            pltpu.VMEM(cut, F32),
        ]
        + [dma((across, deep))] * 2
        + [dma((deep,))] * 2
        + [dma((fsdp_size,))] * 2
        + [dma((seq_size,))] * 2
        + share_sems(chips, count),
        compiler_params=talking(collective_id),
        name="sum_and_share",
    )(partial, vectors, *pieces)


def own_columns(gate, up, me, seq_size, fsdp_size):
    rows, columns = gate.shape
    shard = columns // fsdp_size
    chunk = shard // seq_size

    def kernel(me_ref, gate_ref, up_ref, out_ref):
        for s in range(seq_size):

            @pl.when(me_ref[0] == s)
            def _(s=s):
                for which, ref in enumerate((gate_ref, up_ref)):
                    taken = [
                        ref[:, f * shard + s * chunk : f * shard + (s + 1) * chunk]
                        for f in range(fsdp_size)
                    ]
                    at = which * chunk * fsdp_size
                    out_ref[:, at : at + chunk * fsdp_size] = jnp.concatenate(taken, axis=1)

    return pl.pallas_call(
        kernel,
        grid_spec=pltpu.PrefetchScalarGridSpec(
            num_scalar_prefetch=1,
            grid=(1,),
            in_specs=[pl.BlockSpec((rows, columns), lambda i, m: (0, 0))] * 2,
            out_specs=pl.BlockSpec((rows, 2 * chunk * fsdp_size), lambda i, m: (0, 0)),
        ),
        out_shape=jax.ShapeDtypeStruct((rows, 2 * chunk * fsdp_size), BF16),
        compiler_params=params(),
        cost_estimate=cost(rows, 1, 2 * columns),
        name="own_columns",
    )(jnp.full((1,), me, jnp.int32), gate, up)


def whole_columns(pieces, fsdp_size):
    seq_size, rows, columns = pieces.shape
    units = columns // 2
    chunk = units // fsdp_size

    def kernel(in_ref, gate_ref, up_ref):
        for which, ref in enumerate((gate_ref, up_ref)):
            for f in range(fsdp_size):
                at = which * units + f * chunk
                taken = [in_ref[s, :, at : at + chunk].astype(F32) for s in range(seq_size)]
                whole = jnp.concatenate(taken, axis=1)
                ref[:, f * chunk * seq_size : (f + 1) * chunk * seq_size] = whole

    tile = rows // 4
    out = pl.BlockSpec((tile, units * seq_size), lambda i: (i, 0))
    return pl.pallas_call(
        kernel,
        grid=(4,),
        in_specs=[pl.BlockSpec((seq_size, tile, columns), lambda i: (0, i, 0))],
        out_specs=[out, out],
        out_shape=[jax.ShapeDtypeStruct((rows, units * seq_size), F32)] * 2,
        compiler_params=params(),
        cost_estimate=cost(rows, 1, 2 * columns * seq_size),
        name="whole_columns",
    )(pieces)


def own_heads_spread(project_in, me, pairs, seq_size):
    rows, columns = project_in.shape
    every = columns // 3 // LANES
    step = seq_size // 2

    def kernel(me_ref, low_ref, high_ref, out_ref):
        lane = lax.broadcasted_iota(jnp.int32, (rows, LANES), 1)
        odd = me_ref[0] % 2 == 1
        first = low_ref[...].astype(F32)
        second = high_ref[...].astype(F32)
        first = jnp.where(odd, pltpu.roll(first, HEAD_DIM, 1), first)
        second = jnp.where(odd, second, pltpu.roll(second, HEAD_DIM, 1))
        out_ref[...] = jnp.where(lane < HEAD_DIM, first, second).astype(BF16)

    def source(ahead):
        return pl.BlockSpec(
            (rows, LANES),
            lambda part, p, m: (0, part * every + (2 * p + ahead) * step + m[0] // 2),
        )

    return pl.pallas_call(
        kernel,
        grid_spec=pltpu.PrefetchScalarGridSpec(
            num_scalar_prefetch=1,
            grid=(3, pairs),
            in_specs=[source(0), source(1)],
            out_specs=pl.BlockSpec((rows, LANES), lambda part, p, m: (0, 3 * p + part)),
        ),
        out_shape=jax.ShapeDtypeStruct((rows, 3 * pairs * LANES), BF16),
        compiler_params=params(),
        name="own_heads",
    )(jnp.full((1,), me, jnp.int32), project_in, project_in)


def whole_heads_spread(pieces):
    seq_size, rows, columns = pieces.shape
    each = columns * seq_size // 3
    step = seq_size // 2

    def kernel(in_ref, out_ref):
        lane = lax.broadcasted_iota(jnp.int32, (rows // 4, LANES), 1)
        for part in range(3):
            for b in range(each // LANES):
                shard, seq = b // step, 2 * (b % step)
                at = (3 * (shard // 2) + part) * LANES
                first = in_ref[seq, :, at : at + LANES].astype(F32)
                second = in_ref[seq + 1, :, at : at + LANES].astype(F32)
                if shard % 2:
                    first = pltpu.roll(first, HEAD_DIM, 1)
                else:
                    second = pltpu.roll(second, HEAD_DIM, 1)
                start = part * each + b * LANES
                out_ref[:, start : start + LANES] = jnp.where(lane < HEAD_DIM, first, second)

    return pl.pallas_call(
        kernel,
        grid=(4,),
        in_specs=[pl.BlockSpec((seq_size, rows // 4, columns), lambda i: (0, i, 0))],
        out_specs=pl.BlockSpec((rows // 4, 3 * each), lambda i: (i, 0)),
        out_shape=jax.ShapeDtypeStruct((rows, 3 * each), F32),
        compiler_params=params(),
        cost_estimate=cost(rows, 1, 3 * each),
        name="whole_heads",
    )(pieces)


def gather_fsdp(value):
    return lax.all_gather(value, "fsdp", axis=0, tiled=True)


def scatter_fsdp(value):
    return lax.psum_scatter(value, "fsdp", scatter_dimension=0, tiled=True)


def local(
    tokens,
    cont_lengths,
    project_in,
    project_out,
    gate_weight,
    up_weight,
    down_weight,
    first_gain,
    first_bias,
    second_gain,
    second_bias,
    grad_output,
):
    rows_dev, width = tokens.shape[1:]
    seq_size = lax.axis_size("seq")
    fsdp_size = lax.axis_size("fsdp")
    chips = seq_size // CORES
    total_rows = rows_dev * seq_size
    me = lax.axis_index("seq")
    order = seq_order(chips)
    shard_rows = project_in.shape[0]
    own_pairs = width // LANES // seq_size
    pieces_out = project_out.shape[0] // seq_size
    pieces_down = down_weight.shape[0] // seq_size
    far = range(1, chips)

    spread = pieces_out == HEAD_DIM
    if spread:
        in_part = own_heads_spread(project_in, me, own_pairs, seq_size)
    else:
        in_part = own_heads(project_in, me, own_pairs)
    vectors = jnp.stack([first_gain, first_bias, second_gain, second_bias]).astype(F32)
    all_tokens, w_in, w_out, vectors = opening(
        tokens[0],
        in_part,
        lax.dynamic_slice_in_dim(project_out, me * pieces_out, pieces_out, 0),
        jnp.concatenate([vectors, vectors]),
        seq_size,
        fsdp_size,
    )
    if not spread:
        own_rows = width // seq_size
        w_out = lax.dynamic_slice_in_dim(gather_fsdp(project_out), me * own_rows, own_rows, 0)
    vectors = jnp.transpose(vectors[:, :4], (1, 0, 2)).reshape(4, width)
    gain_one, bias_one, gain_two, bias_two = [vectors[i] for i in range(4)]
    upstream_own = tie(grad_output[0], all_tokens)
    upstream_far = [from_chip(upstream_own, chips, ahead) for ahead in far]
    gate_late, up_late, down_late = tie((gate_weight, up_weight, down_weight), w_in)
    w_down = gather_fsdp(lax.dynamic_slice_in_dim(down_late, me * pieces_down, pieces_down, 0))
    w_gate_up = gather_fsdp(own_columns(gate_late, up_late, me, seq_size, fsdp_size))

    cosine, sine, ends = rope_tables(cont_lengths[0], total_rows)

    qkv, normed_first = project(all_tokens, w_in, gain_one, bias_one, cosine, sine)
    attended, qx = attend(ends, qkv)
    upstream_blocks = [grad_output[0], core_swap(grad_output[0], chips)]
    for block in upstream_far:
        block = tie(block, attended)
        upstream_blocks += [block, core_swap(block, chips)]

    def scatter_end(started):
        arriving, own, other, _ = started
        total = own.astype(F32) + other.astype(F32)
        for part in arriving:
            total = total + part.astype(F32)
        return total

    attended = tie(attended, upstream_blocks)
    parts = chip_matmul(attended, w_out, order, rows_dev, False, "attention_out")
    hidden, normed_blocks = hidden_rows(parts, tokens[0], gain_two, bias_two, seq_size, fsdp_size)
    product, grads, normed_second, upstream_all = feed(
        normed_blocks, upstream_blocks, w_gate_up, w_down
    )

    far_order = jnp.arange(CORES, chips * CORES, dtype=jnp.int32)
    sent = [
        (own.astype(F32) + core_swap(other, chips).astype(F32)).astype(BF16)
        for own, other in chip_matmul(grads, w_gate_up, far_order, rows_dev, True, "feed_back")
    ]
    arriving = [to_chip(value, chips, ahead) for value, ahead in zip(sent, far)]
    own, other, grad_down = near_and_down(
        tie(grads, *sent), w_gate_up, product, upstream_all, rows_dev
    )
    grad_hidden, low_own, sums_two = closing_rows(
        [(own, other)], tie(arriving, grad_down), hidden, grad_output[0], gain_two,
        seq_size, fsdp_size, True, 3,
    )
    low_far = [from_chip(low_own, chips, ahead) for ahead in far]
    low_near = [low_own, core_swap(low_own, chips)]

    normed_late, product_late = tie((normed_second, product), low_own)
    grad_gate_up = weight_grad(normed_late, grads, "grad_gate_up")
    product_late = tie(product_late, grad_gate_up)

    near_order = jnp.arange(chips * CORES, dtype=jnp.int32)
    layer_parts = chip_matmul(product_late, w_down, near_order, rows_dev, False, "feed_down")
    (layer_own, layer_other), layer_far = layer_parts[0], layer_parts[1:]
    low_far = tie(low_far, layer_own)
    layer_far = tie(layer_far, low_far)
    grad_down_piece = scatter_fsdp(tie(grad_down, low_own))
    grad_gate_up_piece = scatter_fsdp(tie(grad_gate_up, low_far))
    low_blocks = low_near
    for block in low_far:
        low_blocks = low_blocks + [block, core_swap(block, chips)]
    layer_sent = [
        (own.astype(F32) + core_swap(other, chips).astype(F32)).astype(BF16)
        for own, other in layer_far
    ]
    layer_arriving = [to_chip(s, chips, ahead) for s, ahead in zip(layer_sent, far)]
    grad_attended, low_hidden = blocks_matmul(tie(low_blocks, layer_sent), w_out, order)
    grad_out = dot_first(attended, low_hidden).astype(BF16)
    grad_attended = tie(grad_attended, grad_out)

    grad_qkv = attend_back(ends, qkv, qx, grad_attended, attended, cosine, sine)
    grad_in = weight_grad(normed_first, grad_qkv, "grad_project_in")
    grad_in_piece = scatter_fsdp(grad_in)
    grad_late = tie(grad_qkv, grad_in)
    parts = chip_matmul(grad_late, w_in, order, rows_dev, True, "project_back")
    input_gradient, sums_one = closing_rows(
        parts, [], tokens[0], grad_hidden, gain_one, seq_size, fsdp_size, False, 4
    )
    layer_rows = hidden + scatter_end(
        (layer_arriving, layer_own, core_swap(layer_other, chips), None)
    )

    sums = jnp.concatenate([sums_one[:2], sums_two[:2], sums_one[2:6]])
    all_gate_up, all_down, all_out, sums = sum_and_share(
        grad_out, sums, [grad_gate_up_piece, grad_down_piece], seq_size, fsdp_size, 5
    )
    (all_in,) = share_pieces([tie(grad_in_piece, all_out)], seq_size, fsdp_size, 6)
    if spread:
        grad_in = whole_heads_spread(all_in)
        grad_out = all_out.reshape(project_out.shape).astype(F32)
    else:
        grad_in = all_in.reshape(seq_size, shard_rows, own_pairs, 3, LANES)
        grad_in = jnp.transpose(grad_in, (1, 3, 0, 2, 4)).reshape(shard_rows, 3 * width)
        grad_in = grad_in.astype(F32)
        whole = jnp.zeros((width, width), F32)
        whole = lax.dynamic_update_slice_in_dim(
            whole, grad_out.astype(F32), me * (width // seq_size), 0
        )
        grad_out = lax.psum(scatter_fsdp(whole), "seq")
    grad_gate, grad_up = whole_columns(all_gate_up, fsdp_size)
    return (
        layer_rows.astype(BF16)[None],
        input_gradient[None],
        grad_in,
        grad_out,
        grad_gate,
        grad_up,
        all_down.reshape(down_weight.shape).astype(F32),
        sums[0],
        sums[1],
        sums[2],
        sums[3],
    )


def solution(mesh):
    return jax.shard_map(
        local,
        mesh=mesh,
        in_specs=(
            P("fsdp", "seq", None),
            P("fsdp", None),
            P("fsdp", None),
            P("fsdp", None),
            P("fsdp", None),
            P("fsdp", None),
            P("fsdp", None),
            P("fsdp"),
            P("fsdp"),
            P("fsdp"),
            P("fsdp"),
            P("fsdp", "seq", None),
        ),
        out_specs=(
            P("fsdp", "seq", None),
            P("fsdp", "seq", None),
            P("fsdp", None),
            P("fsdp", None),
            P("fsdp", None),
            P("fsdp", None),
            P("fsdp", None),
            P("fsdp"),
            P("fsdp"),
            P("fsdp"),
            P("fsdp"),
        ),
        check_vma=False,
    )
```

time: 1420 us -> 1080 us (0.76)
  Pallas kernels: 214 us -> 955 us
  waiting for transfers between devices: 549 us -> 33.7 us
  matrix products: 282 us -> 10.2 us
  local copies, waits for them, and re-layouts: 158 us -> 20.3 us
  starting transfers between devices: 72.4 us -> 7.03 us
  other arithmetic: 88.3 us -> 26.7 us
  blocking collectives: 38.2 us -> 0 us
    pallas_call x0 -> x19, Pallas kernels: none -> 750 us  [the longest x1 128 us: hidden_rows(): pl.pallas_call(kernel, in_specs=[vmem] * (2 * chips + 3), out_specs=[vmem...]
    ppermute x17 -> x4, waiting for transfers between devices: 465 us -> 15.6 us  [from_chip(): lax.ppermute(value, 'seq', [(i, (i - ahead * CORES) % size) for i in rang...]
    dot_general x9 -> x0, matrix products: 184 us -> none  [the longest x5 112 us: dot_last(): lax.dot_general(left_side, right_side, (((1,), (1,)), ((), ())), preferre...]
    dot_general x5 -> x1, matrix products: 98 us -> 10.2 us  [dot_first(): lax.dot_general(left_side, right_side, (((0,), (0,)), ((), ())), preferre...]
    unnamed x12 -> x5, waiting for transfers between devices: 52.6 us -> 0.08 us
    dynamic_update_slice x34 -> x0, local copies, waits for them, and re-layouts: 45.1 us -> none  [gather_rows(): whole = lax.dynamic_update_slice_in_dim(whole, held, start, 0)]
    ppermute x17 -> x4, starting transfers between devices: 37.9 us -> 3.25 us  [from_chip(): lax.ppermute(value, 'seq', [(i, (i - ahead * CORES) % size) for i in rang...]
    unnamed x105 -> x35, local copies, waits for them, and re-layouts: 41.3 us -> 8.74 us
  transfers between devices with their start and end apart: 54 -> 16, of which waited for: 20 -> 5; matrix products, arithmetic and copies ran while one was open for 30% -> 3% of each run, Pallas kernels for 15% -> 67%
where the time goes in v2:
time: 1080 us; the launch traced here: 1070 us
  Pallas kernels  955 us (88%)
  waiting for transfers between devices  33.7 us (3%)
  other arithmetic  26.7 us (2%)
  local copies, waits for them, and re-layouts  20.3 us (2%)
  between operations  14.3 us (1%)
    pallas_call x1, Pallas kernels, hidden_rows(): pl.pallas_call(kernel, in_specs=[vmem] * (2 * chips + 3), out_specs=[vmem...  128 us
    pallas_call x2, Pallas kernels, closing_rows(): pl.pallas_call(kernel, in_specs=[vmem] * len(operands), out_specs=[vmem]...  108 us
    pallas_call x1, Pallas kernels, attend_back(): pl.pallas_call(attend_back_kernel, grid_spec=pltpu.PrefetchScalarGridSpec...  108 us
    pallas_call x1, Pallas kernels, opening(): pl.pallas_call(kernel, in_specs=[pl.BlockSpec(memory_space=pltpu.VMEM)] *...  98.5 us
    pallas_call x1, Pallas kernels, sum_and_share(): pl.pallas_call(kernel, in_specs=[vmem] * (count + 1), out_specs=[pl.Block...  97.8 us
    pallas_call x4, Pallas kernels, chip_matmul(): pl.pallas_call(kernel, grid_spec=pltpu.PrefetchScalarGridSpec(num_scalar_...  88.8 us
    pallas_call x1, Pallas kernels, attend(): pl.pallas_call(attend_kernel, grid_spec=pltpu.PrefetchScalarGridSpec(num_...  69.4 us
    pallas_call x2, Pallas kernels, weight_grad(): pl.pallas_call(kernel, grid=(height // tile, columns // part), in_specs=[...  60.9 us
  transfers between devices with their start and end apart: 16, of which 5 were waited for; matrix products, arithmetic and copies ran while one was open for 3% of the time, Pallas kernels for 67%

profile of v2, /device:TPU:9, one launch (start us, length us, event | category | flops | bytes accessed | tf_op | source)
XLA Modules:
  0.0 1067.6 jit_solution(1438757425396868714)
XLA Ops:
  7.2 0.8 stack.33
  8.1 0.7 stack.34
  8.7 0.7 stack.35
  9.4 0.7 stack.36
  10.1 0.6 concatenate.10.vec_ref
  10.7 1.7 constant_dynamic-slice_fusion.out_ref
  12.3 7.5 own_heads.1.in_ref
  19.9 98.5 %opening.1 = (bf16[2560,2048]{1,0:T(8,128)(2,1)}, bf16[2048,1536]{1,0:T(8,128)(2,1)}, bf16[512,2048]{1,0:T(8,128)(2,1)}, f32[8,8,256]{2,1,0:T(8,128)}) custom-call(bf16[640,2048]{1,0:T(8,128)(2,1)} %bitcast.35, bf16[256,1536]{1,0:T(8,128)(2,1)} %own_heads.1.in_ref, bf16[64,2048]{1,0:T(8,128)(2,1)} %constant_dynamic-slice_fusion.out_ref, ...), custom_call_target="tpu_custom_call" | custom-call | tf_op jit(solution)/shard_map/opening/pallas_call | solution.py:859
  118.4 0.9 constant_dynamic-slice_fusion.1
  119.4 4.6 own_columns.1
  124.1 2.2 collective-permute-start
  126.3 1.3 collective-permute-start.1
  127.9 6.3 fusion.3
  134.2 0.6 broadcast_in_dim.112.gain_ref.refs_6_
  134.8 0.6 broadcast_in_dim.114.bias_ref
  135.5 28.6 %project_in_rope.1 = (bf16[2560,1536]{1,0:T(8,128)(2,1)}, bf16[2560,2048]{1,0:T(8,128)(2,1)}) custom-call(bf16[2560,2048]{1,0:T(8,128)(2,1)} %get-tuple-element.78.x_ref, bf16[2048,1536]{1,0:T(8,128)(2,1)} %get-tuple-element.79.w_ref, f32[8,2048]{1,0:T(8,128)} %broadcast_in_dim.112.gain_ref.refs_6_, f32[8,2048]{1,0:T(8,128)} %broadcast_in_dim.114.bias_ref, ...), custom_call_target="tpu_custom_call" | custom-call | flops 16106127360 | bytes 24641536 | tf_op jit(solution)/shard_map/project_in_rope/pallas_call | solution.py:104
  164.1 69.4 %attend.1 = (bf16[2560,512]{1,0:T(8,128)(2,1)}, bf16[8,2560,128]{2,1,0:T(8,128)(2,1)}) custom-call(s32[2]{0:T(128)} %copy-done.8, bf16[2560,1536]{1,0:T(8,128)(2,1)} %get-tuple-element.81.refs_0_.refs_1_.refs_2_.refs_3_.refs_4_.refs_5_.k_ref.v_ref, bf16[2560,1536]{1,0:T(8,128)(2,1)} %get-tuple-element.81.refs_0_.refs_1_.refs_2_.refs_3_.refs_4_.refs_5_.k_ref.v_ref, ...), custom_call_target="tpu_custom_call" | custom-call | flops 26843545600 | bytes 7864320 | tf_op jit(solution)/shard_map/attend/pallas_call | solution.py:218
  233.5 0.4 collective-permute-start.2
  233.9 0.5 iota_add_fusion.1.order_ref
  234.4 0.7 pad_add_fusion.order_ref
  235.1 3.7 collective-permute-done.2.refs_3_
  238.8 13.7 %attention_out.1 = (bf16[640,2048]{1,0:T(8,128)(2,1)}, bf16[640,2048]{1,0:T(8,128)(2,1)}, bf16[640,2048]{1,0:T(8,128)(2,1)}, bf16[640,2048]{1,0:T(8,128)(2,1)}) custom-call(s32[4]{0:T(128)} %pad_add_fusion.order_ref, bf16[2560,512]{1,0:T(8,128)(2,1)} %get-tuple-element.85.x_ref.o_ref, bf16[512,2048]{1,0:T(8,128)(2,1)} %get-tuple-element.86.w_ref.refs_4_), custom_call_target="tpu_custom_call" | custom-call | flops 5368709120 | bytes 15204352 | tf_op jit(solution)/shard_map/attention_out/pallas_call | solution.py:389
  252.5 0.6 broadcast_in_dim.122.refs_5_
  253.1 0.6 broadcast_in_dim.124.refs_6_
  253.8 127.7 %hidden_rows.1 = (f32[640,2048]{1,0:T(8,128)}, bf16[4,640,2048]{2,1,0:T(8,128)(2,1)}) custom-call(bf16[640,2048]{1,0:T(8,128)(2,1)} %get-tuple-element.87.refs_0_, bf16[640,2048]{1,0:T(8,128)(2,1)} %get-tuple-element.88.refs_1_, bf16[640,2048]{1,0:T(8,128)(2,1)} %get-tuple-element.89.refs_2_, bf16[640,2048]{1,0:T(8,128)(2,1)} %get-tuple-element.90.refs_3_, ...), custom_call_target="tpu_custom_call" | custom-call | tf_op jit(solution)/shard_map/hidden_rows/pallas_call | solution.py:975
  381.5 60.0 %feed.1 = (bf16[2560,1408]{1,0:T(8,128)(2,1)}, bf16[2560,2816]{1,0:T(8,128)(2,1)}, bf16[2560,2048]{1,0:T(8,128)(2,1)}, bf16[2560,2048]{1,0:T(8,128)(2,1)}) custom-call(bf16[4,640,2048]{2,1,0:T(8,128)(2,1)} %get-tuple-element.92.x_ref, bf16[640,2048]{1,0:T(8,128)(2,1)} %bitcast.43, bf16[640,2048]{1,0:T(8,128)(2,1)} %collective-permute-done.refs_1_, ...), custom_call_target="tpu_custom_call" | custom-call | flops 44291850240 | bytes 55967744 | tf_op jit(solution)/shard_map/feed/pallas_call | solution.py:496
  441.5 23.7 %feed_back.1 = (bf16[640,2048]{1,0:T(8,128)(2,1)}, bf16[640,2048]{1,0:T(8,128)(2,1)}) custom-call(s32[2]{0:T(128)} %iota_add_fusion.1.order_ref, bf16[2560,2816]{1,0:T(8,128)(2,1)} %get-tuple-element.101.x_ref.g_ref, bf16[2048,2816]{1,0:T(8,128)(2,1)} %all-gather.3.cloned.1.call-done.refs_4_.w_ref), custom_call_target="tpu_custom_call" | custom-call | flops 14763950080 | bytes 23986176 | tf_op jit(solution)/shard_map/feed_back/pallas_call | solution.py:389
  465.3 5.0 collective-permute-done.3
  470.3 2.8 add_convert_fusion.2
  473.4 42.5 %near_and_down.1 = (bf16[640,2048]{1,0:T(8,128)(2,1)}, bf16[640,2048]{1,0:T(8,128)(2,1)}, bf16[1408,2048]{1,0:T(8,128)(2,1)}) custom-call(bf16[2560,2816]{1,0:T(8,128)(2,1)} %get-tuple-element.101.x_ref.g_ref, bf16[2048,2816]{1,0:T(8,128)(2,1)} %all-gather.3.cloned.1.call-done.refs_4_.w_ref, bf16[2560,1408]{1,0:T(8,128)(2,1)} %get-tuple-element.110.p_ref.x_ref, ...), custom_call_target="tpu_custom_call" | custom-call | flops 36909875200 | bytes 42663936 | tf_op jit(solution)/shard_map/near_and_down/pallas_call | solution.py:552
  515.9 15.6 %collective-permute-done.4.refs_2_ = bf16[640,2048]{1,0:T(8,128)(2,1)S(1)} collective-permute-done((bf16[640,2048]{1,0:T(8,128)(2,1)S(1)}, bf16[640,2048]{1,0:T(8,128)(2,1)S(1)}, u32[]{:S(2)}, u32[]{:S(2)}) %collective-permute-start.4) | collective-permute-done | bytes 2621472 | tf_op jit(solution)/shard_map/ppermute | solution.py:624
  531.5 1.5 copy-done.4
  533.0 16.9 %closing_rows.2 = (f32[640,2048]{1,0:T(8,128)}, bf16[640,2048]{1,0:T(8,128)(2,1)}, f32[8,2048]{1,0:T(8,128)}) custom-call(bf16[640,2048]{1,0:T(8,128)(2,1)} %get-tuple-element.103.refs_0_, bf16[640,2048]{1,0:T(8,128)(2,1)} %get-tuple-element.104.refs_1_, bf16[640,2048]{1,0:T(8,128)(2,1)} %copy-done.4, f32[640,2048]{1,0:T(8,128)} %get-tuple-element.91.refs_3_, ...), custom_call_target="tpu_custom_call" | custom-call | tf_op jit(solution)/shard_map/closing_rows/pallas_call | solution.py:1082
  550.0 1.3 collective-permute-start.6
  551.3 38.3 %grad_gate_up.1 = bf16[2048,2816]{1,0:T(8,128)(2,1)} custom-call(bf16[2560,2048]{1,0:T(8,128)(2,1)} %get-tuple-element.109.x_ref, bf16[2560,2816]{1,0:T(8,128)(2,1)} %get-tuple-element.101.x_ref.g_ref), custom_call_target="tpu_custom_call" | custom-call | flops 29527900160 | bytes 36438016 | tf_op jit(solution)/shard_map/grad_gate_up/pallas_call | solution.py:424
  589.6 0.5 iota.49.order_ref
  590.1 25.4 %feed_down.1 = (bf16[640,2048]{1,0:T(8,128)(2,1)}, bf16[640,2048]{1,0:T(8,128)(2,1)}, bf16[640,2048]{1,0:T(8,128)(2,1)}, bf16[640,2048]{1,0:T(8,128)(2,1)}) custom-call(s32[4]{0:T(128)} %iota.49.order_ref, bf16[2560,1408]{1,0:T(8,128)(2,1)} %get-tuple-element.110.p_ref.x_ref, bf16[1408,2048]{1,0:T(8,128)(2,1)} %all-gather.5.cloned.1.call-done.refs_5_.w_ref), custom_call_target="tpu_custom_call" | custom-call | flops 14763950080 | bytes 23461888 | tf_op jit(solution)/shard_map/feed_down/pallas_call | solution.py:389
  615.6 1.7 copy-done.9
  617.2 0.5 collective-permute-start.9
  617.7 8.1 collective-permute-done.7
  625.8 2.8 add_convert_fusion.1
  628.7 1.2 collective-permute-done.10.refs_3_
  630.1 1.5 copy-done.11
  631.7 15.5 %grad_attended.1 = (bf16[2560,512]{1,0:T(8,128)(2,1)}, bf16[2560,2048]{1,0:T(8,128)(2,1)}) custom-call(s32[4]{0:T(128)} %pad_add_fusion.order_ref, bf16[640,2048]{1,0:T(8,128)(2,1)} %get-tuple-element.119.refs_0_, bf16[640,2048]{1,0:T(8,128)(2,1)} %copy-done.10, bf16[640,2048]{1,0:T(8,128)(2,1)} %collective-permute-done.6.refs_2_, ...), custom_call_target="tpu_custom_call" | custom-call | flops 5368709120 | bytes 15204352 | tf_op jit(solution)/shard_map/grad_attended/pallas_call | solution.py:596
  647.2 10.2 convolution_convert_fusion.part_ref
  657.3 107.6 %attend_back.1.g_ref.x_ref = bf16[2560,1536]{1,0:T(8,128)(2,1)} custom-call(s32[2]{0:T(128)} %copy-done.8, bf16[8,2560,128]{2,1,0:T(8,128)(2,1)} %get-tuple-element.118.qx_ref, bf16[2560,1536]{1,0:T(8,128)(2,1)} %get-tuple-element.81.refs_0_.refs_1_.refs_2_.refs_3_.refs_4_.refs_5_.k_ref.v_ref, ...), custom_call_target="tpu_custom_call" | custom-call | flops 67108864000 | bytes 7864320 | tf_op jit(solution)/shard_map/attend_back/pallas_call | solution.py:331
  764.9 22.6 %grad_project_in.1 = bf16[2048,1536]{1,0:T(8,128)(2,1)} custom-call(bf16[2560,2048]{1,0:T(8,128)(2,1)} %get-tuple-element.126.x_ref, bf16[2560,1536]{1,0:T(8,128)(2,1)} %attend_back.1.g_ref.x_ref), custom_call_target="tpu_custom_call" | custom-call | flops 16106127360 | bytes 24641536 | tf_op jit(solution)/shard_map/grad_project_in/pallas_call | solution.py:424
  787.5 0.4 collective-permute-start.5
  788.2 0.8 slice.46
  789.0 26.0 %project_back.1 = (bf16[640,2048]{1,0:T(8,128)(2,1)}, bf16[640,2048]{1,0:T(8,128)(2,1)}, bf16[640,2048]{1,0:T(8,128)(2,1)}, bf16[640,2048]{1,0:T(8,128)(2,1)}) custom-call(s32[4]{0:T(128)} %pad_add_fusion.order_ref, bf16[2560,1536]{1,0:T(8,128)(2,1)} %attend_back.1.g_ref.x_ref, bf16[2048,1536]{1,0:T(8,128)(2,1)} %get-tuple-element.79.w_ref), custom_call_target="tpu_custom_call" | custom-call | flops 16106127360 | bytes 24641536 | tf_op jit(solution)/shard_map/project_back/pallas_call | solution.py:389
  815.1 91.1 %closing_rows.3 = (f32[640,2048]{1,0:T(8,128)}, f32[8,2048]{1,0:T(8,128)}) custom-call(bf16[640,2048]{1,0:T(8,128)(2,1)} %get-tuple-element.128.refs_0_, bf16[640,2048]{1,0:T(8,128)(2,1)} %get-tuple-element.129.refs_1_, bf16[640,2048]{1,0:T(8,128)(2,1)} %get-tuple-element.130.refs_2_, bf16[640,2048]{1,0:T(8,128)(2,1)} %get-tuple-element.131.refs_3_, ...), custom_call_target="tpu_custom_call" | custom-call | tf_op jit(solution)/shard_map/closing_rows/pallas_call | solution.py:1082
  906.2 0.9 slice.47
  907.1 0.8 slice.45
  907.9 0.7 pad_maximum_fusion.vec_ref
  908.6 7.0 fusion
  915.6 97.8 %sum_and_share.1 = (bf16[4,256,2816]{2,1,0:T(8,128)(2,1)}, bf16[4,176,2048]{2,1,0:T(8,128)(2,1)}, bf16[4,64,2048]{2,1,0:T(8,128)(2,1)}, f32[8,256]{1,0:T(8,128)}) custom-call(bf16[512,2048]{1,0:T(8,128)(2,1)} %convolution_convert_fusion.part_ref, f32[8,2048]{1,0:T(8,128)} %pad_maximum_fusion.vec_ref, ...), custom_call_target="tpu_custom_call" | custom-call | tf_op jit(solution)/shard_map/sum_and_share/pallas_call | solution.py:1267
  1013.4 8.8 whole_columns.1
  1022.2 1.6 bitcast_convert_fusion.1
  1023.9 23.5 %share_pieces.1.in_ref = bf16[4,256,1536]{2,1,0:T(8,128)(2,1)} custom-call(bf16[256,1536]{1,0:T(8,128)(2,1)} %reduce-scatter.4.cloned.1.call-done.refs_0_), custom_call_target="tpu_custom_call" | custom-call | tf_op jit(solution)/shard_map/share_pieces/pallas_call | solution.py:1159
  1047.4 5.6 whole_heads.1
  1053.1 3.5 bitcast_convert_fusion
  1056.6 0.6 fusion.12
  1057.2 2.7 copy.24
  1059.8 1.0 copy-done.1
  (68 shorter events, 1.8 us)
Async XLA Ops:
  7.2 111.2 %copy-start = (bf16[704,2048]{1,0:T(8,128)(2,1)S(1)}, bf16[704,2048]{1,0:T(8,128)(2,1)}, u32[]{:S(2)}) copy-start(bf16[704,2048]{1,0:T(8,128)(2,1)} %param.18) | copy-start | bytes 8650756
  7.2 374.3 %all-gather.5.cloned.1.call-start = ((), (), s32[]{:S(2)}) async-start(), calls=%async_computation.4 | async-start | bytes 6488064 | tf_op jit(solution)/shard_map/all_gather | solution.py:1420
  119.3 4.8 copy-start.3
  119.4 8.2 copy-start.12
  119.4 8.5 copy-start.6
  119.4 262.1 %all-gather.3.cloned.1.call-start = ((), (), s32[]{:S(2)}) async-start(), calls=%async_computation.3 | async-start | bytes 12976128 | tf_op jit(solution)/shard_map/all_gather | solution.py:1420
  124.0 791.5 %reduce-scatter.8.cloned.1.call-start = ((), (), s32[]{:S(2)}) async-start(), calls=%async_computation.7 | async-start | bytes 6488064 | tf_op jit(solution)/shard_map/reduce_scatter | solution.py:1424
  124.1 111.0 %collective-permute-start = (bf16[640,2048]{1,0:T(8,128)(2,1)S(1)}, bf16[640,2048]{1,0:T(8,128)(2,1)}, u32[]{:S(2)}, u32[]{:S(2)}) collective-permute-start(bf16[640,2048]{1,0:T(8,128)(2,1)S(1)} %bitcast.45), channel_id=1, source_target_pairs={{0,8},{8,0},{16,24},{24,16},{1,9},{9,1},{17,25},{25,17},{2,10},{10... | collective-permute-start | bytes 7864328 | tf_op jit(solution)/shard_map/ppermute | solution.py:632
  126.3 107.2 %collective-permute-start.1 = (bf16[640,2048]{1,0:T(8,128)(2,1)S(1)}, bf16[640,2048]{1,0:T(8,128)(2,1)}, u32[]{:S(2)}, u32[]{:S(2)}) collective-permute-start(bf16[640,2048]{1,0:T(8,128)(2,1)S(1)} %bitcast.46), channel_id=1, source_target_pairs={{0,16},{8,24},{16,0},{24,8},{1,17},{9,25},{17,1},{25,9},{2,18},{10... | collective-permute-start | bytes 7864328 | tf_op jit(solution)/shard_map/ppermute | solution.py:624
  127.7 36.4 %copy-start.8 = (s32[2]{0:T(128)}, s32[2]{0:T(128)S(1)}, u32[]{:S(2)}) copy-start(s32[2]{0:T(128)S(1)} %fusion.5.ends_ref) | copy-start | bytes 28
  233.5 5.3 collective-permute-start.2
  465.2 5.1 collective-permute-start.3
  473.1 58.4 %collective-permute-start.4 = (bf16[640,2048]{1,0:T(8,128)(2,1)S(1)}, bf16[640,2048]{1,0:T(8,128)(2,1)S(1)}, u32[]{:S(2)}, u32[]{:S(2)}) collective-permute-start(bf16[640,2048]{1,0:T(8,128)(2,1)S(1)} %add_convert_fusion.2), channel_id=1, source_target_pairs={{0,16},{8,24},{16,0},{24,8},{1,17},{9,25},{17,1},{25,9},{2,18},{10... | collective-permute-start | bytes 7864328 | tf_op jit(solution)/shard_map/ppermute | solution.py:624
  531.5 1.5 copy-start.4
  549.9 365.7 %reduce-scatter.6.cloned.1.call-start = ((), (), s32[]{:S(2)}) async-start(), calls=%async_computation.6 | async-start | bytes 12976128 | tf_op jit(solution)/shard_map/reduce_scatter | solution.py:1424
  550.0 65.5 %collective-permute-start.6 = (bf16[640,2048]{1,0:T(8,128)(2,1)}, bf16[640,2048]{1,0:T(8,128)(2,1)}, u32[]{:S(2)}, u32[]{:S(2)}) collective-permute-start(bf16[640,2048]{1,0:T(8,128)(2,1)} %get-tuple-element.119.refs_0_), channel_id=1, source_target_pairs={{0,16},{8,24},{16,0},{24,8},{1,17},{9,25},{17,1},{25,9},{2,18},{10... | collective-permute-start | bytes 7864328 | tf_op jit(solution)/shard_map/ppermute | solution.py:624
  615.5 1.7 copy-start.9
  615.5 408.4 %reduce-scatter.4.cloned.1.call-start = ((), (), s32[]{:S(2)}) async-start(), calls=%async_computation.5 | async-start | bytes 7077888 | tf_op jit(solution)/shard_map/reduce_scatter | solution.py:1424
  617.2 8.6 collective-permute-start.7
  617.2 11.4 %collective-permute-start.9 = (bf16[640,2048]{1,0:T(8,128)(2,1)}, bf16[640,2048]{1,0:T(8,128)(2,1)S(1)}, u32[]{:S(2)}, u32[]{:S(2)}) collective-permute-start(bf16[640,2048]{1,0:T(8,128)(2,1)} %get-tuple-element.119.refs_0_), channel_id=1, source_target_pairs={{0,8},{8,0},{16,24},{24,16},{1,9},{9,1},{17,25},{25,17},{2,10},{10... | collective-permute-start | bytes 7864328 | tf_op jit(solution)/shard_map/ppermute | solution.py:632
  617.7 12.1 %collective-permute-start.10 = (bf16[640,2048]{1,0:T(8,128)(2,1)}, bf16[640,2048]{1,0:T(8,128)(2,1)S(1)}, u32[]{:S(2)}, u32[]{:S(2)}) collective-permute-start(bf16[640,2048]{1,0:T(8,128)(2,1)} %collective-permute-done.6.refs_2_), channel_id=1, source_target_pairs={{0,8},{8,0},{16,24},{24,16},{1,9},{9,1},{17,25},{25,17},{2,10},{10... | collective-permute-start | bytes 7864328 | tf_op jit(solution)/shard_map/ppermute | solution.py:632
  628.6 1.5 copy-start.10
  630.1 1.5 copy-start.11
  787.5 121.1 %collective-permute-start.5 = (bf16[640,2048]{1,0:T(8,128)(2,1)}, bf16[640,2048]{1,0:T(8,128)(2,1)}, u32[]{:S(2)}, u32[]{:S(2)}) collective-permute-start(bf16[640,2048]{1,0:T(8,128)(2,1)} %get-tuple-element.112), channel_id=1, source_target_pairs={{0,8},{8,0},{16,24},{24,16},{1,9},{9,1},{17,25},{25,17},{2,10},{10... | collective-permute-start | bytes 7864328 | tf_op jit(solution)/shard_map/ppermute | solution.py:632
  787.8 120.7 %collective-permute-start.8 = (bf16[640,2048]{1,0:T(8,128)(2,1)S(1)}, bf16[640,2048]{1,0:T(8,128)(2,1)}, u32[]{:S(2)}, u32[]{:S(2)}) collective-permute-start(bf16[640,2048]{1,0:T(8,128)(2,1)S(1)} %add_convert_fusion.1), channel_id=1, source_target_pairs={{0,16},{8,24},{16,0},{24,8},{1,17},{9,25},{17,1},{25,9},{2,18},{10... | collective-permute-start | bytes 7864328 | tf_op jit(solution)/shard_map/ppermute | solution.py:624
  815.1 93.5 %slice-start = ((s8[5242880]{0:T(1024)(128)(4,1)}), s8[4194304]{0:T(1024)(128)(4,1)S(1)}, s32[]{:S(2)}) async-start(s8[5242880]{0:T(1024)(128)(4,1)} %bitcast.38), calls=%async_computation.8 | async-start | bytes 8388608
  815.1 93.5 %slice-start.1 = ((s8[5242880]{0:T(1024)(128)(4,1)}), s8[1048576]{0:T(1024)(128)(4,1)S(1)}, s32[]{:S(2)}) async-start(s8[5242880]{0:T(1024)(128)(4,1)} %bitcast.38), calls=%async_computation.9 | async-start | bytes 2097152
  1013.4 8.9 copy-start.5
  1023.9 33.3 %slice-start.2 = ((s8[5242880]{0:T(1024)(128)(4,1)}), s8[4194304]{0:T(1024)(128)(4,1)S(1)}, s32[]{:S(2)}) async-start(s8[5242880]{0:T(1024)(128)(4,1)} %bitcast.40), calls=%async_computation.10 | async-start | bytes 8388608
  1047.4 5.6 copy-start.2
  1047.4 9.7 slice-start.3
  1053.1 3.5 copy-start.7
  1057.2 3.7 copy-start.1
Sparse Core Ops, SparseCore 0:
  119.5 91.3 all-gather.4
  213.6 161.8 all-gather.2
  550.0 108.7 reduce-scatter.7
  662.3 190.9 reduce-scatter.5
  857.3 147.4 reduce-scatter.3

commit v3 on v2

--- a/solution.py
+++ b/solution.py
@@ -282,27 +282,30 @@
     dk_ref[...] = jnp.zeros_like(dk_ref)
     dv_ref[...] = jnp.zeros_like(dv_ref)
 
-    def step(start, masked):
-        here = pl.ds(start, BLOCK)
+    def step(start, masked, keys=(0, BLOCK), size=BLOCK):
+        here = pl.ds(start, size)
+        first, end = keys
         if masked:
-            row = lax.broadcasted_iota(jnp.int32, (1, BLOCK), 1) + start
-            col = lax.broadcasted_iota(jnp.int32, (BLOCK, 1), 0) + start
+            row = lax.broadcasted_iota(jnp.int32, (1, size), 1) + start
+            col = lax.broadcasted_iota(jnp.int32, (end - first, 1), 0) + number * BLOCK + first
             visible = (col <= row) & (segment_of(row, ends_ref) == segment_of(col, ends_ref))
         total = None
         for h in range(2):
             qx = qx_ref[h, here, :]
             gx = gx_ref[h, here, :]
-            chances = jnp.exp(dot_last(k_one[h], qx))
+            chances = jnp.exp(dot_last(k_one[h][first:end], qx))
             if masked:
                 chances = jnp.where(visible, chances, 0.0)
-            dv_ref[h] += dot(chances.astype(BF16), gx)
-            grad_scores = (chances * dot_last(v_one[h], gx)).astype(BF16)
-            dk_ref[h] += dot(grad_scores, qx)
-            part = dot(k_turned[h], grad_scores)
+            dv_ref[h, first:end] += dot(chances.astype(BF16), gx)
+            grad_scores = (chances * dot_last(v_one[h][first:end], gx)).astype(BF16)
+            dk_ref[h, first:end] += dot(grad_scores, qx)
+            part = dot(k_turned[h][:, first:end], grad_scores)
             total = part if total is None else total + part
         dq_ref[:, here] += total
 
-    step(pl.multiple_of(number * BLOCK, BLOCK), True)
+    half = BLOCK // 2
+    step(pl.multiple_of(number * BLOCK, BLOCK), True, (0, half))
+    step(pl.multiple_of(number * BLOCK + half, half), True, (half, BLOCK), half)
 
     @pl.loop(number + 1, blocks)
     def _(j):
@@ -520,19 +523,20 @@
     )(normed, *upstream, w_gate_up, w_down)
 
 
-def near_and_down(grads, w_gate_up, product, upstream, rows):
-    columns = grads.shape[1]
-    total, units = product.shape
-    width = upstream.shape[1]
+def near_and_grad(x, weight, order, left, right, rows, name):
+    columns = x.shape[1]
+    total, height = left.shape
+    width = weight.shape[0]
+    breadth = right.shape[1]
     half = rows // 2
-    tile = 512
-
-    def kernel(g_ref, w_ref, p_ref, up_ref, own_ref, other_ref, out_ref):
+    tile = 512 if breadth % 512 == 0 else 256
+
+    def kernel(order_ref, x_ref, w_ref, left_ref, right_ref, own_ref, other_ref, out_ref):
         step = pl.program_id(0)
 
         @pl.when(step < 4)
         def _():
-            made = dot_last(g_ref[...], w_ref[...]).astype(BF16)
+            made = dot_last(x_ref[...], w_ref[...]).astype(BF16)
 
             @pl.when(step < 2)
             def _():
@@ -544,34 +548,41 @@
 
         @pl.when(step >= 4)
         def _():
-            out_ref[...] = dot_first(p_ref[...], up_ref[...]).astype(BF16)
+            out_ref[...] = dot_first(left_ref[...], right_ref[...]).astype(BF16)
 
     def late(i):
         return jnp.maximum(i - 4, 0)
 
+    def near(i, o):
+        step = jnp.minimum(i, 3)
+        return (o[step // 2] * 2 + step % 2, 0)
+
     return pl.pallas_call(
         kernel,
-        grid=(4 + width // tile,),
-        in_specs=[
-            pl.BlockSpec((half, columns), lambda i: (jnp.minimum(i, 3), 0)),
-            pl.BlockSpec(w_gate_up.shape, lambda i: (0, 0), pipeline_mode=pl.Buffered(1)),
-            pl.BlockSpec(product.shape, lambda i: (0, 0), pipeline_mode=pl.Buffered(1)),
-            pl.BlockSpec((total, tile), lambda i: (0, late(i))),
-        ],
-        out_specs=[
-            pl.BlockSpec((half, width), lambda i: (jnp.minimum(i, 1), 0)),
-            pl.BlockSpec((half, width), lambda i: (jnp.clip(i - 2, 0, 1), 0)),
-            pl.BlockSpec((units, tile), lambda i: (0, late(i))),
-        ],
+        grid_spec=pltpu.PrefetchScalarGridSpec(
+            num_scalar_prefetch=1,
+            grid=(4 + breadth // tile,),
+            in_specs=[
+                pl.BlockSpec((half, columns), near),
+                pl.BlockSpec(weight.shape, lambda i, o: (0, 0), pipeline_mode=pl.Buffered(1)),
+                pl.BlockSpec(left.shape, lambda i, o: (0, 0), pipeline_mode=pl.Buffered(1)),
+                pl.BlockSpec((total, tile), lambda i, o: (0, late(i))),
+            ],
+            out_specs=[
+                pl.BlockSpec((half, width), lambda i, o: (jnp.minimum(i, 1), 0)),
+                pl.BlockSpec((half, width), lambda i, o: (jnp.clip(i - 2, 0, 1), 0)),
+                pl.BlockSpec((height, tile), lambda i, o: (0, late(i))),
+            ],
+        ),
         out_shape=[
             jax.ShapeDtypeStruct((rows, width), BF16),
             jax.ShapeDtypeStruct((rows, width), BF16),
-            jax.ShapeDtypeStruct((units, width), BF16),
+            jax.ShapeDtypeStruct((height, breadth), BF16),
         ],
         compiler_params=params(),
         cost_estimate=cost(total + rows, width, columns),
-        name="near_and_down",
-    )(grads, w_gate_up, product, upstream)
+        name=name,
+    )(order, x, weight, left, right)
 
 
 def blocks_matmul(blocks, weight, order):
@@ -784,7 +795,7 @@
     ] * 2
 
 
-def opening(tokens, in_part, out_slice, vectors, seq_size, fsdp_size):
+def opening(tokens, in_part, vectors, seq_size, fsdp_size):
     rows, width = tokens.shape
     chips = seq_size // CORES
     deep = planes(fsdp_size)
@@ -792,7 +803,7 @@
     dma = pltpu.SemaphoreType.DMA
 
     def kernel(
-        tok_ref, in_ref, out_ref, vec_ref, tok_all, w_in, w_out, vec_all,
+        tok_ref, in_ref, vec_ref, tok_all, w_in, vec_all,
         here, x_send, x_recv, c_send, c_recv, v_send, v_recv, *sems,
     ):
         p = Place(seq_size, fsdp_size)
@@ -818,13 +829,11 @@
                 fsdp=(p.fsdp + k) % fsdp_size,
             )
 
-        into = FsdpGather(p, in_ref, w_in, sems[:4])
-        outof = FsdpGather(p, out_ref, w_out, sems[4:])
+        into = FsdpGather(p, in_ref, w_in, sems)
         own = [
             pltpu.make_async_copy(tok_ref, tok_slot(p.seq), here.at[0]),
             pltpu.make_async_copy(in_ref, into.slot(p.fsdp), here.at[1]),
             pltpu.make_async_copy(vec_ref, vec_all.at[p.fsdp], here.at[2]),
-            pltpu.make_async_copy(out_ref, outof.slot(p.fsdp), here.at[3]),
         ]
         for k in range(1, fsdp_size):
             vec(k).start()
@@ -834,18 +843,12 @@
         tok_core(0).start()
         for copy in own:
             copy.start()
-        into.pass_on(1)
-        outof.start()
-        for d in range(2, deep):
+        for d in range(1, deep):
             into.pass_on(d)
-            outof.pass_on(d - 1)
-        for d in range(max(deep - 1, 1), deep):
-            outof.pass_on(d)
         for k in range(1, chips):
             tok_x(k).wait_recv()
             tok_core(k).start()
         into.finish()
-        outof.finish()
         for k in range(chips):
             tok_core(k).wait()
         for k in range(1, chips):
@@ -858,22 +861,21 @@
     any_space = pl.BlockSpec(memory_space=pl.ANY)
     return pl.pallas_call(
         kernel,
-        in_specs=[pl.BlockSpec(memory_space=pltpu.VMEM)] * 4,
-        out_specs=[any_space] * 4,
+        in_specs=[pl.BlockSpec(memory_space=pltpu.VMEM)] * 3,
+        out_specs=[any_space] * 3,
         out_shape=[
             jax.ShapeDtypeStruct((rows * seq_size, width), BF16),
             jax.ShapeDtypeStruct((in_part.shape[0] * fsdp_size, in_part.shape[1]), BF16),
-            jax.ShapeDtypeStruct((out_slice.shape[0] * fsdp_size, width), BF16),
             jax.ShapeDtypeStruct((fsdp_size,) + vectors.shape, F32),
         ],
         scratch_shapes=[
-            dma((4,)), dma((chips,)), dma((chips,)), dma((chips,)), dma((chips,)),
+            dma((3,)), dma((chips,)), dma((chips,)), dma((chips,)), dma((chips,)),
             dma((fsdp_size,)), dma((fsdp_size,)),
         ]
-        + fsdp_sems(deep, across) * 2,
+        + fsdp_sems(deep, across),
         compiler_params=talking(1),
         name="opening",
-    )(tokens, in_part, out_slice, vectors)
+    )(tokens, in_part, vectors)
 
 
 def talking(collective_id):
@@ -885,22 +887,25 @@
 CHUNKS = 4
 
 
-def hidden_rows(parts, residual, gain, bias, seq_size, fsdp_size):
+def hidden_rows(parts, residual, gain, bias, down_slice, seq_size, fsdp_size):
     rows, width = residual.shape
     chips = seq_size // CORES
+    deep = planes(fsdp_size)
     part = rows // CHUNKS
     dma = pltpu.SemaphoreType.DMA
 
     def kernel(*refs):
         own = refs[0 : 2 * chips : 2]
         other = refs[1 : 2 * chips : 2]
-        res_ref, gain_ref, bias_ref, hidden_ref, normed_ref = refs[2 * chips : 2 * chips + 5]
+        refs = refs[2 * chips :]
+        res_ref, gain_ref, bias_ref, down_ref, hidden_ref, normed_ref, w_down = refs[:7]
         (
             from_core, total, from_x, mine,
             c_send, c_recv, x_send, x_recv, g_send, g_recv, f_send, f_recv, here,
-        ) = refs[2 * chips + 5 :]
+        ) = refs[7:20]
         p = Place(seq_size, fsdp_size)
-        greet(p, False)
+        greet(p, True)
+        down = FsdpGather(p, down_ref, w_down, refs[20:])
 
         def span(c):
             return pl.ds(c * part, part)
@@ -940,6 +945,9 @@
                 both = own[k][span(c)].astype(F32) + from_core[k, span(c)].astype(F32)
                 total[k - 1, span(c)] = both.astype(BF16)
                 along(k, c).start()
+        down.start()
+        down_here = pltpu.make_async_copy(down_ref, down.slot(p.fsdp), here.at[1])
+        down_here.start()
         for c in range(CHUNKS):
             to_core(0, c).wait_recv()
             rows_here = own[0][span(c)].astype(F32) + from_core[0, span(c)].astype(F32)
@@ -954,8 +962,12 @@
             for k in far:
                 share(k, c).start()
             pass_on(0, c).start()
-        keep = pltpu.make_async_copy(mine, normed_ref.at[0], here)
+            if c + 1 < deep:
+                down.pass_on(c + 1)
+        keep = pltpu.make_async_copy(mine, normed_ref.at[0], here.at[0])
         keep.start()
+        for d in range(CHUNKS + 1, deep):
+            down.pass_on(d)
         for c in range(CHUNKS):
             for k in far:
                 share(k, c).wait_recv()
@@ -968,17 +980,21 @@
                 along(k, c).wait_send()
                 share(k, c).wait_send()
         keep.wait()
+        down.finish()
+        down_here.wait()
 
     vmem = pl.BlockSpec(memory_space=pltpu.VMEM)
+    any_space = pl.BlockSpec(memory_space=pl.ANY)
     block = (rows, width)
     several = (max(chips - 1, 1),) + block
     return pl.pallas_call(
         kernel,
-        in_specs=[vmem] * (2 * chips + 3),
-        out_specs=[vmem, pl.BlockSpec(memory_space=pl.ANY)],
+        in_specs=[vmem] * (2 * chips + 4),
+        out_specs=[vmem, any_space, any_space],
         out_shape=[
             jax.ShapeDtypeStruct(block, F32),
             jax.ShapeDtypeStruct((2 * chips,) + block, BF16),
+            jax.ShapeDtypeStruct((down_slice.shape[0] * fsdp_size, width), BF16),
         ],
         scratch_shapes=[
             pltpu.VMEM((chips,) + block, BF16),
@@ -987,7 +1003,8 @@
             pltpu.VMEM(block, BF16),
         ]
         + [dma((chips, CHUNKS))] * 8
-        + [dma],
+        + [dma((2,))]
+        + fsdp_sems(deep, fsdp_size // deep),
         compiler_params=talking(2),
         name="hidden_rows",
     )(
@@ -995,6 +1012,7 @@
         residual,
         jnp.broadcast_to(gain[None], (8, width)),
         jnp.broadcast_to(bias[None], (8, width)),
+        down_slice,
     )
 
 
@@ -1457,23 +1475,25 @@
     else:
         in_part = own_heads(project_in, me, own_pairs)
     vectors = jnp.stack([first_gain, first_bias, second_gain, second_bias]).astype(F32)
-    all_tokens, w_in, w_out, vectors = opening(
+    all_tokens, w_in, vectors = opening(
         tokens[0],
         in_part,
-        lax.dynamic_slice_in_dim(project_out, me * pieces_out, pieces_out, 0),
         jnp.concatenate([vectors, vectors]),
         seq_size,
         fsdp_size,
     )
-    if not spread:
+    gate_late, up_late, out_late = tie((gate_weight, up_weight, project_out), w_in)
+    if spread:
+        w_out = gather_fsdp(lax.dynamic_slice_in_dim(out_late, me * pieces_out, pieces_out, 0))
+    else:
         own_rows = width // seq_size
         w_out = lax.dynamic_slice_in_dim(gather_fsdp(project_out), me * own_rows, own_rows, 0)
     vectors = jnp.transpose(vectors[:, :4], (1, 0, 2)).reshape(4, width)
     gain_one, bias_one, gain_two, bias_two = [vectors[i] for i in range(4)]
     upstream_own = tie(grad_output[0], all_tokens)
     upstream_far = [from_chip(upstream_own, chips, ahead) for ahead in far]
-    gate_late, up_late, down_late = tie((gate_weight, up_weight, down_weight), w_in)
-    w_down = gather_fsdp(lax.dynamic_slice_in_dim(down_late, me * pieces_down, pieces_down, 0))
+    down_slice = lax.dynamic_slice_in_dim(down_weight, me * pieces_down, pieces_down, 0)
+    whole_tiles = pieces_down % 16 == 0
     w_gate_up = gather_fsdp(own_columns(gate_late, up_late, me, seq_size, fsdp_size))
 
     cosine, sine, ends = rope_tables(cont_lengths[0], total_rows)
@@ -1494,19 +1514,30 @@
 
     attended = tie(attended, upstream_blocks)
     parts = chip_matmul(attended, w_out, order, rows_dev, False, "attention_out")
-    hidden, normed_blocks = hidden_rows(parts, tokens[0], gain_two, bias_two, seq_size, fsdp_size)
+    hidden, normed_blocks, w_down = hidden_rows(
+        parts, tokens[0], gain_two, bias_two,
+        down_slice if whole_tiles else down_slice[: pieces_down // 16 * 16],
+        seq_size, fsdp_size,
+    )
+    if not whole_tiles:
+        w_down = gather_fsdp(down_slice)
     product, grads, normed_second, upstream_all = feed(
         normed_blocks, upstream_blocks, w_gate_up, w_down
     )
 
-    far_order = jnp.arange(CORES, chips * CORES, dtype=jnp.int32)
-    sent = [
-        (own.astype(F32) + core_swap(other, chips).astype(F32)).astype(BF16)
-        for own, other in chip_matmul(grads, w_gate_up, far_order, rows_dev, True, "feed_back")
-    ]
-    arriving = [to_chip(value, chips, ahead) for value, ahead in zip(sent, far)]
-    own, other, grad_down = near_and_down(
-        tie(grads, *sent), w_gate_up, product, upstream_all, rows_dev
+    near_order = jnp.arange(chips * CORES, dtype=jnp.int32)
+
+    def send_far(x, weight, x_order, name):
+        sent = [
+            (own.astype(F32) + core_swap(other, chips).astype(F32)).astype(BF16)
+            for own, other in chip_matmul(x, weight, x_order[CORES:], rows_dev, True, name)
+        ]
+        return sent, [to_chip(value, chips, ahead) for value, ahead in zip(sent, far)]
+
+    sent, arriving = send_far(grads, w_gate_up, near_order, "feed_back")
+    own, other, grad_down = near_and_grad(
+        tie(grads, *sent), w_gate_up, near_order[:CORES], product, upstream_all, rows_dev,
+        "near_and_down",
     )
     grad_hidden, low_own, sums_two = closing_rows(
         [(own, other)], tie(arriving, grad_down), hidden, grad_output[0], gain_two,
@@ -1519,12 +1550,11 @@
     grad_gate_up = weight_grad(normed_late, grads, "grad_gate_up")
     product_late = tie(product_late, grad_gate_up)
 
-    near_order = jnp.arange(chips * CORES, dtype=jnp.int32)
     layer_parts = chip_matmul(product_late, w_down, near_order, rows_dev, False, "feed_down")
     (layer_own, layer_other), layer_far = layer_parts[0], layer_parts[1:]
     low_far = tie(low_far, layer_own)
     layer_far = tie(layer_far, low_far)
-    grad_down_piece = scatter_fsdp(tie(grad_down, low_own))
+    grad_down_piece = scatter_fsdp(tie(grad_down, arriving))
     grad_gate_up_piece = scatter_fsdp(tie(grad_gate_up, low_far))
     low_blocks = low_near
     for block in low_far:
@@ -1539,12 +1569,17 @@
     grad_attended = tie(grad_attended, grad_out)
 
     grad_qkv = attend_back(ends, qkv, qx, grad_attended, attended, cosine, sine)
-    grad_in = weight_grad(normed_first, grad_qkv, "grad_project_in")
-    grad_in_piece = scatter_fsdp(grad_in)
-    grad_late = tie(grad_qkv, grad_in)
-    parts = chip_matmul(grad_late, w_in, order, rows_dev, True, "project_back")
+    grad_qkv = tie(grad_qkv, layer_arriving)
+    sent, arriving = send_far(grad_qkv, w_in, order, "project_back")
+    grad_late = tie(grad_qkv, *sent)
+    own, other, grad_in = near_and_grad(
+        grad_late, w_in, order[:CORES], normed_first, grad_late, rows_dev, "near_and_project_in"
+    )
+    arriving = tie(arriving, grad_in)
+    grad_in_piece = scatter_fsdp(tie(grad_in, arriving))
     input_gradient, sums_one = closing_rows(
-        parts, [], tokens[0], grad_hidden, gain_one, seq_size, fsdp_size, False, 4
+        [(own, other)], arriving, tokens[0], grad_hidden, gain_one,
+        seq_size, fsdp_size, False, 4,
     )
     layer_rows = hidden + scatter_end(
         (layer_arriving, layer_own, core_swap(layer_other, chips), None)

time: 1080 us -> 1020 us (0.944)
  Pallas kernels: 955 us -> 862 us
  waiting for transfers between devices: 33.7 us -> 62.7 us
    pallas_call x2, Pallas kernels: 108 us -> 34.8 us  [closing_rows(): pl.pallas_call(kernel, in_specs=[vmem] * len(operands), out_specs=[vmem]...]
    pallas_call x2 -> x3, Pallas kernels: 170 us -> 222 us  [the longest x1 141 us: hidden_rows(): pl.pallas_call(kernel, in_specs=[vmem] * (2 * chips + 4), out_specs=[vmem...]
    pallas_call x1, Pallas kernels: 98.5 us -> 75.7 us  [opening(): pl.pallas_call(kernel, in_specs=[pl.BlockSpec(memory_space=pltpu.VMEM)] *...]
    pallas_call x2 -> x1, Pallas kernels: 60.9 us -> 38.3 us  [weight_grad(): pl.pallas_call(kernel, grid=(height // tile, columns // part), in_specs=[...]
    ppermute x4 -> x5, waiting for transfers between devices: 15.6 us -> 32.2 us  [from_chip(): lax.ppermute(value, 'seq', [(i, (i - ahead * CORES) % size) for i in rang...]
    ppermute x7 -> x8, waiting for transfers between devices: 18 us -> 24.9 us  [core_swap(): lax.ppermute(value, 'seq', [(i, i ^ 1) for i in range(chips * CORES)])]
  transfers between devices with their start and end apart: 16 -> 18, of which waited for: 5 -> 10; matrix products, arithmetic and copies ran while one was open for 3% -> 4% of each run, Pallas kernels for 67% -> 66%
where the time goes in v3:
time: 1020 us; the launch traced here: 1010 us
  Pallas kernels  862 us (85%)
  waiting for transfers between devices  62.7 us (6%)
  other arithmetic  28.2 us (3%)
  local copies, waits for them, and re-layouts  22.4 us (2%)
  between operations  14.5 us (1%)
  starting transfers between devices  13 us (1%)
    pallas_call x1, Pallas kernels, hidden_rows(): pl.pallas_call(kernel, in_specs=[vmem] * (2 * chips + 4), out_specs=[vmem...  141 us
    pallas_call x1, Pallas kernels, attend_back(): pl.pallas_call(attend_back_kernel, grid_spec=pltpu.PrefetchScalarGridSpec...  107 us
    pallas_call x1, Pallas kernels, sum_and_share(): pl.pallas_call(kernel, in_specs=[vmem] * (count + 1), out_specs=[pl.Block...  90.8 us
    pallas_call x2, Pallas kernels, near_and_grad(): pl.pallas_call(kernel, grid_spec=pltpu.PrefetchScalarGridSpec(num_scalar_...  80.4 us
    pallas_call x4, Pallas kernels, chip_matmul(): pl.pallas_call(kernel, grid_spec=pltpu.PrefetchScalarGridSpec(num_scalar_...  78 us
    pallas_call x1, Pallas kernels, opening(): pl.pallas_call(kernel, in_specs=[pl.BlockSpec(memory_space=pltpu.VMEM)] *...  75.7 us
    pallas_call x1, Pallas kernels, attend(): pl.pallas_call(attend_kernel, grid_spec=pltpu.PrefetchScalarGridSpec(num_...  60.9 us
    pallas_call x1, Pallas kernels, feed(): pl.pallas_call(kernel, grid=(2 * count,), in_specs=[pl.BlockSpec((1, half...  60 us
  transfers between devices with their start and end apart: 18, of which 10 were waited for; matrix products, arithmetic and copies ran while one was open for 4% of the time, Pallas kernels for 66%

profile of v3, /device:TPU:9, one launch (start us, length us, event | category | flops | bytes accessed | tf_op | source)
XLA Modules:
  0.0 1012.9 jit_solution(8306129785653433314)
XLA Ops:
  7.2 0.8 stack.37
  8.1 0.7 stack.38
  8.7 0.7 stack.39
  9.4 0.7 stack.40
  10.7 7.5 own_heads.1.in_ref
  18.2 75.7 %opening.1 = (bf16[2560,2048]{1,0:T(8,128)(2,1)}, bf16[2048,1536]{1,0:T(8,128)(2,1)}, f32[8,8,256]{2,1,0:T(8,128)}) custom-call(bf16[640,2048]{1,0:T(8,128)(2,1)} %bitcast.36, bf16[256,1536]{1,0:T(8,128)(2,1)} %own_heads.1.in_ref, f32[8,256]{1,0:T(8,128)} %concatenate.12.vec_ref), custom_call_target="tpu_custom_call" | custom-call | tf_op jit(solution)/shard_map/opening/pallas_call | solution.py:862
  93.9 1.7 constant_dynamic-slice_fusion.1
  95.7 4.4 own_columns.1
  100.2 2.2 collective-permute-start
  102.4 1.3 collective-permute-start.1
  104.0 6.3 fusion.3
  111.6 28.6 %project_in_rope.1 = (bf16[2560,1536]{1,0:T(8,128)(2,1)}, bf16[2560,2048]{1,0:T(8,128)(2,1)}) custom-call(bf16[2560,2048]{1,0:T(8,128)(2,1)} %get-tuple-element.82.x_ref, bf16[2048,1536]{1,0:T(8,128)(2,1)} %get-tuple-element.83.w_ref, f32[8,2048]{1,0:T(8,128)} %broadcast_in_dim.112.gain_ref.refs_5_, f32[8,2048]{1,0:T(8,128)} %broadcast_in_dim.114.bias_ref, ...), custom_call_target="tpu_custom_call" | custom-call | flops 16106127360 | bytes 24641536 | tf_op jit(solution)/shard_map/project_in_rope/pallas_call | solution.py:104
  140.2 60.9 %attend.1 = (bf16[2560,512]{1,0:T(8,128)(2,1)}, bf16[8,2560,128]{2,1,0:T(8,128)(2,1)}) custom-call(s32[2]{0:T(128)} %copy-done.11, bf16[2560,1536]{1,0:T(8,128)(2,1)} %get-tuple-element.85.refs_0_.refs_1_.refs_2_.refs_3_.refs_4_.refs_5_.k_ref.v_ref, bf16[2560,1536]{1,0:T(8,128)(2,1)} %get-tuple-element.85.refs_0_.refs_1_.refs_2_.refs_3_.refs_4_.refs_5_.k_ref.v_ref, ...), custom_call_target="tpu_custom_call" | custom-call | flops 26843545600 | bytes 7864320 | tf_op jit(solution)/shard_map/attend/pallas_call | solution.py:218
  201.6 0.6 slice.56.order_ref
  202.9 0.9 constant_dynamic-slice_fusion.refs_7_
  203.8 2.7 collective-permute-done.2.refs_3_
  206.5 13.7 %attention_out.1 = (bf16[640,2048]{1,0:T(8,128)(2,1)}, bf16[640,2048]{1,0:T(8,128)(2,1)}, bf16[640,2048]{1,0:T(8,128)(2,1)}, bf16[640,2048]{1,0:T(8,128)(2,1)}) custom-call(s32[4]{0:T(128)} %pad_add_fusion.order_ref, bf16[2560,512]{1,0:T(8,128)(2,1)} %get-tuple-element.89.x_ref.o_ref, bf16[512,2048]{1,0:T(8,128)(2,1)} %all-gather.3.cloned.1.call-done.w_ref.refs_4_), custom_call_target="tpu_custom_call" | custom-call | flops 5368709120 | bytes 15204352 | tf_op jit(solution)/shard_map/attention_out/pallas_call | solution.py:392
  220.2 0.6 broadcast_in_dim.122.refs_5_
  221.5 141.2 %hidden_rows.1 = (f32[640,2048]{1,0:T(8,128)}, bf16[4,640,2048]{2,1,0:T(8,128)(2,1)}, bf16[1408,2048]{1,0:T(8,128)(2,1)}) custom-call(bf16[640,2048]{1,0:T(8,128)(2,1)} %get-tuple-element.91.refs_0_, bf16[640,2048]{1,0:T(8,128)(2,1)} %get-tuple-element.92.refs_1_, bf16[640,2048]{1,0:T(8,128)(2,1)} %get-tuple-element.93.refs_2_, ...), custom_call_target="tpu_custom_call" | custom-call | tf_op jit(solution)/shard_map/hidden_rows/pallas_call | solution.py:990
  362.8 60.0 %feed.1 = (bf16[2560,1408]{1,0:T(8,128)(2,1)}, bf16[2560,2816]{1,0:T(8,128)(2,1)}, bf16[2560,2048]{1,0:T(8,128)(2,1)}, bf16[2560,2048]{1,0:T(8,128)(2,1)}) custom-call(bf16[4,640,2048]{2,1,0:T(8,128)(2,1)} %get-tuple-element.96.x_ref, bf16[640,2048]{1,0:T(8,128)(2,1)} %bitcast.44, bf16[640,2048]{1,0:T(8,128)(2,1)} %collective-permute-done.refs_1_, ...), custom_call_target="tpu_custom_call" | custom-call | flops 44291850240 | bytes 55967744 | tf_op jit(solution)/shard_map/feed/pallas_call | solution.py:499
  422.8 23.7 %feed_back.1 = (bf16[640,2048]{1,0:T(8,128)(2,1)}, bf16[640,2048]{1,0:T(8,128)(2,1)}) custom-call(s32[2]{0:T(128)} %slice.56.order_ref, bf16[2560,2816]{1,0:T(8,128)(2,1)} %get-tuple-element.105.x_ref.g_ref, bf16[2048,2816]{1,0:T(8,128)(2,1)} %all-gather.5.cloned.1.call-done.refs_4_.w_ref), custom_call_target="tpu_custom_call" | custom-call | flops 14763950080 | bytes 23986176 | tf_op jit(solution)/shard_map/feed_back/pallas_call | solution.py:392
  447.0 4.7 collective-permute-done.3
  451.7 2.8 add_convert_fusion.3
  454.5 2.3 collective-permute-start.4
  457.3 43.0 %near_and_down.1 = (bf16[640,2048]{1,0:T(8,128)(2,1)}, bf16[640,2048]{1,0:T(8,128)(2,1)}, bf16[1408,2048]{1,0:T(8,128)(2,1)}) custom-call(s32[2]{0:T(128)} %bitcast.55, bf16[2560,2816]{1,0:T(8,128)(2,1)} %get-tuple-element.105.x_ref.g_ref, bf16[2048,2816]{1,0:T(8,128)(2,1)} %all-gather.5.cloned.1.call-done.refs_4_.w_ref, ...), custom_call_target="tpu_custom_call" | custom-call | flops 36909875200 | bytes 42663936 | tf_op jit(solution)/shard_map/near_and_down/pallas_call | solution.py:560
  500.3 13.4 %collective-permute-done.4.refs_2_ = bf16[640,2048]{1,0:T(8,128)(2,1)S(1)} collective-permute-done((bf16[640,2048]{1,0:T(8,128)(2,1)S(1)}, bf16[640,2048]{1,0:T(8,128)(2,1)S(1)}, u32[]{:S(2)}, u32[]{:S(2)}) %collective-permute-start.4) | collective-permute-done | bytes 2621472 | tf_op jit(solution)/shard_map/ppermute | solution.py:635
  513.7 1.5 copy-done.7
  515.7 18.1 %closing_rows.2 = (f32[640,2048]{1,0:T(8,128)}, bf16[640,2048]{1,0:T(8,128)(2,1)}, f32[8,2048]{1,0:T(8,128)}) custom-call(bf16[640,2048]{1,0:T(8,128)(2,1)} %get-tuple-element.107.refs_0_, bf16[640,2048]{1,0:T(8,128)(2,1)} %get-tuple-element.108.refs_1_, bf16[640,2048]{1,0:T(8,128)(2,1)} %copy-done.7, f32[640,2048]{1,0:T(8,128)} %get-tuple-element.95.refs_3_, ...), custom_call_target="tpu_custom_call" | custom-call | tf_op jit(solution)/shard_map/closing_rows/pallas_call | solution.py:1100
  533.9 38.3 %grad_gate_up.1 = bf16[2048,2816]{1,0:T(8,128)(2,1)} custom-call(bf16[2560,2048]{1,0:T(8,128)(2,1)} %get-tuple-element.113.x_ref, bf16[2560,2816]{1,0:T(8,128)(2,1)} %get-tuple-element.105.x_ref.g_ref), custom_call_target="tpu_custom_call" | custom-call | flops 29527900160 | bytes 36438016 | tf_op jit(solution)/shard_map/grad_gate_up/pallas_call | solution.py:427
  572.7 25.4 %feed_down.1 = (bf16[640,2048]{1,0:T(8,128)(2,1)}, bf16[640,2048]{1,0:T(8,128)(2,1)}, bf16[640,2048]{1,0:T(8,128)(2,1)}, bf16[640,2048]{1,0:T(8,128)(2,1)}) custom-call(s32[4]{0:T(128)} %iota.50.order_ref, bf16[2560,1408]{1,0:T(8,128)(2,1)} %get-tuple-element.114.left_ref.x_ref, bf16[1408,2048]{1,0:T(8,128)(2,1)} %get-tuple-element.99.refs_5_.w_ref), custom_call_target="tpu_custom_call" | custom-call | flops 14763950080 | bytes 23461888 | tf_op jit(solution)/shard_map/feed_down/pallas_call | solution.py:392
  598.1 1.5 copy-done.12
  600.9 0.6 pad_add_fusion.2.order_ref
  601.5 3.6 collective-permute-done.7
  605.1 1.0 add_convert_fusion.2
  606.2 1.4 collective-permute-start.8
  607.6 5.0 collective-permute-done.9.refs_1_
  612.7 1.4 copy-done.13
  614.1 15.3 %grad_attended.1 = (bf16[2560,512]{1,0:T(8,128)(2,1)}, bf16[2560,2048]{1,0:T(8,128)(2,1)}) custom-call(s32[4]{0:T(128)} %pad_add_fusion.order_ref, bf16[640,2048]{1,0:T(8,128)(2,1)} %get-tuple-element.123.refs_0_, bf16[640,2048]{1,0:T(8,128)(2,1)} %copy-done.13, bf16[640,2048]{1,0:T(8,128)(2,1)} %copy-done.12, ...), custom_call_target="tpu_custom_call" | custom-call | flops 5368709120 | bytes 15204352 | tf_op jit(solution)/shard_map/grad_attended/pallas_call | solution.py:607
  629.4 10.2 %convolution_convert_fusion.part_ref = bf16[512,2048]{1,0:T(8,128)(2,1)} fusion(bf16[2560,512]{1,0:T(8,128)(2,1)} %get-tuple-element.89.x_ref.o_ref, bf16[2560,2048]{1,0:T(8,128)(2,1)} %get-tuple-element.128), kind=kOutput, calls=%fused_computation.4 | convolution fusion | flops 5369757696 | bytes 15204352 | tf_op jit(solution)/shard_map/dot_general | solution.py:31
  639.6 107.4 %attend_back.1.x_ref.right_ref = bf16[2560,1536]{1,0:T(8,128)(2,1)} custom-call(s32[2]{0:T(128)} %copy-done.11, bf16[8,2560,128]{2,1,0:T(8,128)(2,1)} %get-tuple-element.122.qx_ref, bf16[2560,1536]{1,0:T(8,128)(2,1)} %get-tuple-element.85.refs_0_.refs_1_.refs_2_.refs_3_.refs_4_.refs_5_.k_ref.v_ref, ...), custom_call_target="tpu_custom_call" | custom-call | flops 67108864000 | bytes 7864320 | tf_op jit(solution)/shard_map/attend_back/pallas_call | solution.py:334
  746.9 15.2 %project_back.1 = (bf16[640,2048]{1,0:T(8,128)(2,1)}, bf16[640,2048]{1,0:T(8,128)(2,1)}) custom-call(s32[2]{0:T(128)} %pad_add_fusion.2.order_ref, bf16[2560,1536]{1,0:T(8,128)(2,1)} %attend_back.1.x_ref.right_ref, bf16[2048,1536]{1,0:T(8,128)(2,1)} %get-tuple-element.83.w_ref), custom_call_target="tpu_custom_call" | custom-call | flops 8053063680 | bytes 15466496 | tf_op jit(solution)/shard_map/project_back/pallas_call | solution.py:392
  762.5 4.7 collective-permute-done.11
  767.3 2.8 add_convert_fusion
  770.1 1.5 collective-permute-start.12
  772.1 37.4 %near_and_project_in.1 = (bf16[640,2048]{1,0:T(8,128)(2,1)}, bf16[640,2048]{1,0:T(8,128)(2,1)}, bf16[2048,1536]{1,0:T(8,128)(2,1)}) custom-call(s32[2]{0:T(128)} %pad_add_fusion.1.order_ref, bf16[2560,1536]{1,0:T(8,128)(2,1)} %attend_back.1.x_ref.right_ref, bf16[2048,1536]{1,0:T(8,128)(2,1)} %get-tuple-element.83.w_ref, ...), custom_call_target="tpu_custom_call" | custom-call | flops 20132659200 | bytes 29229056 | tf_op jit(solution)/shard_map/near_and_project_in/pallas_call | solution.py:560
  809.6 18.7 %collective-permute-done.12.refs_2_ = bf16[640,2048]{1,0:T(8,128)(2,1)S(1)} collective-permute-done((bf16[640,2048]{1,0:T(8,128)(2,1)S(1)}, bf16[640,2048]{1,0:T(8,128)(2,1)S(1)}, u32[]{:S(2)}, u32[]{:S(2)}) %collective-permute-start.12) | collective-permute-done | bytes 2621472 | tf_op jit(solution)/shard_map/ppermute | solution.py:635
  828.3 1.5 copy-done.6
  829.8 1.2 collective-permute-start.5
  831.0 0.8 slice.58
  831.8 3.9 collective-permute-done.5
  835.7 6.8 fusion
  842.6 16.7 %closing_rows.3 = (f32[640,2048]{1,0:T(8,128)}, f32[8,2048]{1,0:T(8,128)}) custom-call(bf16[640,2048]{1,0:T(8,128)(2,1)} %get-tuple-element.135.refs_0_, bf16[640,2048]{1,0:T(8,128)(2,1)} %get-tuple-element.136.refs_1_, bf16[640,2048]{1,0:T(8,128)(2,1)} %copy-done.6, bf16[640,2048]{1,0:T(8,128)(2,1)} %bitcast.38, f32[640,2048]{1,0:T(8,128)} %get-tuple-element.139.refs_4_, ...), custom_call_target="tpu_custom_call" | custom-call | tf_op jit(solution)/shard_map/closing_rows/pallas_call | solution.py:1100
  859.3 0.8 slice.59
  860.1 0.8 slice.57
  861.0 0.7 pad_maximum_fusion.vec_ref
  861.6 90.8 %sum_and_share.1 = (bf16[4,256,2816]{2,1,0:T(8,128)(2,1)}, bf16[4,176,2048]{2,1,0:T(8,128)(2,1)}, bf16[4,64,2048]{2,1,0:T(8,128)(2,1)}, f32[8,256]{1,0:T(8,128)}) custom-call(bf16[512,2048]{1,0:T(8,128)(2,1)} %convolution_convert_fusion.part_ref, f32[8,2048]{1,0:T(8,128)} %pad_maximum_fusion.vec_ref, ...), custom_call_target="tpu_custom_call" | custom-call | tf_op jit(solution)/shard_map/sum_and_share/pallas_call | solution.py:1285
  952.5 8.9 whole_columns.1
  961.9 1.6 bitcast_convert_fusion.1
  963.6 3.5 bitcast_convert_fusion
  967.0 5.6 reduce-scatter.4.cloned.1.call-done.refs_0_
  972.6 24.1 %share_pieces.1.in_ref = bf16[4,256,1536]{2,1,0:T(8,128)(2,1)} custom-call(bf16[256,1536]{1,0:T(8,128)(2,1)} %reduce-scatter.4.cloned.1.call-done.refs_0_), custom_call_target="tpu_custom_call" | custom-call | tf_op jit(solution)/shard_map/share_pieces/pallas_call | solution.py:1177
  996.7 5.5 whole_heads.1
  1002.3 2.7 copy.24
  1004.9 1.0 copy-done.1
  (76 shorter events, 9.1 us)
Async XLA Ops:
  7.2 195.7 %copy-start = (bf16[704,2048]{1,0:T(8,128)(2,1)S(1)}, bf16[704,2048]{1,0:T(8,128)(2,1)}, u32[]{:S(2)}) copy-start(bf16[704,2048]{1,0:T(8,128)(2,1)} %param.18) | copy-start | bytes 8650756
  7.2 199.3 %all-gather.3.cloned.1.call-start = ((), (), s32[]{:S(2)}) async-start(), calls=%async_computation.3 | async-start | bytes 2359296 | tf_op jit(solution)/shard_map/all_gather | solution.py:1438
  95.6 8.1 copy-start.14
  95.7 8.3 copy-start.9
  95.7 267.1 %all-gather.5.cloned.1.call-start = ((), (), s32[]{:S(2)}) async-start(), calls=%async_computation.4 | async-start | bytes 12976128 | tf_op jit(solution)/shard_map/all_gather | solution.py:1438
  100.2 761.4 %reduce-scatter.8.cloned.1.call-start = ((), (), s32[]{:S(2)}) async-start(), calls=%async_computation.7 | async-start | bytes 6488064 | tf_op jit(solution)/shard_map/reduce_scatter | solution.py:1442
  100.2 103.6 %collective-permute-start = (bf16[640,2048]{1,0:T(8,128)(2,1)}, bf16[640,2048]{1,0:T(8,128)(2,1)}, u32[]{:S(2)}, u32[]{:S(2)}) collective-permute-start(bf16[640,2048]{1,0:T(8,128)(2,1)} %bitcast.42), channel_id=1, source_target_pairs={{0,8},{8,0},{16,24},{24,16},{1,9},{9,1},{17,25},{25,17},{2,10},{10... | collective-permute-start | bytes 7864328 | tf_op jit(solution)/shard_map/ppermute | solution.py:643
  102.4 98.8 %collective-permute-start.1 = (bf16[640,2048]{1,0:T(8,128)(2,1)}, bf16[640,2048]{1,0:T(8,128)(2,1)}, u32[]{:S(2)}, u32[]{:S(2)}) collective-permute-start(bf16[640,2048]{1,0:T(8,128)(2,1)} %bitcast.43), channel_id=1, source_target_pairs={{0,16},{8,24},{16,0},{24,8},{1,17},{9,25},{17,1},{25,9},{2,18},{10... | collective-permute-start | bytes 7864328 | tf_op jit(solution)/shard_map/ppermute | solution.py:635
  103.8 36.4 %copy-start.11 = (s32[2]{0:T(128)}, s32[2]{0:T(128)S(1)}, u32[]{:S(2)}) copy-start(s32[2]{0:T(128)S(1)} %fusion.5.ends_ref) | copy-start | bytes 28
  201.2 5.3 collective-permute-start.2
  446.5 5.2 collective-permute-start.3
  454.5 59.2 %collective-permute-start.4 = (bf16[640,2048]{1,0:T(8,128)(2,1)S(1)}, bf16[640,2048]{1,0:T(8,128)(2,1)S(1)}, u32[]{:S(2)}, u32[]{:S(2)}) collective-permute-start(bf16[640,2048]{1,0:T(8,128)(2,1)S(1)} %add_convert_fusion.3), channel_id=1, source_target_pairs={{0,16},{8,24},{16,0},{24,8},{1,17},{9,25},{17,1},{25,9},{2,18},{10... | collective-permute-start | bytes 7864328 | tf_op jit(solution)/shard_map/ppermute | solution.py:635
  513.7 1.5 copy-start.7
  515.2 346.4 %reduce-scatter.6.cloned.1.call-start = ((), (), s32[]{:S(2)}) async-start(), calls=%async_computation.6 | async-start | bytes 12976128 | tf_op jit(solution)/shard_map/reduce_scatter | solution.py:1442
  533.8 64.3 %collective-permute-start.6 = (bf16[640,2048]{1,0:T(8,128)(2,1)}, bf16[640,2048]{1,0:T(8,128)(2,1)S(1)}, u32[]{:S(2)}, u32[]{:S(2)}) collective-permute-start(bf16[640,2048]{1,0:T(8,128)(2,1)} %get-tuple-element.123.refs_0_), channel_id=1, source_target_pairs={{0,16},{8,24},{16,0},{24,8},{1,17},{9,25},{17,1},{25,9},{2,18},{10... | collective-permute-start | bytes 7864328 | tf_op jit(solution)/shard_map/ppermute | solution.py:635
  598.1 1.5 copy-start.12
  599.6 5.5 copy-start.3
  599.6 373.0 %reduce-scatter.4.cloned.1.call-start = ((), (), s32[]{:S(2)}) async-start(), calls=%async_computation.5 | async-start | bytes 7077888 | tf_op jit(solution)/shard_map/reduce_scatter | solution.py:1442
  599.8 5.3 collective-permute-start.7
  600.4 12.2 %collective-permute-start.9 = (bf16[640,2048]{1,0:T(8,128)(2,1)}, bf16[640,2048]{1,0:T(8,128)(2,1)S(1)}, u32[]{:S(2)}, u32[]{:S(2)}) collective-permute-start(bf16[640,2048]{1,0:T(8,128)(2,1)} %get-tuple-element.123.refs_0_), channel_id=1, source_target_pairs={{0,8},{8,0},{16,24},{24,16},{1,9},{9,1},{17,25},{25,17},{2,10},{10... | collective-permute-start | bytes 7864328 | tf_op jit(solution)/shard_map/ppermute | solution.py:643
  600.4 12.3 %collective-permute-start.10 = (bf16[640,2048]{1,0:T(8,128)(2,1)}, bf16[640,2048]{1,0:T(8,128)(2,1)}, u32[]{:S(2)}, u32[]{:S(2)}) collective-permute-start(bf16[640,2048]{1,0:T(8,128)(2,1)} %copy-done.12), channel_id=1, source_target_pairs={{0,8},{8,0},{16,24},{24,16},{1,9},{9,1},{17,25},{25,17},{2,10},{10... | collective-permute-start | bytes 7864328 | tf_op jit(solution)/shard_map/ppermute | solution.py:643
  606.2 140.8 %collective-permute-start.8 = (bf16[640,2048]{1,0:T(8,128)(2,1)S(1)}, bf16[640,2048]{1,0:T(8,128)(2,1)S(1)}, u32[]{:S(2)}, u32[]{:S(2)}) collective-permute-start(bf16[640,2048]{1,0:T(8,128)(2,1)S(1)} %add_convert_fusion.2), channel_id=1, source_target_pairs={{0,16},{8,24},{16,0},{24,8},{1,17},{9,25},{17,1},{25,9},{2,18},{10... | collective-permute-start | bytes 7864328 | tf_op jit(solution)/shard_map/ppermute | solution.py:635
  612.6 1.5 copy-start.13
  746.9 15.2 %copy-start.5 = (bf16[640,2048]{1,0:T(8,128)(2,1)}, bf16[640,2048]{1,0:T(8,128)(2,1)S(1)}, u32[]{:S(2)}) copy-start(bf16[640,2048]{1,0:T(8,128)(2,1)S(1)} %collective-permute-done.8) | copy-start | bytes 7864324
  762.1 5.1 collective-permute-start.11
  770.1 58.2 %collective-permute-start.12 = (bf16[640,2048]{1,0:T(8,128)(2,1)S(1)}, bf16[640,2048]{1,0:T(8,128)(2,1)S(1)}, u32[]{:S(2)}, u32[]{:S(2)}) collective-permute-start(bf16[640,2048]{1,0:T(8,128)(2,1)S(1)} %add_convert_fusion), channel_id=1, source_target_pairs={{0,16},{8,24},{16,0},{24,8},{1,17},{9,25},{17,1},{25,9},{2,18},{10... | collective-permute-start | bytes 7864328 | tf_op jit(solution)/shard_map/ppermute | solution.py:635
  828.3 1.5 copy-start.6
  829.8 5.9 copy-start.4
  829.8 5.9 collective-permute-start.5
  952.5 8.9 copy-start.10
  952.5 9.5 copy-start.8
  961.3 2.2 copy-start.2
  972.6 29.6 %slice-start = ((s8[5242880]{0:T(1024)(128)(4,1)}), s8[4194304]{0:T(1024)(128)(4,1)S(1)}, s32[]{:S(2)}) async-start(s8[5242880]{0:T(1024)(128)(4,1)} %bitcast.39), calls=%async_computation.8 | async-start | bytes 8388608
  996.7 5.5 slice-start.1
  1002.2 3.7 copy-start.1
Sparse Core Ops, SparseCore 0:
  95.8 50.3 all-gather.2
  148.9 203.9 all-gather.4
  515.3 127.7 reduce-scatter.7
  646.6 190.8 reduce-scatter.5
  841.5 131.0 reduce-scatter.3

commit v4 on v3

--- a/solution.py
+++ b/solution.py
@@ -887,7 +887,7 @@
 CHUNKS = 4
 
 
-def hidden_rows(parts, residual, gain, bias, down_slice, seq_size, fsdp_size):
+def hidden_rows(parts, residual, gain, bias, carry, seq_size, fsdp_size):
     rows, width = residual.shape
     chips = seq_size // CORES
     deep = planes(fsdp_size)
@@ -898,14 +898,14 @@
         own = refs[0 : 2 * chips : 2]
         other = refs[1 : 2 * chips : 2]
         refs = refs[2 * chips :]
-        res_ref, gain_ref, bias_ref, down_ref, hidden_ref, normed_ref, w_down = refs[:7]
+        res_ref, gain_ref, bias_ref, carry_ref, hidden_ref, normed_ref, carried_all = refs[:7]
         (
             from_core, total, from_x, mine,
             c_send, c_recv, x_send, x_recv, g_send, g_recv, f_send, f_recv, here,
         ) = refs[7:20]
         p = Place(seq_size, fsdp_size)
         greet(p, True)
-        down = FsdpGather(p, down_ref, w_down, refs[20:])
+        carried = FsdpGather(p, carry_ref, carried_all, refs[20:])
 
         def span(c):
             return pl.ds(c * part, part)
@@ -945,9 +945,9 @@
                 both = own[k][span(c)].astype(F32) + from_core[k, span(c)].astype(F32)
                 total[k - 1, span(c)] = both.astype(BF16)
                 along(k, c).start()
-        down.start()
-        down_here = pltpu.make_async_copy(down_ref, down.slot(p.fsdp), here.at[1])
-        down_here.start()
+        carried.start()
+        carry_here = pltpu.make_async_copy(carry_ref, carried.slot(p.fsdp), here.at[1])
+        carry_here.start()
         for c in range(CHUNKS):
             to_core(0, c).wait_recv()
             rows_here = own[0][span(c)].astype(F32) + from_core[0, span(c)].astype(F32)
@@ -962,16 +962,17 @@
             for k in far:
                 share(k, c).start()
             pass_on(0, c).start()
-            if c + 1 < deep:
-                down.pass_on(c + 1)
+            if c % 2 == 1 and c // 2 + 1 < deep:
+                carried.pass_on(c // 2 + 1)
         keep = pltpu.make_async_copy(mine, normed_ref.at[0], here.at[0])
         keep.start()
-        for d in range(CHUNKS + 1, deep):
-            down.pass_on(d)
         for c in range(CHUNKS):
             for k in far:
                 share(k, c).wait_recv()
                 pass_on(k, c).start()
+            if c == 1:
+                for d in range(CHUNKS // 2 + 1, deep):
+                    carried.pass_on(d)
         for c in range(CHUNKS):
             for k in range(chips):
                 to_core(k, c).wait_send()
@@ -980,8 +981,8 @@
                 along(k, c).wait_send()
                 share(k, c).wait_send()
         keep.wait()
-        down.finish()
-        down_here.wait()
+        carried.finish()
+        carry_here.wait()
 
     vmem = pl.BlockSpec(memory_space=pltpu.VMEM)
     any_space = pl.BlockSpec(memory_space=pl.ANY)
@@ -994,7 +995,7 @@
         out_shape=[
             jax.ShapeDtypeStruct(block, F32),
             jax.ShapeDtypeStruct((2 * chips,) + block, BF16),
-            jax.ShapeDtypeStruct((down_slice.shape[0] * fsdp_size, width), BF16),
+            jax.ShapeDtypeStruct((carry.shape[0] * fsdp_size, carry.shape[1]), BF16),
         ],
         scratch_shapes=[
             pltpu.VMEM((chips,) + block, BF16),
@@ -1012,7 +1013,7 @@
         residual,
         jnp.broadcast_to(gain[None], (8, width)),
         jnp.broadcast_to(bias[None], (8, width)),
-        down_slice,
+        carry,
     )
 
 
@@ -1482,7 +1483,7 @@
         seq_size,
         fsdp_size,
     )
-    gate_late, up_late, out_late = tie((gate_weight, up_weight, project_out), w_in)
+    down_late, out_late = tie((down_weight, project_out), w_in)
     if spread:
         w_out = gather_fsdp(lax.dynamic_slice_in_dim(out_late, me * pieces_out, pieces_out, 0))
     else:
@@ -1492,9 +1493,8 @@
     gain_one, bias_one, gain_two, bias_two = [vectors[i] for i in range(4)]
     upstream_own = tie(grad_output[0], all_tokens)
     upstream_far = [from_chip(upstream_own, chips, ahead) for ahead in far]
-    down_slice = lax.dynamic_slice_in_dim(down_weight, me * pieces_down, pieces_down, 0)
-    whole_tiles = pieces_down % 16 == 0
-    w_gate_up = gather_fsdp(own_columns(gate_late, up_late, me, seq_size, fsdp_size))
+    w_down = gather_fsdp(lax.dynamic_slice_in_dim(down_late, me * pieces_down, pieces_down, 0))
+    gate_up_part = own_columns(gate_weight, up_weight, me, seq_size, fsdp_size)
 
     cosine, sine, ends = rope_tables(cont_lengths[0], total_rows)
 
@@ -1514,13 +1514,9 @@
 
     attended = tie(attended, upstream_blocks)
     parts = chip_matmul(attended, w_out, order, rows_dev, False, "attention_out")
-    hidden, normed_blocks, w_down = hidden_rows(
-        parts, tokens[0], gain_two, bias_two,
-        down_slice if whole_tiles else down_slice[: pieces_down // 16 * 16],
-        seq_size, fsdp_size,
-    )
-    if not whole_tiles:
-        w_down = gather_fsdp(down_slice)
+    hidden, normed_blocks, w_gate_up = hidden_rows(
+        parts, tokens[0], gain_two, bias_two, gate_up_part, seq_size, fsdp_size
+    )
     product, grads, normed_second, upstream_all = feed(
         normed_blocks, upstream_blocks, w_gate_up, w_down
     )
@@ -1564,9 +1560,9 @@
         for own, other in layer_far
     ]
     layer_arriving = [to_chip(s, chips, ahead) for s, ahead in zip(layer_sent, far)]
-    grad_attended, low_hidden = blocks_matmul(tie(low_blocks, layer_sent), w_out, order)
+    grad_attended, low_hidden = blocks_matmul(low_blocks, w_out, order)
     grad_out = dot_first(attended, low_hidden).astype(BF16)
-    grad_attended = tie(grad_attended, grad_out)
+    grad_attended = tie(grad_attended, grad_out, layer_sent)
 
     grad_qkv = attend_back(ends, qkv, qx, grad_attended, attended, cosine, sine)
     grad_qkv = tie(grad_qkv, layer_arriving)

time: 1020 us -> 1010 us (level)
    pallas_call x1, Pallas kernels: 90.8 us -> 75.2 us  [sum_and_share(): pl.pallas_call(kernel, in_specs=[vmem] * (count + 1), out_specs=[pl.Block...]
  transfers between devices with their start and end apart: 18 -> 18, of which waited for: 10 -> 9; matrix products, arithmetic and copies ran while one was open for 4% -> 4% of each run, Pallas kernels for 66% -> 65%
where the time goes in v4:
time: 1010 us; the launch traced here: 1000 us
  Pallas kernels  854 us (85%)
  waiting for transfers between devices  63.4 us (6%)
  other arithmetic  28.2 us (3%)
  local copies, waits for them, and re-layouts  22.4 us (2%)
  between operations  14.3 us (1%)
  starting transfers between devices  12.2 us (1%)
  matrix products  10.1 us (1%)
    pallas_call x1, Pallas kernels, hidden_rows(): pl.pallas_call(kernel, in_specs=[vmem] * (2 * chips + 4), out_specs=[vmem...  146 us
    pallas_call x1, Pallas kernels, attend_back(): pl.pallas_call(attend_back_kernel, grid_spec=pltpu.PrefetchScalarGridSpec...  107 us
    pallas_call x2, Pallas kernels, near_and_grad(): pl.pallas_call(kernel, grid_spec=pltpu.PrefetchScalarGridSpec(num_scalar_...  81.3 us
    pallas_call x4, Pallas kernels, chip_matmul(): pl.pallas_call(kernel, grid_spec=pltpu.PrefetchScalarGridSpec(num_scalar_...  78.1 us
    pallas_call x1, Pallas kernels, opening(): pl.pallas_call(kernel, in_specs=[pl.BlockSpec(memory_space=pltpu.VMEM)] *...  75.7 us
    pallas_call x1, Pallas kernels, sum_and_share(): pl.pallas_call(kernel, in_specs=[vmem] * (count + 1), out_specs=[pl.Block...  75.2 us
    pallas_call x1, Pallas kernels, attend(): pl.pallas_call(attend_kernel, grid_spec=pltpu.PrefetchScalarGridSpec(num_...  62.2 us
    pallas_call x1, Pallas kernels, feed(): pl.pallas_call(kernel, grid=(2 * count,), in_specs=[pl.BlockSpec((1, half...  60 us
  transfers between devices with their start and end apart: 18, of which 9 were waited for; matrix products, arithmetic and copies ran while one was open for 4% of the time, Pallas kernels for 65%

profile of v4, /device:TPU:9, one launch (start us, length us, event | category | flops | bytes accessed | tf_op | source)
XLA Modules:
  0.0 1004.1 jit_solution(14951879136330879310)
XLA Ops:
  7.2 0.8 stack.37
  8.1 0.7 stack.38
  8.7 0.7 stack.39
  9.4 0.7 stack.40
  10.7 7.5 own_heads.1.in_ref
  18.2 75.7 %opening.1 = (bf16[2560,2048]{1,0:T(8,128)(2,1)}, bf16[2048,1536]{1,0:T(8,128)(2,1)}, f32[8,8,256]{2,1,0:T(8,128)}) custom-call(bf16[640,2048]{1,0:T(8,128)(2,1)} %bitcast.36, bf16[256,1536]{1,0:T(8,128)(2,1)} %own_heads.1.in_ref, f32[8,256]{1,0:T(8,128)} %concatenate.12.vec_ref), custom_call_target="tpu_custom_call" | custom-call | tf_op jit(solution)/shard_map/opening/pallas_call | solution.py:862
  94.0 1.7 constant_dynamic-slice_fusion.1
  95.8 0.9 constant_dynamic-slice_fusion
  96.8 2.3 collective-permute-start
  99.0 1.2 collective-permute-start.1
  100.6 6.3 fusion.3
  107.5 0.6 broadcast_in_dim.114.bias_ref
  108.1 28.6 %project_in_rope.1 = (bf16[2560,1536]{1,0:T(8,128)(2,1)}, bf16[2560,2048]{1,0:T(8,128)(2,1)}) custom-call(bf16[2560,2048]{1,0:T(8,128)(2,1)} %get-tuple-element.77.x_ref, bf16[2048,1536]{1,0:T(8,128)(2,1)} %get-tuple-element.78.w_ref, f32[8,2048]{1,0:T(8,128)} %broadcast_in_dim.112.gain_ref.refs_5_, f32[8,2048]{1,0:T(8,128)} %broadcast_in_dim.114.bias_ref, ...), custom_call_target="tpu_custom_call" | custom-call | flops 16106127360 | bytes 24641536 | tf_op jit(solution)/shard_map/project_in_rope/pallas_call | solution.py:104
  136.8 62.2 %attend.1 = (bf16[2560,512]{1,0:T(8,128)(2,1)}, bf16[8,2560,128]{2,1,0:T(8,128)(2,1)}) custom-call(s32[2]{0:T(128)} %copy-done.11, bf16[2560,1536]{1,0:T(8,128)(2,1)} %get-tuple-element.80.refs_0_.refs_1_.refs_2_.refs_3_.refs_4_.refs_5_.k_ref.v_ref, bf16[2560,1536]{1,0:T(8,128)(2,1)} %get-tuple-element.80.refs_0_.refs_1_.refs_2_.refs_3_.refs_4_.refs_5_.k_ref.v_ref, ...), custom_call_target="tpu_custom_call" | custom-call | flops 26843545600 | bytes 7864320 | tf_op jit(solution)/shard_map/attend/pallas_call | solution.py:218
  199.3 0.6 slice.56.order_ref
  199.9 4.4 own_columns.1.refs_7_
  205.0 13.9 %attention_out.1 = (bf16[640,2048]{1,0:T(8,128)(2,1)}, bf16[640,2048]{1,0:T(8,128)(2,1)}, bf16[640,2048]{1,0:T(8,128)(2,1)}, bf16[640,2048]{1,0:T(8,128)(2,1)}) custom-call(s32[4]{0:T(128)} %pad_add_fusion.order_ref, bf16[2560,512]{1,0:T(8,128)(2,1)} %get-tuple-element.84.x_ref.o_ref, bf16[512,2048]{1,0:T(8,128)(2,1)} %all-gather.3.cloned.1.call-done.w_ref.refs_4_), custom_call_target="tpu_custom_call" | custom-call | flops 5368709120 | bytes 15204352 | tf_op jit(solution)/shard_map/attention_out/pallas_call | solution.py:392
  220.1 146.2 %hidden_rows.1 = (f32[640,2048]{1,0:T(8,128)}, bf16[4,640,2048]{2,1,0:T(8,128)(2,1)}, bf16[2048,2816]{1,0:T(8,128)(2,1)}) custom-call(bf16[640,2048]{1,0:T(8,128)(2,1)} %get-tuple-element.86.refs_0_, bf16[640,2048]{1,0:T(8,128)(2,1)} %get-tuple-element.87.refs_1_, bf16[640,2048]{1,0:T(8,128)(2,1)} %get-tuple-element.88.refs_2_, ...), custom_call_target="tpu_custom_call" | custom-call | tf_op jit(solution)/shard_map/hidden_rows/pallas_call | solution.py:991
  366.3 60.0 %feed.1 = (bf16[2560,1408]{1,0:T(8,128)(2,1)}, bf16[2560,2816]{1,0:T(8,128)(2,1)}, bf16[2560,2048]{1,0:T(8,128)(2,1)}, bf16[2560,2048]{1,0:T(8,128)(2,1)}) custom-call(bf16[4,640,2048]{2,1,0:T(8,128)(2,1)} %get-tuple-element.91.x_ref, bf16[640,2048]{1,0:T(8,128)(2,1)} %bitcast.44, bf16[640,2048]{1,0:T(8,128)(2,1)} %copy-done.12, ...), custom_call_target="tpu_custom_call" | custom-call | flops 44291850240 | bytes 55967744 | tf_op jit(solution)/shard_map/feed/pallas_call | solution.py:499
  426.3 23.7 %feed_back.1 = (bf16[640,2048]{1,0:T(8,128)(2,1)}, bf16[640,2048]{1,0:T(8,128)(2,1)}) custom-call(s32[2]{0:T(128)} %slice.56.order_ref, bf16[2560,2816]{1,0:T(8,128)(2,1)} %get-tuple-element.99.x_ref.g_ref, bf16[2048,2816]{1,0:T(8,128)(2,1)} %get-tuple-element.92.refs_4_.w_ref), custom_call_target="tpu_custom_call" | custom-call | flops 14763950080 | bytes 23986176 | tf_op jit(solution)/shard_map/feed_back/pallas_call | solution.py:392
  450.0 1.0 collective-permute-start.3
  451.1 4.7 collective-permute-done.3
  455.8 2.8 add_convert_fusion.3
  458.6 1.3 collective-permute-start.4
  460.4 43.1 %near_and_down.1 = (bf16[640,2048]{1,0:T(8,128)(2,1)}, bf16[640,2048]{1,0:T(8,128)(2,1)}, bf16[1408,2048]{1,0:T(8,128)(2,1)}) custom-call(s32[2]{0:T(128)} %bitcast.55, bf16[2560,2816]{1,0:T(8,128)(2,1)} %get-tuple-element.99.x_ref.g_ref, bf16[2048,2816]{1,0:T(8,128)(2,1)} %get-tuple-element.92.refs_4_.w_ref, ...), custom_call_target="tpu_custom_call" | custom-call | flops 36909875200 | bytes 42663936 | tf_op jit(solution)/shard_map/near_and_down/pallas_call | solution.py:560
  503.5 13.2 %collective-permute-done.4.refs_2_ = bf16[640,2048]{1,0:T(8,128)(2,1)S(1)} collective-permute-done((bf16[640,2048]{1,0:T(8,128)(2,1)S(1)}, bf16[640,2048]{1,0:T(8,128)(2,1)S(1)}, u32[]{:S(2)}, u32[]{:S(2)}) %collective-permute-start.4) | collective-permute-done | bytes 2621472 | tf_op jit(solution)/shard_map/ppermute | solution.py:635
  516.8 1.5 copy-done.7
  518.7 18.3 %closing_rows.2 = (f32[640,2048]{1,0:T(8,128)}, bf16[640,2048]{1,0:T(8,128)(2,1)}, f32[8,2048]{1,0:T(8,128)}) custom-call(bf16[640,2048]{1,0:T(8,128)(2,1)} %get-tuple-element.101.refs_0_, bf16[640,2048]{1,0:T(8,128)(2,1)} %get-tuple-element.102.refs_1_, bf16[640,2048]{1,0:T(8,128)(2,1)} %copy-done.7, f32[640,2048]{1,0:T(8,128)} %get-tuple-element.90.refs_3_, ...), custom_call_target="tpu_custom_call" | custom-call | tf_op jit(solution)/shard_map/closing_rows/pallas_call | solution.py:1101
  537.3 38.4 %grad_gate_up.1 = bf16[2048,2816]{1,0:T(8,128)(2,1)} custom-call(bf16[2560,2048]{1,0:T(8,128)(2,1)} %get-tuple-element.107.x_ref, bf16[2560,2816]{1,0:T(8,128)(2,1)} %get-tuple-element.99.x_ref.g_ref), custom_call_target="tpu_custom_call" | custom-call | flops 29527900160 | bytes 36438016 | tf_op jit(solution)/shard_map/grad_gate_up/pallas_call | solution.py:427
  576.2 25.4 %feed_down.1 = (bf16[640,2048]{1,0:T(8,128)(2,1)}, bf16[640,2048]{1,0:T(8,128)(2,1)}, bf16[640,2048]{1,0:T(8,128)(2,1)}, bf16[640,2048]{1,0:T(8,128)(2,1)}) custom-call(s32[4]{0:T(128)} %iota.50.order_ref, bf16[2560,1408]{1,0:T(8,128)(2,1)} %get-tuple-element.108.left_ref.x_ref, bf16[1408,2048]{1,0:T(8,128)(2,1)} %all-gather.5.cloned.1.call-done.refs_5_.w_ref), custom_call_target="tpu_custom_call" | custom-call | flops 14763950080 | bytes 23461888 | tf_op jit(solution)/shard_map/feed_down/pallas_call | solution.py:392
  601.6 1.5 copy-done.13
  604.2 0.7 pad_add_fusion.2.order_ref
  604.9 3.7 collective-permute-done.7
  608.6 1.0 add_convert_fusion.2
  609.6 1.3 collective-permute-start.8
  611.0 5.1 collective-permute-done.9.refs_1_
  616.2 1.4 copy-done.14
  617.6 15.0 %grad_attended.1 = (bf16[2560,512]{1,0:T(8,128)(2,1)}, bf16[2560,2048]{1,0:T(8,128)(2,1)}) custom-call(s32[4]{0:T(128)} %pad_add_fusion.order_ref, bf16[640,2048]{1,0:T(8,128)(2,1)} %get-tuple-element.105.refs_0_, bf16[640,2048]{1,0:T(8,128)(2,1)} %copy-done.14, bf16[640,2048]{1,0:T(8,128)(2,1)} %copy-done.13, ...), custom_call_target="tpu_custom_call" | custom-call | flops 5368709120 | bytes 15204352 | tf_op jit(solution)/shard_map/grad_attended/pallas_call | solution.py:607
  632.6 10.1 %convolution_convert_fusion.part_ref = bf16[512,2048]{1,0:T(8,128)(2,1)} fusion(bf16[2560,512]{1,0:T(8,128)(2,1)} %get-tuple-element.84.x_ref.o_ref, bf16[2560,2048]{1,0:T(8,128)(2,1)} %get-tuple-element.118), kind=kOutput, calls=%fused_computation.4 | convolution fusion | flops 5369757696 | bytes 15204352 | tf_op jit(solution)/shard_map/dot_general | solution.py:31
  642.7 107.5 %attend_back.1.x_ref.right_ref = bf16[2560,1536]{1,0:T(8,128)(2,1)} custom-call(s32[2]{0:T(128)} %copy-done.11, bf16[8,2560,128]{2,1,0:T(8,128)(2,1)} %get-tuple-element.116.qx_ref, bf16[2560,1536]{1,0:T(8,128)(2,1)} %get-tuple-element.80.refs_0_.refs_1_.refs_2_.refs_3_.refs_4_.refs_5_.k_ref.v_ref, ...), custom_call_target="tpu_custom_call" | custom-call | flops 67108864000 | bytes 7864320 | tf_op jit(solution)/shard_map/attend_back/pallas_call | solution.py:334
  750.1 15.1 %project_back.1 = (bf16[640,2048]{1,0:T(8,128)(2,1)}, bf16[640,2048]{1,0:T(8,128)(2,1)}) custom-call(s32[2]{0:T(128)} %pad_add_fusion.2.order_ref, bf16[2560,1536]{1,0:T(8,128)(2,1)} %attend_back.1.x_ref.right_ref, bf16[2048,1536]{1,0:T(8,128)(2,1)} %get-tuple-element.78.w_ref), custom_call_target="tpu_custom_call" | custom-call | flops 8053063680 | bytes 15466496 | tf_op jit(solution)/shard_map/project_back/pallas_call | solution.py:392
  765.6 4.7 collective-permute-done.11
  770.4 2.8 add_convert_fusion
  773.2 1.3 collective-permute-start.12
  775.0 38.2 %near_and_project_in.1 = (bf16[640,2048]{1,0:T(8,128)(2,1)}, bf16[640,2048]{1,0:T(8,128)(2,1)}, bf16[2048,1536]{1,0:T(8,128)(2,1)}) custom-call(s32[2]{0:T(128)} %pad_add_fusion.1.order_ref, bf16[2560,1536]{1,0:T(8,128)(2,1)} %attend_back.1.x_ref.right_ref, bf16[2048,1536]{1,0:T(8,128)(2,1)} %get-tuple-element.78.w_ref, ...), custom_call_target="tpu_custom_call" | custom-call | flops 20132659200 | bytes 29229056 | tf_op jit(solution)/shard_map/near_and_project_in/pallas_call | solution.py:560
  813.2 18.1 %collective-permute-done.12.refs_2_ = bf16[640,2048]{1,0:T(8,128)(2,1)S(1)} collective-permute-done((bf16[640,2048]{1,0:T(8,128)(2,1)S(1)}, bf16[640,2048]{1,0:T(8,128)(2,1)S(1)}, u32[]{:S(2)}, u32[]{:S(2)}) %collective-permute-start.12) | collective-permute-done | bytes 2621472 | tf_op jit(solution)/shard_map/ppermute | solution.py:635
  831.3 1.5 copy-done.6
  832.8 1.3 collective-permute-start.5
  834.1 0.8 slice.58
  835.0 3.9 collective-permute-done.5
  838.9 6.8 fusion
  845.6 16.5 %closing_rows.3 = (f32[640,2048]{1,0:T(8,128)}, f32[8,2048]{1,0:T(8,128)}) custom-call(bf16[640,2048]{1,0:T(8,128)(2,1)} %get-tuple-element.125.refs_0_, bf16[640,2048]{1,0:T(8,128)(2,1)} %get-tuple-element.126.refs_1_, bf16[640,2048]{1,0:T(8,128)(2,1)} %copy-done.6, bf16[640,2048]{1,0:T(8,128)(2,1)} %bitcast.38, f32[640,2048]{1,0:T(8,128)} %get-tuple-element.129.refs_4_, ...), custom_call_target="tpu_custom_call" | custom-call | tf_op jit(solution)/shard_map/closing_rows/pallas_call | solution.py:1101
  862.2 0.8 slice.59
  863.0 0.8 slice.57
  863.9 0.7 pad_maximum_fusion.vec_ref
  864.5 75.2 %sum_and_share.1 = (bf16[4,256,2816]{2,1,0:T(8,128)(2,1)}, bf16[4,176,2048]{2,1,0:T(8,128)(2,1)}, bf16[4,64,2048]{2,1,0:T(8,128)(2,1)}, f32[8,256]{1,0:T(8,128)}) custom-call(bf16[512,2048]{1,0:T(8,128)(2,1)} %convolution_convert_fusion.part_ref, f32[8,2048]{1,0:T(8,128)} %pad_maximum_fusion.vec_ref, ...), custom_call_target="tpu_custom_call" | custom-call | tf_op jit(solution)/shard_map/sum_and_share/pallas_call | solution.py:1286
  939.7 8.9 whole_columns.1
  948.6 1.6 bitcast_convert_fusion.1
  950.2 9.6 reduce-scatter.4.cloned.1.call-done.refs_0_
  959.8 24.1 %share_pieces.1.in_ref = bf16[4,256,1536]{2,1,0:T(8,128)(2,1)} custom-call(bf16[256,1536]{1,0:T(8,128)(2,1)} %reduce-scatter.4.cloned.1.call-done.refs_0_), custom_call_target="tpu_custom_call" | custom-call | tf_op jit(solution)/shard_map/share_pieces/pallas_call | solution.py:1178
  983.9 5.6 whole_heads.1
  989.5 3.5 bitcast_convert_fusion
  993.6 2.7 copy.24
  996.3 1.0 copy-done.1
  (78 shorter events, 8.4 us)
Async XLA Ops:
  7.2 88.6 %copy-start = (bf16[704,2048]{1,0:T(8,128)(2,1)S(1)}, bf16[704,2048]{1,0:T(8,128)(2,1)}, u32[]{:S(2)}) copy-start(bf16[704,2048]{1,0:T(8,128)(2,1)} %param.18) | copy-start | bytes 8650756
  7.2 197.8 %all-gather.3.cloned.1.call-start = ((), (), s32[]{:S(2)}) async-start(), calls=%async_computation.3 | async-start | bytes 2359296 | tf_op jit(solution)/shard_map/all_gather | solution.py:1439
  18.2 82.0 %copy-start.15 = (s32[1,2]{1,0:T(1,128)S(1)}, s32[1,2]{1,0:T(1,128)}, u32[]{:S(2)}) copy-start(s32[1,2]{1,0:T(1,128)} %param.13) | copy-start | bytes 28
  94.0 6.6 copy-start.9
  95.7 270.6 %all-gather.5.cloned.1.call-start = ((), (), s32[]{:S(2)}) async-start(), calls=%async_computation.4 | async-start | bytes 6488064 | tf_op jit(solution)/shard_map/all_gather | solution.py:1439
  96.7 767.8 %reduce-scatter.8.cloned.1.call-start = ((), (), s32[]{:S(2)}) async-start(), calls=%async_computation.7 | async-start | bytes 6488064 | tf_op jit(solution)/shard_map/reduce_scatter | solution.py:1443
  96.8 108.2 %collective-permute-start = (bf16[640,2048]{1,0:T(8,128)(2,1)}, bf16[640,2048]{1,0:T(8,128)(2,1)S(1)}, u32[]{:S(2)}, u32[]{:S(2)}) collective-permute-start(bf16[640,2048]{1,0:T(8,128)(2,1)} %bitcast.42), channel_id=1, source_target_pairs={{0,8},{8,0},{16,24},{24,16},{1,9},{9,1},{17,25},{25,17},{2,10},{10... | collective-permute-start | bytes 7864328 | tf_op jit(solution)/shard_map/ppermute | solution.py:643
  99.0 100.0 %collective-permute-start.1 = (bf16[640,2048]{1,0:T(8,128)(2,1)}, bf16[640,2048]{1,0:T(8,128)(2,1)}, u32[]{:S(2)}, u32[]{:S(2)}) collective-permute-start(bf16[640,2048]{1,0:T(8,128)(2,1)} %bitcast.43), channel_id=1, source_target_pairs={{0,16},{8,24},{16,0},{24,8},{1,17},{9,25},{17,1},{25,9},{2,18},{10... | collective-permute-start | bytes 7864328 | tf_op jit(solution)/shard_map/ppermute | solution.py:635
  100.4 36.4 %copy-start.11 = (s32[2]{0:T(128)}, s32[2]{0:T(128)S(1)}, u32[]{:S(2)}) copy-start(s32[2]{0:T(128)S(1)} %fusion.5.ends_ref) | copy-start | bytes 28
  199.0 6.0 collective-permute-start.2
  205.0 13.9 %copy-start.12 = (bf16[640,2048]{1,0:T(8,128)(2,1)}, bf16[640,2048]{1,0:T(8,128)(2,1)S(1)}, u32[]{:S(2)}) copy-start(bf16[640,2048]{1,0:T(8,128)(2,1)S(1)} %collective-permute-done.refs_1_) | copy-start | bytes 7864324
  450.0 5.8 collective-permute-start.3
  458.6 58.1 %collective-permute-start.4 = (bf16[640,2048]{1,0:T(8,128)(2,1)S(1)}, bf16[640,2048]{1,0:T(8,128)(2,1)S(1)}, u32[]{:S(2)}, u32[]{:S(2)}) collective-permute-start(bf16[640,2048]{1,0:T(8,128)(2,1)S(1)} %add_convert_fusion.3), channel_id=1, source_target_pairs={{0,16},{8,24},{16,0},{24,8},{1,17},{9,25},{17,1},{25,9},{2,18},{10... | collective-permute-start | bytes 7864328 | tf_op jit(solution)/shard_map/ppermute | solution.py:635
  516.8 1.5 copy-start.7
  518.3 346.2 %reduce-scatter.6.cloned.1.call-start = ((), (), s32[]{:S(2)}) async-start(), calls=%async_computation.6 | async-start | bytes 12976128 | tf_op jit(solution)/shard_map/reduce_scatter | solution.py:1443
  537.0 64.6 %collective-permute-start.6 = (bf16[640,2048]{1,0:T(8,128)(2,1)}, bf16[640,2048]{1,0:T(8,128)(2,1)S(1)}, u32[]{:S(2)}, u32[]{:S(2)}) collective-permute-start(bf16[640,2048]{1,0:T(8,128)(2,1)} %get-tuple-element.105.refs_0_), channel_id=1, source_target_pairs={{0,16},{8,24},{16,0},{24,8},{1,17},{9,25},{17,1},{25,9},{2,18},{10... | collective-permute-start | bytes 7864328 | tf_op jit(solution)/shard_map/ppermute | solution.py:635
  601.6 1.5 copy-start.13
  603.1 5.4 copy-start.3
  603.2 356.6 %reduce-scatter.4.cloned.1.call-start = ((), (), s32[]{:S(2)}) async-start(), calls=%async_computation.5 | async-start | bytes 7077888 | tf_op jit(solution)/shard_map/reduce_scatter | solution.py:1443
  603.4 5.2 collective-permute-start.7
  603.7 12.4 %collective-permute-start.9 = (bf16[640,2048]{1,0:T(8,128)(2,1)}, bf16[640,2048]{1,0:T(8,128)(2,1)S(1)}, u32[]{:S(2)}, u32[]{:S(2)}) collective-permute-start(bf16[640,2048]{1,0:T(8,128)(2,1)} %get-tuple-element.105.refs_0_), channel_id=1, source_target_pairs={{0,8},{8,0},{16,24},{24,16},{1,9},{9,1},{17,25},{25,17},{2,10},{10... | collective-permute-start | bytes 7864328 | tf_op jit(solution)/shard_map/ppermute | solution.py:643
  604.0 12.2 %collective-permute-start.10 = (bf16[640,2048]{1,0:T(8,128)(2,1)}, bf16[640,2048]{1,0:T(8,128)(2,1)}, u32[]{:S(2)}, u32[]{:S(2)}) collective-permute-start(bf16[640,2048]{1,0:T(8,128)(2,1)} %copy-done.13), channel_id=1, source_target_pairs={{0,8},{8,0},{16,24},{24,16},{1,9},{9,1},{17,25},{25,17},{2,10},{10... | collective-permute-start | bytes 7864328 | tf_op jit(solution)/shard_map/ppermute | solution.py:643
  609.6 140.5 %collective-permute-start.8 = (bf16[640,2048]{1,0:T(8,128)(2,1)S(1)}, bf16[640,2048]{1,0:T(8,128)(2,1)S(1)}, u32[]{:S(2)}, u32[]{:S(2)}) collective-permute-start(bf16[640,2048]{1,0:T(8,128)(2,1)S(1)} %add_convert_fusion.2), channel_id=1, source_target_pairs={{0,16},{8,24},{16,0},{24,8},{1,17},{9,25},{17,1},{25,9},{2,18},{10... | collective-permute-start | bytes 7864328 | tf_op jit(solution)/shard_map/ppermute | solution.py:635
  616.1 1.5 copy-start.14
  750.1 15.1 %copy-start.5 = (bf16[640,2048]{1,0:T(8,128)(2,1)}, bf16[640,2048]{1,0:T(8,128)(2,1)S(1)}, u32[]{:S(2)}) copy-start(bf16[640,2048]{1,0:T(8,128)(2,1)S(1)} %collective-permute-done.8) | copy-start | bytes 7864324
  765.3 5.1 collective-permute-start.11
  773.2 58.1 %collective-permute-start.12 = (bf16[640,2048]{1,0:T(8,128)(2,1)S(1)}, bf16[640,2048]{1,0:T(8,128)(2,1)S(1)}, u32[]{:S(2)}, u32[]{:S(2)}) collective-permute-start(bf16[640,2048]{1,0:T(8,128)(2,1)S(1)} %add_convert_fusion), channel_id=1, source_target_pairs={{0,16},{8,24},{16,0},{24,8},{1,17},{9,25},{17,1},{25,9},{2,18},{10... | collective-permute-start | bytes 7864328 | tf_op jit(solution)/shard_map/ppermute | solution.py:635
  831.3 1.5 copy-start.6
  832.8 6.0 copy-start.4
  832.8 6.0 collective-permute-start.5
  939.7 8.9 copy-start.8
  959.8 33.8 %slice-start = ((s8[5242880]{0:T(1024)(128)(4,1)}), s8[4194304]{0:T(1024)(128)(4,1)S(1)}, s32[]{:S(2)}) async-start(s8[5242880]{0:T(1024)(128)(4,1)} %bitcast.39), calls=%async_computation.8 | async-start | bytes 8388608
  983.9 5.6 copy-start.2
  983.9 9.7 slice-start.1
  989.5 3.5 copy-start.10
  993.6 3.7 copy-start.1
Sparse Core Ops, SparseCore 0:
  95.8 50.3 all-gather.2
  148.4 91.6 all-gather.4
  518.4 113.3 reduce-scatter.7
  635.3 190.9 reduce-scatter.5
  833.0 126.7 reduce-scatter.3

commit v5 on v4

--- a/solution.py
+++ b/solution.py
@@ -1371,36 +1371,41 @@
 
 def own_heads_spread(project_in, me, pairs, seq_size):
     rows, columns = project_in.shape
-    every = columns // 3 // LANES
     step = seq_size // 2
 
-    def kernel(me_ref, low_ref, high_ref, out_ref):
+    def kernel(me_ref, in_ref, out_ref):
         lane = lax.broadcasted_iota(jnp.int32, (rows, LANES), 1)
         odd = me_ref[0] % 2 == 1
-        first = low_ref[...].astype(F32)
-        second = high_ref[...].astype(F32)
-        first = jnp.where(odd, pltpu.roll(first, HEAD_DIM, 1), first)
-        second = jnp.where(odd, second, pltpu.roll(second, HEAD_DIM, 1))
-        out_ref[...] = jnp.where(lane < HEAD_DIM, first, second).astype(BF16)
-
-    def source(ahead):
-        return pl.BlockSpec(
-            (rows, LANES),
-            lambda part, p, m: (0, part * every + (2 * p + ahead) * step + m[0] // 2),
-        )
+
+        def take(part, place):
+            for p in range(pairs):
+                at = (2 * p * step + place) * LANES
+                first = in_ref[:, at : at + LANES].astype(F32)
+                at = at + step * LANES
+                second = in_ref[:, at : at + LANES].astype(F32)
+                first = jnp.where(odd, pltpu.roll(first, HEAD_DIM, 1), first)
+                second = jnp.where(odd, second, pltpu.roll(second, HEAD_DIM, 1))
+                both = jnp.where(lane < HEAD_DIM, first, second).astype(BF16)
+                at = (3 * p + part) * LANES
+                out_ref[:, at : at + LANES] = both
+
+        for part in range(3):
+            for place in range(step):
+                here = (pl.program_id(0) == part) & (me_ref[0] // 2 == place)
+                pl.when(here)(functools.partial(take, part, place))
 
     return pl.pallas_call(
         kernel,
         grid_spec=pltpu.PrefetchScalarGridSpec(
             num_scalar_prefetch=1,
-            grid=(3, pairs),
-            in_specs=[source(0), source(1)],
-            out_specs=pl.BlockSpec((rows, LANES), lambda part, p, m: (0, 3 * p + part)),
+            grid=(3,),
+            in_specs=[pl.BlockSpec((rows, columns // 3), lambda part, m: (0, part))],
+            out_specs=pl.BlockSpec((rows, 3 * pairs * LANES), lambda part, m: (0, 0)),
         ),
         out_shape=jax.ShapeDtypeStruct((rows, 3 * pairs * LANES), BF16),
         compiler_params=params(),
         name="own_heads",
-    )(jnp.full((1,), me, jnp.int32), project_in, project_in)
+    )(jnp.full((1,), me, jnp.int32), project_in)
 
 
 def whole_heads_spread(pieces):

time: 1010 us -> 1010 us (level)
  transfers between devices with their start and end apart: 18 -> 18, of which waited for: 9 -> 9; matrix products, arithmetic and copies ran while one was open for 4% -> 4% of each run, Pallas kernels for 65% -> 66%
where the time goes in v5:
time: 1010 us; the launch traced here: 1000 us
  Pallas kernels  850 us (84%)
  waiting for transfers between devices  63.4 us (6%)
  other arithmetic  28.2 us (3%)
  local copies, waits for them, and re-layouts  22.4 us (2%)
  between operations  14.5 us (1%)
  starting transfers between devices  12.2 us (1%)
  matrix products  10.1 us (1%)
    pallas_call x1, Pallas kernels, hidden_rows(): pl.pallas_call(kernel, in_specs=[vmem] * (2 * chips + 4), out_specs=[vmem...  146 us
    pallas_call x1, Pallas kernels, attend_back(): pl.pallas_call(attend_back_kernel, grid_spec=pltpu.PrefetchScalarGridSpec...  107 us
    pallas_call x2, Pallas kernels, near_and_grad(): pl.pallas_call(kernel, grid_spec=pltpu.PrefetchScalarGridSpec(num_scalar_...  81.3 us
    pallas_call x4, Pallas kernels, chip_matmul(): pl.pallas_call(kernel, grid_spec=pltpu.PrefetchScalarGridSpec(num_scalar_...  78.1 us
    pallas_call x1, Pallas kernels, opening(): pl.pallas_call(kernel, in_specs=[pl.BlockSpec(memory_space=pltpu.VMEM)] *...  75.7 us
    pallas_call x1, Pallas kernels, sum_and_share(): pl.pallas_call(kernel, in_specs=[vmem] * (count + 1), out_specs=[pl.Block...  75.2 us
    pallas_call x1, Pallas kernels, attend(): pl.pallas_call(attend_kernel, grid_spec=pltpu.PrefetchScalarGridSpec(num_...  62.3 us
    pallas_call x1, Pallas kernels, feed(): pl.pallas_call(kernel, grid=(2 * count,), in_specs=[pl.BlockSpec((1, half...  60 us
  transfers between devices with their start and end apart: 18, of which 9 were waited for; matrix products, arithmetic and copies ran while one was open for 4% of the time, Pallas kernels for 66%

profile of v5, /device:TPU:9, one launch (start us, length us, event | category | flops | bytes accessed | tf_op | source)
XLA Modules:
  0.0 1000.7 jit_solution(7045819289659666852)
XLA Ops:
  7.2 0.8 stack.37
  8.1 0.7 stack.38
  8.7 0.7 stack.39
  9.4 0.7 stack.40
  10.7 3.9 own_heads.1.in_ref
  14.6 75.7 %opening.1 = (bf16[2560,2048]{1,0:T(8,128)(2,1)}, bf16[2048,1536]{1,0:T(8,128)(2,1)}, f32[8,8,256]{2,1,0:T(8,128)}) custom-call(bf16[640,2048]{1,0:T(8,128)(2,1)} %bitcast.36, bf16[256,1536]{1,0:T(8,128)(2,1)} %own_heads.1.in_ref, f32[8,256]{1,0:T(8,128)} %concatenate.12.vec_ref), custom_call_target="tpu_custom_call" | custom-call | tf_op jit(solution)/shard_map/opening/pallas_call | solution.py:862
  90.3 1.7 constant_dynamic-slice_fusion.1
  92.1 0.9 constant_dynamic-slice_fusion
  93.1 2.3 collective-permute-start
  95.4 1.2 collective-permute-start.1
  96.9 6.3 fusion.3
  103.9 0.6 broadcast_in_dim.114.bias_ref
  104.5 28.6 %project_in_rope.1 = (bf16[2560,1536]{1,0:T(8,128)(2,1)}, bf16[2560,2048]{1,0:T(8,128)(2,1)}) custom-call(bf16[2560,2048]{1,0:T(8,128)(2,1)} %get-tuple-element.77.x_ref, bf16[2048,1536]{1,0:T(8,128)(2,1)} %get-tuple-element.78.w_ref, f32[8,2048]{1,0:T(8,128)} %broadcast_in_dim.112.gain_ref.refs_5_, f32[8,2048]{1,0:T(8,128)} %broadcast_in_dim.114.bias_ref, ...), custom_call_target="tpu_custom_call" | custom-call | flops 16106127360 | bytes 24641536 | tf_op jit(solution)/shard_map/project_in_rope/pallas_call | solution.py:104
  133.1 62.3 %attend.1 = (bf16[2560,512]{1,0:T(8,128)(2,1)}, bf16[8,2560,128]{2,1,0:T(8,128)(2,1)}) custom-call(s32[2]{0:T(128)} %copy-done.11, bf16[2560,1536]{1,0:T(8,128)(2,1)} %get-tuple-element.80.refs_0_.refs_1_.refs_2_.refs_3_.refs_4_.refs_5_.k_ref.v_ref, bf16[2560,1536]{1,0:T(8,128)(2,1)} %get-tuple-element.80.refs_0_.refs_1_.refs_2_.refs_3_.refs_4_.refs_5_.k_ref.v_ref, ...), custom_call_target="tpu_custom_call" | custom-call | flops 26843545600 | bytes 7864320 | tf_op jit(solution)/shard_map/attend/pallas_call | solution.py:218
  195.7 0.6 slice.56.order_ref
  196.4 4.4 own_columns.1.refs_7_
  201.5 13.9 %attention_out.1 = (bf16[640,2048]{1,0:T(8,128)(2,1)}, bf16[640,2048]{1,0:T(8,128)(2,1)}, bf16[640,2048]{1,0:T(8,128)(2,1)}, bf16[640,2048]{1,0:T(8,128)(2,1)}) custom-call(s32[4]{0:T(128)} %pad_add_fusion.order_ref, bf16[2560,512]{1,0:T(8,128)(2,1)} %get-tuple-element.84.x_ref.o_ref, bf16[512,2048]{1,0:T(8,128)(2,1)} %all-gather.3.cloned.1.call-done.w_ref.refs_4_), custom_call_target="tpu_custom_call" | custom-call | flops 5368709120 | bytes 15204352 | tf_op jit(solution)/shard_map/attention_out/pallas_call | solution.py:392
  216.6 146.0 %hidden_rows.1 = (f32[640,2048]{1,0:T(8,128)}, bf16[4,640,2048]{2,1,0:T(8,128)(2,1)}, bf16[2048,2816]{1,0:T(8,128)(2,1)}) custom-call(bf16[640,2048]{1,0:T(8,128)(2,1)} %get-tuple-element.86.refs_0_, bf16[640,2048]{1,0:T(8,128)(2,1)} %get-tuple-element.87.refs_1_, bf16[640,2048]{1,0:T(8,128)(2,1)} %get-tuple-element.88.refs_2_, ...), custom_call_target="tpu_custom_call" | custom-call | tf_op jit(solution)/shard_map/hidden_rows/pallas_call | solution.py:991
  362.7 60.0 %feed.1 = (bf16[2560,1408]{1,0:T(8,128)(2,1)}, bf16[2560,2816]{1,0:T(8,128)(2,1)}, bf16[2560,2048]{1,0:T(8,128)(2,1)}, bf16[2560,2048]{1,0:T(8,128)(2,1)}) custom-call(bf16[4,640,2048]{2,1,0:T(8,128)(2,1)} %get-tuple-element.91.x_ref, bf16[640,2048]{1,0:T(8,128)(2,1)} %bitcast.44, bf16[640,2048]{1,0:T(8,128)(2,1)} %copy-done.12, ...), custom_call_target="tpu_custom_call" | custom-call | flops 44291850240 | bytes 55967744 | tf_op jit(solution)/shard_map/feed/pallas_call | solution.py:499
  422.7 23.7 %feed_back.1 = (bf16[640,2048]{1,0:T(8,128)(2,1)}, bf16[640,2048]{1,0:T(8,128)(2,1)}) custom-call(s32[2]{0:T(128)} %slice.56.order_ref, bf16[2560,2816]{1,0:T(8,128)(2,1)} %get-tuple-element.99.x_ref.g_ref, bf16[2048,2816]{1,0:T(8,128)(2,1)} %get-tuple-element.92.refs_4_.w_ref), custom_call_target="tpu_custom_call" | custom-call | flops 14763950080 | bytes 23986176 | tf_op jit(solution)/shard_map/feed_back/pallas_call | solution.py:392
  446.4 1.0 collective-permute-start.3
  447.4 4.7 collective-permute-done.3
  452.2 2.8 add_convert_fusion.3
  455.0 1.3 collective-permute-start.4
  456.8 43.1 %near_and_down.1 = (bf16[640,2048]{1,0:T(8,128)(2,1)}, bf16[640,2048]{1,0:T(8,128)(2,1)}, bf16[1408,2048]{1,0:T(8,128)(2,1)}) custom-call(s32[2]{0:T(128)} %bitcast.55, bf16[2560,2816]{1,0:T(8,128)(2,1)} %get-tuple-element.99.x_ref.g_ref, bf16[2048,2816]{1,0:T(8,128)(2,1)} %get-tuple-element.92.refs_4_.w_ref, ...), custom_call_target="tpu_custom_call" | custom-call | flops 36909875200 | bytes 42663936 | tf_op jit(solution)/shard_map/near_and_down/pallas_call | solution.py:560
  499.9 13.2 %collective-permute-done.4.refs_2_ = bf16[640,2048]{1,0:T(8,128)(2,1)S(1)} collective-permute-done((bf16[640,2048]{1,0:T(8,128)(2,1)S(1)}, bf16[640,2048]{1,0:T(8,128)(2,1)S(1)}, u32[]{:S(2)}, u32[]{:S(2)}) %collective-permute-start.4) | collective-permute-done | bytes 2621472 | tf_op jit(solution)/shard_map/ppermute | solution.py:635
  513.1 1.5 copy-done.7
  515.1 18.3 %closing_rows.2 = (f32[640,2048]{1,0:T(8,128)}, bf16[640,2048]{1,0:T(8,128)(2,1)}, f32[8,2048]{1,0:T(8,128)}) custom-call(bf16[640,2048]{1,0:T(8,128)(2,1)} %get-tuple-element.101.refs_0_, bf16[640,2048]{1,0:T(8,128)(2,1)} %get-tuple-element.102.refs_1_, bf16[640,2048]{1,0:T(8,128)(2,1)} %copy-done.7, f32[640,2048]{1,0:T(8,128)} %get-tuple-element.90.refs_3_, ...), custom_call_target="tpu_custom_call" | custom-call | tf_op jit(solution)/shard_map/closing_rows/pallas_call | solution.py:1101
  533.6 38.4 %grad_gate_up.1 = bf16[2048,2816]{1,0:T(8,128)(2,1)} custom-call(bf16[2560,2048]{1,0:T(8,128)(2,1)} %get-tuple-element.107.x_ref, bf16[2560,2816]{1,0:T(8,128)(2,1)} %get-tuple-element.99.x_ref.g_ref), custom_call_target="tpu_custom_call" | custom-call | flops 29527900160 | bytes 36438016 | tf_op jit(solution)/shard_map/grad_gate_up/pallas_call | solution.py:427
  572.6 25.4 %feed_down.1 = (bf16[640,2048]{1,0:T(8,128)(2,1)}, bf16[640,2048]{1,0:T(8,128)(2,1)}, bf16[640,2048]{1,0:T(8,128)(2,1)}, bf16[640,2048]{1,0:T(8,128)(2,1)}) custom-call(s32[4]{0:T(128)} %iota.50.order_ref, bf16[2560,1408]{1,0:T(8,128)(2,1)} %get-tuple-element.108.left_ref.x_ref, bf16[1408,2048]{1,0:T(8,128)(2,1)} %all-gather.5.cloned.1.call-done.refs_5_.w_ref), custom_call_target="tpu_custom_call" | custom-call | flops 14763950080 | bytes 23461888 | tf_op jit(solution)/shard_map/feed_down/pallas_call | solution.py:392
  598.0 1.5 copy-done.13
  600.5 0.7 pad_add_fusion.2.order_ref
  601.2 3.7 collective-permute-done.7
  604.9 1.0 add_convert_fusion.2
  606.0 1.3 collective-permute-start.8
  607.3 5.1 collective-permute-done.9.refs_1_
  612.6 1.4 copy-done.14
  613.9 15.0 %grad_attended.1 = (bf16[2560,512]{1,0:T(8,128)(2,1)}, bf16[2560,2048]{1,0:T(8,128)(2,1)}) custom-call(s32[4]{0:T(128)} %pad_add_fusion.order_ref, bf16[640,2048]{1,0:T(8,128)(2,1)} %get-tuple-element.105.refs_0_, bf16[640,2048]{1,0:T(8,128)(2,1)} %copy-done.14, bf16[640,2048]{1,0:T(8,128)(2,1)} %copy-done.13, ...), custom_call_target="tpu_custom_call" | custom-call | flops 5368709120 | bytes 15204352 | tf_op jit(solution)/shard_map/grad_attended/pallas_call | solution.py:607
  628.9 10.1 %convolution_convert_fusion.part_ref = bf16[512,2048]{1,0:T(8,128)(2,1)} fusion(bf16[2560,512]{1,0:T(8,128)(2,1)} %get-tuple-element.84.x_ref.o_ref, bf16[2560,2048]{1,0:T(8,128)(2,1)} %get-tuple-element.118), kind=kOutput, calls=%fused_computation.4 | convolution fusion | flops 5369757696 | bytes 15204352 | tf_op jit(solution)/shard_map/dot_general | solution.py:31
  639.0 107.5 %attend_back.1.x_ref.right_ref = bf16[2560,1536]{1,0:T(8,128)(2,1)} custom-call(s32[2]{0:T(128)} %copy-done.11, bf16[8,2560,128]{2,1,0:T(8,128)(2,1)} %get-tuple-element.116.qx_ref, bf16[2560,1536]{1,0:T(8,128)(2,1)} %get-tuple-element.80.refs_0_.refs_1_.refs_2_.refs_3_.refs_4_.refs_5_.k_ref.v_ref, ...), custom_call_target="tpu_custom_call" | custom-call | flops 67108864000 | bytes 7864320 | tf_op jit(solution)/shard_map/attend_back/pallas_call | solution.py:334
  746.5 15.1 %project_back.1 = (bf16[640,2048]{1,0:T(8,128)(2,1)}, bf16[640,2048]{1,0:T(8,128)(2,1)}) custom-call(s32[2]{0:T(128)} %pad_add_fusion.2.order_ref, bf16[2560,1536]{1,0:T(8,128)(2,1)} %attend_back.1.x_ref.right_ref, bf16[2048,1536]{1,0:T(8,128)(2,1)} %get-tuple-element.78.w_ref), custom_call_target="tpu_custom_call" | custom-call | flops 8053063680 | bytes 15466496 | tf_op jit(solution)/shard_map/project_back/pallas_call | solution.py:392
  761.9 4.8 collective-permute-done.11
  766.7 2.8 add_convert_fusion
  769.5 1.3 collective-permute-start.12
  771.3 38.2 %near_and_project_in.1 = (bf16[640,2048]{1,0:T(8,128)(2,1)}, bf16[640,2048]{1,0:T(8,128)(2,1)}, bf16[2048,1536]{1,0:T(8,128)(2,1)}) custom-call(s32[2]{0:T(128)} %pad_add_fusion.1.order_ref, bf16[2560,1536]{1,0:T(8,128)(2,1)} %attend_back.1.x_ref.right_ref, bf16[2048,1536]{1,0:T(8,128)(2,1)} %get-tuple-element.78.w_ref, ...), custom_call_target="tpu_custom_call" | custom-call | flops 20132659200 | bytes 29229056 | tf_op jit(solution)/shard_map/near_and_project_in/pallas_call | solution.py:560
  809.5 18.1 %collective-permute-done.12.refs_2_ = bf16[640,2048]{1,0:T(8,128)(2,1)S(1)} collective-permute-done((bf16[640,2048]{1,0:T(8,128)(2,1)S(1)}, bf16[640,2048]{1,0:T(8,128)(2,1)S(1)}, u32[]{:S(2)}, u32[]{:S(2)}) %collective-permute-start.12) | collective-permute-done | bytes 2621472 | tf_op jit(solution)/shard_map/ppermute | solution.py:635
  827.6 1.5 copy-done.6
  829.2 1.3 collective-permute-start.5
  830.4 0.8 slice.58
  831.3 3.9 collective-permute-done.5
  835.2 6.8 fusion
  841.9 16.5 %closing_rows.3 = (f32[640,2048]{1,0:T(8,128)}, f32[8,2048]{1,0:T(8,128)}) custom-call(bf16[640,2048]{1,0:T(8,128)(2,1)} %get-tuple-element.125.refs_0_, bf16[640,2048]{1,0:T(8,128)(2,1)} %get-tuple-element.126.refs_1_, bf16[640,2048]{1,0:T(8,128)(2,1)} %copy-done.6, bf16[640,2048]{1,0:T(8,128)(2,1)} %bitcast.38, f32[640,2048]{1,0:T(8,128)} %get-tuple-element.129.refs_4_, ...), custom_call_target="tpu_custom_call" | custom-call | tf_op jit(solution)/shard_map/closing_rows/pallas_call | solution.py:1101
  858.4 0.8 slice.59
  859.3 0.8 slice.57
  860.1 0.7 pad_maximum_fusion.vec_ref
  860.8 75.2 %sum_and_share.1 = (bf16[4,256,2816]{2,1,0:T(8,128)(2,1)}, bf16[4,176,2048]{2,1,0:T(8,128)(2,1)}, bf16[4,64,2048]{2,1,0:T(8,128)(2,1)}, f32[8,256]{1,0:T(8,128)}) custom-call(bf16[512,2048]{1,0:T(8,128)(2,1)} %convolution_convert_fusion.part_ref, f32[8,2048]{1,0:T(8,128)} %pad_maximum_fusion.vec_ref, ...), custom_call_target="tpu_custom_call" | custom-call | tf_op jit(solution)/shard_map/sum_and_share/pallas_call | solution.py:1286
  936.1 8.9 whole_columns.1
  944.9 1.6 bitcast_convert_fusion.1
  946.6 9.6 reduce-scatter.4.cloned.1.call-done.refs_0_
  956.1 24.1 %share_pieces.1.in_ref = bf16[4,256,1536]{2,1,0:T(8,128)(2,1)} custom-call(bf16[256,1536]{1,0:T(8,128)(2,1)} %reduce-scatter.4.cloned.1.call-done.refs_0_), custom_call_target="tpu_custom_call" | custom-call | tf_op jit(solution)/shard_map/share_pieces/pallas_call | solution.py:1178
  980.3 5.6 whole_heads.1
  985.9 3.5 bitcast_convert_fusion
  990.0 2.7 copy.24
  992.7 1.0 copy-done.1
  (78 shorter events, 8.5 us)
Async XLA Ops:
  7.2 84.9 %copy-start = (bf16[704,2048]{1,0:T(8,128)(2,1)S(1)}, bf16[704,2048]{1,0:T(8,128)(2,1)}, u32[]{:S(2)}) copy-start(bf16[704,2048]{1,0:T(8,128)(2,1)} %param.18) | copy-start | bytes 8650756
  7.2 194.3 %all-gather.3.cloned.1.call-start = ((), (), s32[]{:S(2)}) async-start(), calls=%async_computation.3 | async-start | bytes 2359296 | tf_op jit(solution)/shard_map/all_gather | solution.py:1444
  14.6 82.0 %copy-start.15 = (s32[1,2]{1,0:T(1,128)S(1)}, s32[1,2]{1,0:T(1,128)}, u32[]{:S(2)}) copy-start(s32[1,2]{1,0:T(1,128)} %param.13) | copy-start | bytes 28
  90.3 6.6 copy-start.9
  92.1 270.6 %all-gather.5.cloned.1.call-start = ((), (), s32[]{:S(2)}) async-start(), calls=%async_computation.4 | async-start | bytes 6488064 | tf_op jit(solution)/shard_map/all_gather | solution.py:1444
  93.1 767.7 %reduce-scatter.8.cloned.1.call-start = ((), (), s32[]{:S(2)}) async-start(), calls=%async_computation.7 | async-start | bytes 6488064 | tf_op jit(solution)/shard_map/reduce_scatter | solution.py:1448
  93.1 108.3 %collective-permute-start = (bf16[640,2048]{1,0:T(8,128)(2,1)}, bf16[640,2048]{1,0:T(8,128)(2,1)S(1)}, u32[]{:S(2)}, u32[]{:S(2)}) collective-permute-start(bf16[640,2048]{1,0:T(8,128)(2,1)} %bitcast.42), channel_id=1, source_target_pairs={{0,8},{8,0},{16,24},{24,16},{1,9},{9,1},{17,25},{25,17},{2,10},{10... | collective-permute-start | bytes 7864328 | tf_op jit(solution)/shard_map/ppermute | solution.py:643
  95.4 100.0 %collective-permute-start.1 = (bf16[640,2048]{1,0:T(8,128)(2,1)}, bf16[640,2048]{1,0:T(8,128)(2,1)}, u32[]{:S(2)}, u32[]{:S(2)}) collective-permute-start(bf16[640,2048]{1,0:T(8,128)(2,1)} %bitcast.43), channel_id=1, source_target_pairs={{0,16},{8,24},{16,0},{24,8},{1,17},{9,25},{17,1},{25,9},{2,18},{10... | collective-permute-start | bytes 7864328 | tf_op jit(solution)/shard_map/ppermute | solution.py:635
  96.7 36.4 %copy-start.11 = (s32[2]{0:T(128)}, s32[2]{0:T(128)S(1)}, u32[]{:S(2)}) copy-start(s32[2]{0:T(128)S(1)} %fusion.5.ends_ref) | copy-start | bytes 28
  195.4 6.0 collective-permute-start.2
  201.4 13.9 %copy-start.12 = (bf16[640,2048]{1,0:T(8,128)(2,1)}, bf16[640,2048]{1,0:T(8,128)(2,1)S(1)}, u32[]{:S(2)}) copy-start(bf16[640,2048]{1,0:T(8,128)(2,1)S(1)} %collective-permute-done.refs_1_) | copy-start | bytes 7864324
  446.4 5.8 collective-permute-start.3
  455.0 58.1 %collective-permute-start.4 = (bf16[640,2048]{1,0:T(8,128)(2,1)S(1)}, bf16[640,2048]{1,0:T(8,128)(2,1)S(1)}, u32[]{:S(2)}, u32[]{:S(2)}) collective-permute-start(bf16[640,2048]{1,0:T(8,128)(2,1)S(1)} %add_convert_fusion.3), channel_id=1, source_target_pairs={{0,16},{8,24},{16,0},{24,8},{1,17},{9,25},{17,1},{25,9},{2,18},{10... | collective-permute-start | bytes 7864328 | tf_op jit(solution)/shard_map/ppermute | solution.py:635
  513.1 1.5 copy-start.7
  514.6 346.2 %reduce-scatter.6.cloned.1.call-start = ((), (), s32[]{:S(2)}) async-start(), calls=%async_computation.6 | async-start | bytes 12976128 | tf_op jit(solution)/shard_map/reduce_scatter | solution.py:1448
  533.3 64.6 %collective-permute-start.6 = (bf16[640,2048]{1,0:T(8,128)(2,1)}, bf16[640,2048]{1,0:T(8,128)(2,1)S(1)}, u32[]{:S(2)}, u32[]{:S(2)}) collective-permute-start(bf16[640,2048]{1,0:T(8,128)(2,1)} %get-tuple-element.105.refs_0_), channel_id=1, source_target_pairs={{0,16},{8,24},{16,0},{24,8},{1,17},{9,25},{17,1},{25,9},{2,18},{10... | collective-permute-start | bytes 7864328 | tf_op jit(solution)/shard_map/ppermute | solution.py:635
  598.0 1.5 copy-start.13
  599.5 5.4 copy-start.3
  599.5 356.6 %reduce-scatter.4.cloned.1.call-start = ((), (), s32[]{:S(2)}) async-start(), calls=%async_computation.5 | async-start | bytes 7077888 | tf_op jit(solution)/shard_map/reduce_scatter | solution.py:1448
  599.7 5.2 collective-permute-start.7
  600.0 12.4 %collective-permute-start.9 = (bf16[640,2048]{1,0:T(8,128)(2,1)}, bf16[640,2048]{1,0:T(8,128)(2,1)S(1)}, u32[]{:S(2)}, u32[]{:S(2)}) collective-permute-start(bf16[640,2048]{1,0:T(8,128)(2,1)} %get-tuple-element.105.refs_0_), channel_id=1, source_target_pairs={{0,8},{8,0},{16,24},{24,16},{1,9},{9,1},{17,25},{25,17},{2,10},{10... | collective-permute-start | bytes 7864328 | tf_op jit(solution)/shard_map/ppermute | solution.py:643
  600.3 12.2 %collective-permute-start.10 = (bf16[640,2048]{1,0:T(8,128)(2,1)}, bf16[640,2048]{1,0:T(8,128)(2,1)}, u32[]{:S(2)}, u32[]{:S(2)}) collective-permute-start(bf16[640,2048]{1,0:T(8,128)(2,1)} %copy-done.13), channel_id=1, source_target_pairs={{0,8},{8,0},{16,24},{24,16},{1,9},{9,1},{17,25},{25,17},{2,10},{10... | collective-permute-start | bytes 7864328 | tf_op jit(solution)/shard_map/ppermute | solution.py:643
  606.0 140.5 %collective-permute-start.8 = (bf16[640,2048]{1,0:T(8,128)(2,1)S(1)}, bf16[640,2048]{1,0:T(8,128)(2,1)S(1)}, u32[]{:S(2)}, u32[]{:S(2)}) collective-permute-start(bf16[640,2048]{1,0:T(8,128)(2,1)S(1)} %add_convert_fusion.2), channel_id=1, source_target_pairs={{0,16},{8,24},{16,0},{24,8},{1,17},{9,25},{17,1},{25,9},{2,18},{10... | collective-permute-start | bytes 7864328 | tf_op jit(solution)/shard_map/ppermute | solution.py:635
  612.4 1.5 copy-start.14
  746.5 15.1 %copy-start.5 = (bf16[640,2048]{1,0:T(8,128)(2,1)}, bf16[640,2048]{1,0:T(8,128)(2,1)S(1)}, u32[]{:S(2)}) copy-start(bf16[640,2048]{1,0:T(8,128)(2,1)S(1)} %collective-permute-done.8) | copy-start | bytes 7864324
  761.6 5.1 collective-permute-start.11
  769.5 58.1 %collective-permute-start.12 = (bf16[640,2048]{1,0:T(8,128)(2,1)S(1)}, bf16[640,2048]{1,0:T(8,128)(2,1)S(1)}, u32[]{:S(2)}, u32[]{:S(2)}) collective-permute-start(bf16[640,2048]{1,0:T(8,128)(2,1)S(1)} %add_convert_fusion), channel_id=1, source_target_pairs={{0,16},{8,24},{16,0},{24,8},{1,17},{9,25},{17,1},{25,9},{2,18},{10... | collective-permute-start | bytes 7864328 | tf_op jit(solution)/shard_map/ppermute | solution.py:635
  827.6 1.5 copy-start.6
  829.1 6.0 copy-start.4
  829.2 6.0 collective-permute-start.5
  936.1 8.9 copy-start.8
  956.1 33.8 %slice-start = ((s8[5242880]{0:T(1024)(128)(4,1)}), s8[4194304]{0:T(1024)(128)(4,1)S(1)}, s32[]{:S(2)}) async-start(s8[5242880]{0:T(1024)(128)(4,1)} %bitcast.39), calls=%async_computation.8 | async-start | bytes 8388608
  980.2 5.6 copy-start.2
  980.3 9.7 slice-start.1
  985.9 3.5 copy-start.10
  990.0 3.7 copy-start.1
Sparse Core Ops, SparseCore 0:
  92.2 50.3 all-gather.2
  144.7 91.5 all-gather.4
  514.7 113.2 reduce-scatter.7
  631.5 190.9 reduce-scatter.5
  829.3 126.8 reduce-scatter.3
